TPU v7x, 32 devices: a whole 2x2x4 slice. The times are simulated.
32 devices in a mesh: fsdp: 4 (over z), seq: 8 (over y, x, core).
Axes of the slice: x: 2, y: 2, z: 4, core: 2. Of those that a mesh axis runs over, the one named last changes fastest.
Arguments:
- block_input: bfloat16 [8, 1536, 1024], P('fsdp', 'seq'), may hold values from -6 to 6
- positions: int32 [8, 1536], P('fsdp'), may hold values from 0 to 1535, as said below
- cotangent: bfloat16 [8, 1536, 1024], P('fsdp', 'seq'), may hold values from -6 to 6
- attention_gain: bfloat16 [1024], P(('fsdp', 'seq')), may hold values from 0.099609375 to 1.8984375
- query_weight: bfloat16 [1024, 1024], P(('fsdp', 'seq')), may hold values from -0.1875 to 0.1875
- key_weight: bfloat16 [1024, 512], P(('fsdp', 'seq')), may hold values from -0.1875 to 0.1875
- value_weight: bfloat16 [1024, 512], P(('fsdp', 'seq')), may hold values from -0.1875 to 0.1875
- query_gain: bfloat16 [64], replicated, may hold values from 0.8 to 2
- key_gain: bfloat16 [64], replicated, may hold values from 0.8 to 2
- output_weight: bfloat16 [1024, 1024], P(('fsdp', 'seq')), may hold values from -0.75 to 0.75
- feedforward_gain: bfloat16 [1024], P(('fsdp', 'seq')), may hold values from 0.099609375 to 1.8984375
- gate_weight: bfloat16 [1024, 4608], P(('fsdp', 'seq')), may hold values from -0.1875 to 0.1875
- up_weight: bfloat16 [1024, 4608], P(('fsdp', 'seq')), may hold values from -0.1875 to 0.1875
- down_weight: bfloat16 [4608, 1024], P(('fsdp', 'seq')), may hold values from -0.09375 to 0.09375
Outputs:
- block_output: bfloat16 [8, 1536, 1024], P('fsdp', 'seq')
- input_grad: bfloat16 [8, 1536, 1024], P('fsdp', 'seq')
- attention_gain_grad: float32 [1024], P(('fsdp', 'seq'))
- query_grad: float32 [1024, 1024], P(('fsdp', 'seq'))
- key_grad: float32 [1024, 512], P(('fsdp', 'seq'))
- value_grad: float32 [1024, 512], P(('fsdp', 'seq'))
- query_gain_grad: float32 [64], replicated
- key_gain_grad: float32 [64], replicated
- output_grad: float32 [1024, 1024], P(('fsdp', 'seq'))
- feedforward_gain_grad: float32 [1024], P(('fsdp', 'seq'))
- gate_grad: float32 [1024, 4608], P(('fsdp', 'seq'))
- up_grad: float32 [1024, 4608], P(('fsdp', 'seq'))
- down_grad: float32 [4608, 1024], P(('fsdp', 'seq'))
Inputs may be any that keep to these rules, and one draw needn't show every extreme that they name: In every sequence positions begin at 0, and each next one is one more or 0 (a new document); the first sequence is one document.
All inputs are finite; a program needn't handle non-finite values.
Results may differ from a plain program's by a relative error of at most 0.015.
Values may be sent and summed in bfloat16 or wider, within the bound.
No kernel may reach another device: no remote copies, remote signals or barrier semaphores. Data moves between devices by JAX's collectives and lax.ppermute only.
A program may use at most 256 MiB of HBM per device.

v0:
```python
import jax
import jax.numpy as jnp
from jax import lax
from jax.sharding import PartitionSpec as P

H = 16
KV = 8
HD = 64


rope_base = 1000000.0
eps = 1e-05
masked = -1e30


def shortened(array):

    def short(part):
        return part.astype(jnp.bfloat16) if part.dtype == jnp.float32 else part

    return jax.tree.map(short, array)


def contract(formula, left, right):
    return jnp.einsum(formula, left, right, preferred_element_type=jnp.float32)


def matmul(left, right):
    return jnp.dot(left, right, preferred_element_type=jnp.float32)


def rope_tables(places, head_width):
    half_width = head_width // 2
    inverse = rope_base ** (-(jnp.arange(half_width, dtype=jnp.float32) * 2.0) / head_width)
    angles = places.astype(jnp.float32)[:, None] * inverse[None, :]
    return (jnp.cos(angles)[:, None, :], jnp.sin(angles)[:, None, :])


def head_prep(raw_rows, gain_row, cosine, sine, head_count):
    row_count = raw_rows.shape[0]
    split_rows = raw_rows.reshape(row_count, head_count, -1)
    factor = lax.rsqrt(jnp.mean(split_rows * split_rows, axis=-1, keepdims=True) + eps)
    normed = split_rows * factor * gain_row
    half_width = normed.shape[-1] // 2
    lower = normed[..., :half_width]
    upper = normed[..., half_width:]
    turned = jnp.concatenate(
        [lower * cosine - upper * sine, upper * cosine + lower * sine], axis=-1
    )
    return turned.reshape(row_count, -1)


def norm_fwd(values, gain_row):
    factor = lax.rsqrt(jnp.mean(values * values, axis=-1, keepdims=True) + eps)
    return (values * factor * gain_row, factor)


def norm_bwd(values, factor, gain_row, grad_result):
    normed = values * factor
    grad_normed = grad_result * gain_row
    grad_values = factor * (
        grad_normed - normed * jnp.mean(grad_normed * normed, axis=-1, keepdims=True)
    )
    return (grad_values, jnp.sum(grad_result * normed, axis=0))


def masked_scores(queries, key_rows, doc_start, begin_row, end_row, scaling):
    query_index = jnp.arange(begin_row, end_row, dtype=jnp.int32)
    key_index = jnp.arange(end_row, dtype=jnp.int32)
    allowed = (key_index[None, :] <= query_index[:, None]) & (
        key_index[None, :] >= doc_start[begin_row:end_row, None]
    )
    scores = contract("qhd,khd->hqk", queries[begin_row:end_row], key_rows[:end_row]) * scaling
    return jnp.where(allowed[None, :, :], scores, masked)


def attend_fwd(queries, key_rows, value_rows, doc_start):
    seq_length, head_count, head_width = queries.shape
    block_rows = min(512, seq_length)
    scaling = head_width ** (-0.5)
    out_blocks = []
    total_blocks = []
    for begin_row in range(0, seq_length, block_rows):
        end_row = begin_row + block_rows
        scores = masked_scores(queries, key_rows, doc_start, begin_row, end_row, scaling)
        largest = jnp.max(scores, axis=-1, keepdims=True)
        log_total = largest + jnp.log(jnp.sum(jnp.exp(scores - largest), axis=-1, keepdims=True))
        attn_prob = jnp.exp(scores - log_total).astype(jnp.bfloat16)
        out_blocks.append(
            contract("hqk,khd->qhd", attn_prob, value_rows[:end_row]).astype(jnp.bfloat16)
        )
        total_blocks.append(log_total[..., 0])
    return (jnp.concatenate(out_blocks, axis=0), jnp.concatenate(total_blocks, axis=1))


def attend_bwd(queries, key_rows, value_rows, outputs, log_totals, grad_result, doc_start):
    seq_length, head_count, head_width = queries.shape
    block_rows = min(512, seq_length)
    scaling = head_width ** (-0.5)
    carried = jnp.sum(grad_result.astype(jnp.float32) * outputs.astype(jnp.float32), axis=-1).T
    grad_query = []
    grad_key = jnp.zeros((seq_length, head_count, head_width), jnp.float32)
    grad_value = jnp.zeros((seq_length, head_count, head_width), jnp.float32)
    for begin_row in range(0, seq_length, block_rows):
        end_row = begin_row + block_rows
        scores = masked_scores(queries, key_rows, doc_start, begin_row, end_row, scaling)
        attn_prob = jnp.exp(scores - log_totals[:, begin_row:end_row, None])
        prob_half = attn_prob.astype(jnp.bfloat16)
        grad_rows = grad_result[begin_row:end_row]
        grad_value = grad_value.at[:end_row].add(contract("hqk,qhd->khd", prob_half, grad_rows))
        grad_prob = contract("qhd,khd->hqk", grad_rows, value_rows[:end_row])
        grad_score = (
            attn_prob * (grad_prob - carried[:, begin_row:end_row, None]) * scaling
        ).astype(jnp.bfloat16)
        grad_query.append(contract("hqk,khd->qhd", grad_score, key_rows[:end_row]))
        grad_key = grad_key.at[:end_row].add(
            contract("hqk,qhd->khd", grad_score, queries[begin_row:end_row])
        )
    return (
        jnp.concatenate(grad_query, axis=0).astype(jnp.bfloat16),
        grad_key.astype(jnp.bfloat16),
        grad_value.astype(jnp.bfloat16),
    )


def body(
    block_input,
    positions,
    cotangent,
    attention_gain,
    query_weight,
    key_weight,
    value_weight,
    query_gain,
    key_gain,
    output_weight,
    feedforward_gain,
    gate_weight,
    up_weight,
    down_weight,
):
    seq_count, span_rows, model_width = block_input.shape
    groups = lax.axis_size("seq")
    row_count = seq_count * span_rows
    full_length = span_rows * groups
    local_heads = H // groups
    copies = max(1, groups // KV)
    group_size = H // KV
    gathered = (
        lax.all_gather(attention_gain, ("fsdp", "seq"), axis=0, tiled=True),
        lax.all_gather(query_weight, ("fsdp", "seq"), axis=0, tiled=True),
        lax.all_gather(key_weight, ("fsdp", "seq"), axis=0, tiled=True),
        lax.all_gather(value_weight, ("fsdp", "seq"), axis=0, tiled=True),
        lax.all_gather(output_weight, ("fsdp", "seq"), axis=0, tiled=True),
        lax.all_gather(feedforward_gain, ("fsdp", "seq"), axis=0, tiled=True),
        lax.all_gather(gate_weight, ("fsdp", "seq"), axis=0, tiled=True),
        lax.all_gather(up_weight, ("fsdp", "seq"), axis=0, tiled=True),
        lax.all_gather(down_weight, ("fsdp", "seq"), axis=0, tiled=True),
    )
    (
        gain_one_full,
        query_full,
        key_full,
        value_full,
        output_full,
        gain_two_full,
        gate_full,
        up_full,
        down_full,
    ) = gathered
    gain_one = gain_one_full.astype(jnp.float32)
    gain_two = gain_two_full.astype(jnp.float32)
    query_scale = query_gain.astype(jnp.float32)
    key_scale = key_gain.astype(jnp.float32)
    local_places = lax.dynamic_slice_in_dim(
        positions, lax.axis_index("seq") * span_rows, span_rows, 1
    ).reshape(row_count)
    cosine, sine = rope_tables(local_places, HD)

    def query_side(raw_rows, gain_row):
        return head_prep(raw_rows, gain_row, cosine, sine, H)

    def key_side(raw_rows, gain_row):
        return head_prep(raw_rows, gain_row, cosine, sine, KV)

    def spread_heads(rows_packed):
        shaped = rows_packed.reshape(seq_count, span_rows, KV, HD)
        if copies > 1:
            shaped = jnp.repeat(shaped, copies, axis=2)
        return shaped.reshape(seq_count, span_rows, KV * copies * HD)

    def head_view(packed):
        shaped = packed.reshape(seq_count, full_length, -1, HD)
        repeat_count = local_heads // shaped.shape[2]
        if repeat_count > 1:
            shaped = jnp.repeat(shaped, repeat_count, axis=2)
        return shaped

    def fold_groups(packed):
        summed = jnp.sum(packed.reshape(row_count, KV, group_size, HD).astype(jnp.float32), axis=2)
        return summed.reshape(row_count, KV * HD)

    residual_in = block_input.reshape(row_count, model_width).astype(jnp.float32)
    normed_one, factor_one = norm_fwd(residual_in, gain_one)
    normed_in = normed_one.astype(jnp.bfloat16)
    query_raw = matmul(normed_in, query_full)
    key_raw = matmul(normed_in, key_full)
    value_rows = matmul(normed_in, value_full).astype(jnp.bfloat16)
    query_rows = query_side(query_raw, query_scale).astype(jnp.bfloat16)
    key_rows = key_side(key_raw, key_scale).astype(jnp.bfloat16)
    query_seq, key_seq, value_seq = (
        lax.all_to_all(
            query_rows.reshape(seq_count, span_rows, H * HD),
            "seq",
            split_axis=2,
            concat_axis=1,
            tiled=True,
        ),
        lax.all_to_all(spread_heads(key_rows), "seq", split_axis=2, concat_axis=1, tiled=True),
        lax.all_to_all(spread_heads(value_rows), "seq", split_axis=2, concat_axis=1, tiled=True),
    )
    queries = query_seq.reshape(seq_count, full_length, local_heads, HD)
    keys_local = head_view(key_seq)
    values_local = head_view(value_seq)
    doc_start = jnp.arange(full_length, dtype=jnp.int32)[None, :] - positions
    outputs, log_totals = jax.vmap(attend_fwd)(queries, keys_local, values_local, doc_start)
    mixed_back = lax.all_to_all(
        shortened(outputs.reshape(seq_count, full_length, local_heads * HD)),
        "seq",
        split_axis=1,
        concat_axis=2,
        tiled=True,
    )
    attn_out = mixed_back.reshape(row_count, H * HD)
    residual_mid = residual_in + matmul(attn_out, output_full)
    normed_two, factor_two = norm_fwd(residual_mid, gain_two)
    normed_mid = normed_two.astype(jnp.bfloat16)
    gate_rows = matmul(normed_mid, gate_full)
    up_rows = matmul(normed_mid, up_full)
    sigma = jax.nn.sigmoid(gate_rows)
    hidden = (gate_rows * sigma * up_rows).astype(jnp.bfloat16)
    result = residual_mid + matmul(hidden, down_full)
    block_output = result.astype(jnp.bfloat16).reshape(seq_count, span_rows, model_width)
    back_weights = (
        lax.all_gather(attention_gain, ("fsdp", "seq"), axis=0, tiled=True),
        lax.all_gather(query_weight, ("fsdp", "seq"), axis=0, tiled=True),
        lax.all_gather(key_weight, ("fsdp", "seq"), axis=0, tiled=True),
        lax.all_gather(value_weight, ("fsdp", "seq"), axis=0, tiled=True),
        lax.all_gather(output_weight, ("fsdp", "seq"), axis=0, tiled=True),
        lax.all_gather(feedforward_gain, ("fsdp", "seq"), axis=0, tiled=True),
        lax.all_gather(gate_weight, ("fsdp", "seq"), axis=0, tiled=True),
        lax.all_gather(up_weight, ("fsdp", "seq"), axis=0, tiled=True),
        lax.all_gather(down_weight, ("fsdp", "seq"), axis=0, tiled=True),
    )
    (
        gain_one_back,
        query_back_w,
        key_back_w,
        value_back_w,
        output_back_w,
        gain_two_back,
        gate_back_w,
        up_back_w,
        down_back_w,
    ) = back_weights
    gain_one_b = gain_one_back.astype(jnp.float32)
    gain_two_b = gain_two_back.astype(jnp.float32)
    cot_rows = cotangent.reshape(row_count, model_width)
    down_term = matmul(hidden.T, cot_rows)
    grad_hidden = matmul(cot_rows, down_back_w.T)
    grad_gate = (grad_hidden * up_rows * sigma * (1.0 + gate_rows * (1.0 - sigma))).astype(
        jnp.bfloat16
    )
    grad_up = (grad_hidden * gate_rows * sigma).astype(jnp.bfloat16)
    gate_term = matmul(normed_mid.T, grad_gate)
    up_term = matmul(normed_mid.T, grad_up)
    grad_normed_mid = matmul(grad_gate, gate_back_w.T) + matmul(grad_up, up_back_w.T)
    grad_mid_norm, gain_two_term = norm_bwd(residual_mid, factor_two, gain_two_b, grad_normed_mid)
    grad_mid = cot_rows.astype(jnp.float32) + grad_mid_norm
    grad_mid_half = grad_mid.astype(jnp.bfloat16)
    output_term = matmul(attn_out.T, grad_mid_half)
    grad_attn_out = matmul(grad_mid_half, output_back_w.T).astype(jnp.bfloat16)
    grad_heads = lax.all_to_all(
        grad_attn_out.reshape(seq_count, span_rows, H * HD),
        "seq",
        split_axis=2,
        concat_axis=1,
        tiled=True,
    )
    grad_query_heads, grad_key_heads, grad_value_heads = jax.vmap(attend_bwd)(
        queries,
        keys_local,
        values_local,
        outputs,
        log_totals,
        grad_heads.reshape(seq_count, full_length, local_heads, HD),
        doc_start,
    )
    head_shape = (seq_count, full_length, local_heads * HD)
    query_home, key_home, value_home = (
        lax.all_to_all(
            shortened(grad_query_heads.reshape(head_shape)),
            "seq",
            split_axis=1,
            concat_axis=2,
            tiled=True,
        ),
        lax.all_to_all(
            shortened(grad_key_heads.reshape(head_shape)),
            "seq",
            split_axis=1,
            concat_axis=2,
            tiled=True,
        ),
        lax.all_to_all(
            shortened(grad_value_heads.reshape(head_shape)),
            "seq",
            split_axis=1,
            concat_axis=2,
            tiled=True,
        ),
    )
    grad_key_sum = fold_groups(key_home)
    grad_value_rows = fold_groups(value_home).astype(jnp.bfloat16)
    _, query_back = jax.vjp(query_side, query_raw, query_scale)
    grad_query_raw, query_gain_term = query_back(
        query_home.reshape(row_count, H * HD).astype(jnp.float32)
    )
    _, key_back = jax.vjp(key_side, key_raw, key_scale)
    grad_key_raw, key_gain_term = key_back(grad_key_sum)
    grad_query_half = grad_query_raw.astype(jnp.bfloat16)
    grad_key_half = grad_key_raw.astype(jnp.bfloat16)
    query_term = matmul(normed_in.T, grad_query_half)
    key_term = matmul(normed_in.T, grad_key_half)
    value_term = matmul(normed_in.T, grad_value_rows)
    grad_normed_in = (
        matmul(grad_query_half, query_back_w.T)
        + matmul(grad_key_half, key_back_w.T)
        + matmul(grad_value_rows, value_back_w.T)
    )
    grad_in_norm, gain_one_term = norm_bwd(residual_in, factor_one, gain_one_b, grad_normed_in)
    input_grad = (
        (grad_mid + grad_in_norm).astype(jnp.bfloat16).reshape(seq_count, span_rows, model_width)
    )
    reduced = (
        lax.psum_scatter(gain_one_term, ("fsdp", "seq"), scatter_dimension=0, tiled=True),
        lax.psum_scatter(query_term, ("fsdp", "seq"), scatter_dimension=0, tiled=True),
        lax.psum_scatter(key_term, ("fsdp", "seq"), scatter_dimension=0, tiled=True),
        lax.psum_scatter(value_term, ("fsdp", "seq"), scatter_dimension=0, tiled=True),
        lax.psum_scatter(output_term, ("fsdp", "seq"), scatter_dimension=0, tiled=True),
        lax.psum_scatter(gain_two_term, ("fsdp", "seq"), scatter_dimension=0, tiled=True),
        lax.psum_scatter(gate_term, ("fsdp", "seq"), scatter_dimension=0, tiled=True),
        lax.psum_scatter(up_term, ("fsdp", "seq"), scatter_dimension=0, tiled=True),
        lax.psum_scatter(down_term, ("fsdp", "seq"), scatter_dimension=0, tiled=True),
    )
    (
        gain_one_grad,
        query_grad,
        key_grad,
        value_grad,
        output_grad,
        gain_two_grad,
        gate_grad,
        up_grad,
        down_grad,
    ) = reduced
    query_gain_grad, key_gain_grad = lax.psum((query_gain_term, key_gain_term), ("fsdp", "seq"))
    return (
        block_output,
        input_grad,
        gain_one_grad,
        query_grad,
        key_grad,
        value_grad,
        query_gain_grad,
        key_gain_grad,
        output_grad,
        gain_two_grad,
        gate_grad,
        up_grad,
        down_grad,
    )


def solution(mesh):
    return jax.shard_map(
        body,
        mesh=mesh,
        in_specs=(
            P("fsdp", "seq", None),
            P("fsdp", None),
            P("fsdp", "seq", None),
            P(("fsdp", "seq")),
            P(("fsdp", "seq"), None),
            P(("fsdp", "seq"), None),
            P(("fsdp", "seq"), None),
            P(),
            P(),
            P(("fsdp", "seq"), None),
            P(("fsdp", "seq")),
            P(("fsdp", "seq"), None),
            P(("fsdp", "seq"), None),
            P(("fsdp", "seq"), None),
        ),
        out_specs=(
            P("fsdp", "seq", None),
            P("fsdp", "seq", None),
            P(("fsdp", "seq")),
            P(("fsdp", "seq"), None),
            P(("fsdp", "seq"), None),
            P(("fsdp", "seq"), None),
            P(),
            P(),
            P(("fsdp", "seq"), None),
            P(("fsdp", "seq")),
            P(("fsdp", "seq"), None),
            P(("fsdp", "seq"), None),
            P(("fsdp", "seq"), None),
        ),
        check_vma=False,
    )
```

profile of v0, /device:TPU:0, one launch (start us, length us, event | category | flops | bytes accessed | tf_op | source)
XLA Modules:
  0.0 1808.4 jit_solution(11954303523884179258)
XLA Ops:
  13.6 42.0 %all-reduce.11 = (bf16[1024]{0:T(1024)(128)(2,1)S(1)}, bf16[1024]{0:T(1024)(128)(2,1)}) all-reduce(bf16[1024]{0:T(1024)(128)(2,1)S(1)} %dynamic-update-slice.16, bf16[1024]{0:T(1024)(128)(2,1)S(1)} %dynamic-update-slice.17), channel_id=1, replica_groups=mesh['fsdp'=4,'seq'=8] {'fsdp','seq'}, use_global_device_ids=true, to_apply=%add.6 | all-reduce | flops 2048 | bytes 8192
  70.1 4.2 all-to-all-start
  74.3 48.6 %all-gather.12.cloned.1.call-done = bf16[1024,512]{1,0:T(8,128)(2,1)} async-done(((bf16[32,512]{1,0:T(8,128)(2,1)}), bf16[1024,512]{1,0:T(8,128)(2,1)}) %all-gather.12.cloned.1.call-update) | async-done | bytes 1048592 | tf_op jit(solution)/shard_map/all_gather | solution.py:152
  127.4 53.7 %all-gather.10.cloned.1.call-done = bf16[1024,1024]{1,0:T(8,128)(2,1)} async-done(((bf16[32,1024]{1,0:T(8,128)(2,1)}), bf16[1024,1024]{1,0:T(8,128)(2,1)}) %all-gather.10.cloned.1.call-update) | async-done | bytes 2097168 | tf_op jit(solution)/shard_map/all_gather | solution.py:151
  181.1 3.9 copy.82
  190.1 4.1 all-to-all-start.2
  196.8 3.8 convert_element_type.218
  204.0 4.7 all-to-all-start.1
  229.8 4.4 fusion.1
  250.4 3.9 fusion.34
  258.4 4.2 all-to-all-start.3
  263.3 15.8 all-to-all-done.3
  286.1 40.8 %all-gather.16.cloned.1.call-done = bf16[1024,4608]{1,0:T(8,128)(2,1)} async-done(((bf16[32,4608]{1,0:T(8,128)(2,1)}), bf16[1024,4608]{1,0:T(8,128)(2,1)}) %all-gather.16.cloned.1.call-update) | async-done | bytes 9437200 | tf_op jit(solution)/shard_map/all_gather | solution.py:156
  326.9 9.8 fusion.80
  336.8 73.7 %all-gather.18.cloned.1.call-done = bf16[1024,4608]{1,0:T(8,128)(2,1)} async-done(((bf16[32,4608]{1,0:T(8,128)(2,1)}), bf16[1024,4608]{1,0:T(8,128)(2,1)}) %all-gather.18.cloned.1.call-update) | async-done | bytes 9437200 | tf_op jit(solution)/shard_map/all_gather | solution.py:157
  410.4 9.6 fusion.81
  420.0 74.0 %all-gather.20.cloned.1.call-done = bf16[4608,1024]{1,0:T(8,128)(2,1)} async-done(((bf16[144,1024]{1,0:T(8,128)(2,1)}), bf16[4608,1024]{1,0:T(8,128)(2,1)}) %all-gather.20.cloned.1.call-update) | async-done | bytes 9437200 | tf_op jit(solution)/shard_map/all_gather | solution.py:158
  494.0 13.8 multiply_convert_fusion.2
  507.8 8.8 fusion.82
  516.7 7.4 multiply_reduce_fusion
  531.5 19.2 %all_to_all.102 = bf16[2,192,1024]{1,0,2:T(2,128)(2,1)S(1)} all-to-all(bf16[2,192,1024]{1,0,2:T(2,128)(2,1)} %copy.90), channel_id=1, replica_groups=mesh['fsdp'=4,'seq'=8] {'seq'}, dimensions={2} | all-to-all | bytes 1572864 | tf_op jit(solution)/shard_map/all_to_all | solution.py:283
  556.7 8.0 multiply_convert_fusion
  564.8 7.9 multiply_convert_fusion.1
  582.9 16.2 all_to_all.103
  600.5 4.0 copy.103
  604.5 3.8 reshape.662
  616.8 3.8 convolution_bitcast_fusion.4
  620.9 5.1 fusion.31
  627.0 4.7 fusion.11
  634.7 18.3 %all_to_all.105 = bf16[2,1536,128]{2,0,1:T(2,128)(2,1)S(1)} all-to-all(bf16[2,1536,128]{2,0,1:T(2,128)(2,1)} %copy.105), channel_id=1, replica_groups=mesh['fsdp'=4,'seq'=8] {'seq'}, dimensions={1} | all-to-all | bytes 1572864 | tf_op jit(solution)/shard_map/all_to_all | solution.py:315
  664.8 4.9 fusion.36
  669.8 5.7 convolution_convert_fusion.2
  677.3 4.4 convolution_convert_fusion.6
  688.2 4.6 pad_maximum_fusion.2
  692.8 17.0 all_to_all.104
  711.3 4.0 copy.99
  715.3 3.8 reshape.661
  727.0 11.2 fusion.88
  738.2 11.2 fusion.89
  750.5 11.1 fusion.90
  763.0 9.6 add_convert_fusion
  777.0 39.7 %all-reduce.10 = (f32[1024]{0:T(1024)S(1)}, f32[64]{0:T(128)}, f32[64]{0:T(128)}, f32[1024]{0:T(1024)S(1)}) all-reduce(f32[1024]{0:T(1024)S(1)} %get-tuple-element.105, f32[64]{0:T(128)S(1)} %get-tuple-element.103, f32[64]{0:T(128)S(1)} %get-tuple-element.107, ...), channel_id=2, replica_groups=mesh['fsdp'=4,'seq'=8] {'fsdp','seq'}, use_global_device_ids=true, to_apply=%region_18.19.clone | all-reduce | flops 2176 | bytes 17408
  820.6 67.0 %reduce-scatter.12.cloned.1.call-done = f32[32,512]{1,0:T(8,128)} async-done(((f32[1024,512]{1,0:T(8,128)}), f32[32,512]{1,0:T(8,128)}) %reduce-scatter.12.cloned.1.call-update) | async-done | bytes 65552 | tf_op jit(solution)/shard_map/reduce_scatter | solution.py:349
  887.6 139.4 %reduce-scatter.14.cloned.1.call-done = f32[32,1024]{1,0:T(8,128)} async-done(((f32[1024,1024]{1,0:T(8,128)}), f32[32,1024]{1,0:T(8,128)}) %reduce-scatter.14.cloned.1.call-update) | async-done | bytes 131088 | tf_op jit(solution)/shard_map/reduce_scatter | solution.py:350
  1027.0 139.7 %reduce-scatter.8.cloned.1.call-done = f32[32,1024]{1,0:T(8,128)} async-done(((f32[1024,1024]{1,0:T(8,128)}), f32[32,1024]{1,0:T(8,128)}) %reduce-scatter.8.cloned.1.call-update) | async-done | bytes 131088 | tf_op jit(solution)/shard_map/reduce_scatter | solution.py:347
  1166.8 209.6 %reduce-scatter.16.cloned.1.call-done = f32[32,4608]{1,0:T(8,128)} async-done(((f32[1024,4608]{1,0:T(8,128)}), f32[32,4608]{1,0:T(8,128)}) %reduce-scatter.16.cloned.1.call-update) | async-done | bytes 589840 | tf_op jit(solution)/shard_map/reduce_scatter | solution.py:352
  1376.3 212.6 %reduce-scatter.18.cloned.1.call-done = f32[32,4608]{1,0:T(8,128)} async-done(((f32[1024,4608]{1,0:T(8,128)}), f32[32,4608]{1,0:T(8,128)}) %reduce-scatter.18.cloned.1.call-update) | async-done | bytes 589840 | tf_op jit(solution)/shard_map/reduce_scatter | solution.py:353
  1588.9 212.5 %reduce-scatter.20.cloned.1.call-done = f32[144,1024]{1,0:T(8,128)} async-done(((f32[4608,1024]{1,0:T(8,128)}), f32[144,1024]{1,0:T(8,128)}) %reduce-scatter.20.cloned.1.call-update) | async-done | bytes 589840 | tf_op jit(solution)/shard_map/reduce_scatter | solution.py:354
  (313 shorter events, 162.3 us)
Async XLA Ops:
  7.2 55.0 %copy-start.1 = (bf16[2,192,1024]{2,1,0:T(8,128)(2,1)S(1)}, bf16[2,192,1024]{2,1,0:T(8,128)(2,1)}, u32[]{:S(2)}) copy-start(bf16[2,192,1024]{2,1,0:T(8,128)(2,1)} %param.30) | copy-start | bytes 2359300
  7.2 60.1 %all-gather.8.cloned.1.call-start = ((), (), s32[]{:S(2)}) async-start(), calls=%async_computation.15 | async-start | bytes 1081344 | tf_op jit(solution)/shard_map/all_gather | solution.py:153
  7.9 115.0 %all-gather.12.cloned.1.call-start = ((), (), s32[]{:S(2)}) async-start(), calls=%async_computation.17 | async-start | bytes 1081344 | tf_op jit(solution)/shard_map/all_gather | solution.py:152
  8.7 172.5 %all-gather.10.cloned.1.call-start = ((), (), s32[]{:S(2)}) async-start(), calls=%async_computation.16 | async-start | bytes 2162688 | tf_op jit(solution)/shard_map/all_gather | solution.py:151
  9.4 272.4 %all-gather.14.cloned.1.call-start = ((), (), s32[]{:S(2)}) async-start(), calls=%async_computation.18 | async-start | bytes 2162688 | tf_op jit(solution)/shard_map/all_gather | solution.py:154
  10.0 317.0 %all-gather.16.cloned.1.call-start = ((), (), s32[]{:S(2)}) async-start(), calls=%async_computation.19 | async-start | bytes 9732096 | tf_op jit(solution)/shard_map/all_gather | solution.py:156
  10.6 399.8 %all-gather.18.cloned.1.call-start = ((), (), s32[]{:S(2)}) async-start(), calls=%async_computation.20 | async-start | bytes 9732096 | tf_op jit(solution)/shard_map/all_gather | solution.py:157
  11.1 482.8 %all-gather.20.cloned.1.call-start = ((), (), s32[]{:S(2)}) async-start(), calls=%async_computation.21 | async-start | bytes 9732096 | tf_op jit(solution)/shard_map/all_gather | solution.py:158
  55.6 10.0 copy-start.55
  57.1 8.5 copy-start.61
  57.8 67.4 %copy-start.72 = (f32[64]{0:T(128)}, f32[64]{0:T(128)S(1)}, u32[]{:S(2)}) copy-start(f32[64]{0:T(128)S(1)} %convert_element_type.219) | copy-start | bytes 772
  59.3 128.7 %copy-start.74 = (f32[64]{0:T(128)}, f32[64]{0:T(128)S(1)}, u32[]{:S(2)}) copy-start(f32[64]{0:T(128)S(1)} %convert_element_type.215) | copy-start | bytes 772
  60.4 133.8 %copy-start.39 = (f32[384,32]{0,1:T(8,128)}, f32[384,32]{0,1:T(8,128)S(1)}, u32[]{:S(2)}) copy-start(f32[384,32]{0,1:T(8,128)S(1)} %get-tuple-element.132) | copy-start | bytes 147460
  60.4 133.8 %copy-start.41 = (f32[384,32]{0,1:T(8,128)}, f32[384,32]{0,1:T(8,128)S(1)}, u32[]{:S(2)}) copy-start(f32[384,32]{0,1:T(8,128)S(1)} %get-tuple-element.133) | copy-start | bytes 147460
  70.1 119.9 %all-to-all-start = ((bf16[2,192,512]{1,0,2:T(2,128)(2,1)}), bf16[2,192,512]{1,0,2:T(2,128)(2,1)}, u32[]{:S(2)}, u32[]{:S(2)}) async-start(bf16[2,192,512]{1,0,2:T(2,128)(2,1)} %copy.79), calls=%async_computation | async-start | bytes 1048576 | tf_op jit(solution)/shard_map/all_to_all | solution.py:220
  125.1 59.9 %copy-start.59 = (f32[384,8]{0,1:T(8,128)}, f32[384,8]{0,1:T(8,128)S(1)}, u32[]{:S(2)}) copy-start(f32[384,8]{0,1:T(8,128)S(1)} %get-tuple-element.134) | copy-start | bytes 36868
  188.0 8.9 copy-start.57
  190.1 13.9 all-to-all-start.2
  204.0 20.1 %all-to-all-start.1 = ((bf16[2,192,1024]{1,0,2:T(2,128)(2,1)}), bf16[2,192,1024]{1,0,2:T(2,128)(2,1)}, u32[]{:S(2)}, u32[]{:S(2)}) async-start(bf16[2,192,1024]{1,0,2:T(2,128)(2,1)} %convert_element_type.218), calls=%async_computation.1 | async-start | bytes 2097152 | tf_op jit(solution)/shard_map/all_to_all | solution.py:212
  221.9 12.4 copy-start.24
  234.3 16.1 copy-start.6
  238.1 12.3 copy-start.65
  258.4 20.8 %all-to-all-start.3 = ((bf16[2,1536,128]{2,0,1:T(2,128)(2,1)}), bf16[2,1536,128]{2,0,1:T(2,128)(2,1)}, u32[]{:S(2)}, u32[]{:S(2)}) async-start(bf16[2,1536,128]{2,0,1:T(2,128)(2,1)} %copy.87), calls=%async_computation.3 | async-start | bytes 1572864 | tf_op jit(solution)/shard_map/all_to_all | solution.py:227
  262.6 558.0 %reduce-scatter.10.cloned.1.call-start = ((), (), s32[]{:S(2)}) async-start(), calls=%async_computation.23 | async-start | bytes 2162688 | tf_op jit(solution)/shard_map/reduce_scatter | solution.py:348
  507.8 8.8 copy-start.25
  507.8 8.8 copy-start.12
  507.8 8.8 copy-start.64
  556.6 8.1 copy-start.18
  556.7 8.1 copy-start.26
  556.7 8.1 copy-start.52
  556.7 8.1 copy-start.68
  564.7 13.0 copy-start
  564.8 7.9 copy-start.21
  564.8 7.9 copy-start.35
  564.8 7.9 copy-start.54
  564.8 7.9 copy-start.71
  616.7 270.8 %reduce-scatter.12.cloned.1.call-start = ((), (), s32[]{:S(2)}) async-start(), calls=%async_computation.24 | async-start | bytes 2162688 | tf_op jit(solution)/shard_map/reduce_scatter | solution.py:349
  616.8 9.1 slice-start
  664.6 362.4 %reduce-scatter.14.cloned.1.call-start = ((), (), s32[]{:S(2)}) async-start(), calls=%async_computation.25 | async-start | bytes 4325376 | tf_op jit(solution)/shard_map/reduce_scatter | solution.py:350
  669.8 497.0 %reduce-scatter.8.cloned.1.call-start = ((), (), s32[]{:S(2)}) async-start(), calls=%async_computation.22 | async-start | bytes 4325376 | tf_op jit(solution)/shard_map/reduce_scatter | solution.py:347
  726.6 649.7 %reduce-scatter.16.cloned.1.call-start = ((), (), s32[]{:S(2)}) async-start(), calls=%async_computation.26 | async-start | bytes 19464192 | tf_op jit(solution)/shard_map/reduce_scatter | solution.py:352
  738.2 850.7 %reduce-scatter.18.cloned.1.call-start = ((), (), s32[]{:S(2)}) async-start(), calls=%async_computation.27 | async-start | bytes 19464192 | tf_op jit(solution)/shard_map/reduce_scatter | solution.py:353
  749.4 1052.0 %reduce-scatter.20.cloned.1.call-start = ((), (), s32[]{:S(2)}) async-start(), calls=%async_computation.28 | async-start | bytes 19464192 | tf_op jit(solution)/shard_map/reduce_scatter | solution.py:354
  763.0 9.7 copy-start.16
  763.0 9.7 copy-start.23
  763.0 10.3 copy-start.31
  763.0 10.3 copy-start.36
  774.8 43.0 %copy-start.5 = (f32[384,1024]{1,0:T(8,128)S(1)}, f32[384,1024]{1,0:T(8,128)}, u32[]{:S(2)}) copy-start(f32[384,1024]{1,0:T(8,128)} %copy-done.4) | copy-start | bytes 4718596
  (51 other events, 168.9 us)
Sparse Core Ops, SparseCore 0:
  10.9 56.3 all-gather.7
  70.1 52.7 all-gather.11
  125.8 55.3 all-gather.9
  183.8 56.0 all-gather.13
  242.6 84.2 all-gather.15
  329.7 80.6 all-gather.17
  413.3 80.6 all-gather.19
  616.9 134.9 reduce-scatter.9
  754.7 132.7 reduce-scatter.11
  890.3 136.6 reduce-scatter.13
  1029.9 136.8 reduce-scatter.7
  1173.6 202.6 reduce-scatter.15
  1383.3 205.5 reduce-scatter.17
  1595.7 205.6 reduce-scatter.19
where the time goes:
time: 1820 us; the launch traced here: 1810 us
  waiting for transfers between devices  1300 us (71%)
  matrix products  182 us (10%)
  blocking collectives  152 us (8%)
  local copies, waits for them, and re-layouts  92.4 us (5%)
  other arithmetic  49.9 us (3%)
  starting transfers between devices  18.2 us (1%)
    reduce_scatter x1, waiting for transfers between devices, body(): lax.psum_scatter(up_term, ('fsdp', 'seq'), scatter_dimension=0, tiled=True)  213 us
    reduce_scatter x1, waiting for transfers between devices, body(): lax.psum_scatter(down_term, ('fsdp', 'seq'), scatter_dimension=0, tiled=T...  213 us
    reduce_scatter x1, waiting for transfers between devices, body(): lax.psum_scatter(gate_term, ('fsdp', 'seq'), scatter_dimension=0, tiled=T...  210 us
    reduce_scatter x1, waiting for transfers between devices, body(): lax.psum_scatter(query_term, ('fsdp', 'seq'), scatter_dimension=0, tiled=...  140 us
    reduce_scatter x1, waiting for transfers between devices, body(): lax.psum_scatter(output_term, ('fsdp', 'seq'), scatter_dimension=0, tiled...  139 us
    dot_general x21, matrix products, matmul(): return jnp.dot(left, right, preferred_element_type=jnp.float32)  119 us
    unnamed x2, blocking collectives  81.7 us
    all_gather x1, waiting for transfers between devices, body(): lax.all_gather(down_weight, ('fsdp', 'seq'), axis=0, tiled=True)  74 us
  transfers between devices with their start and end apart: 18, of which 15 were waited for; matrix products, arithmetic and copies ran while one was open for 13% of the time, Pallas kernels for 0%

commit v1 on v0

v1 whole, which is shorter than its diff:
```python
import jax
import jax.numpy as jnp
from jax import lax
from jax.sharding import PartitionSpec as P

H = 16
KV = 8
HD = 64

rope_base = 1000000.0
eps = 1e-05
masked = -1e30
f32 = jnp.float32
bf16 = jnp.bfloat16


def contract(formula, left, right):
    return jnp.einsum(formula, left, right, preferred_element_type=f32)


def matmul(left, right):
    return jnp.dot(left, right, preferred_element_type=f32)


def matmul_nt(left, right):
    return lax.dot_general(left, right, (((1,), (1,)), ((), ())), preferred_element_type=f32)


def matmul_tn(left, right):
    return lax.dot_general(left, right, (((0,), (0,)), ((), ())), preferred_element_type=f32)


def rope_tables(places, head_width):
    half_width = head_width // 2
    inverse = rope_base ** (-(jnp.arange(half_width, dtype=f32) * 2.0) / head_width)
    angles = places.astype(f32)[:, None] * inverse[None, :]
    return (jnp.cos(angles)[:, None, :], jnp.sin(angles)[:, None, :])


def head_prep(raw_rows, gain_row, cosine, sine, head_count):
    row_count = raw_rows.shape[0]
    split_rows = raw_rows.reshape(row_count, head_count, -1)
    factor = lax.rsqrt(jnp.mean(split_rows * split_rows, axis=-1, keepdims=True) + eps)
    normed = split_rows * factor * gain_row
    half_width = normed.shape[-1] // 2
    lower = normed[..., :half_width]
    upper = normed[..., half_width:]
    turned = jnp.concatenate(
        [lower * cosine - upper * sine, upper * cosine + lower * sine], axis=-1
    )
    return turned.reshape(row_count, -1)


def inv_rms(values):
    return lax.rsqrt(jnp.mean(values * values, axis=-1, keepdims=True) + eps)


def norm_bwd(values, factor, gain_row, grad_result):
    normed = values * factor
    grad_normed = grad_result * gain_row
    return factor * (
        grad_normed - normed * jnp.mean(grad_normed * normed, axis=-1, keepdims=True)
    )


def masked_scores(queries, key_rows, doc_start, begin_row, end_row, scaling):
    query_index = jnp.arange(begin_row, end_row, dtype=jnp.int32)
    key_index = jnp.arange(end_row, dtype=jnp.int32)
    allowed = (key_index[None, :] <= query_index[:, None]) & (
        key_index[None, :] >= doc_start[begin_row:end_row, None]
    )
    scores = contract("qhd,khd->hqk", queries[begin_row:end_row], key_rows[:end_row]) * scaling
    return jnp.where(allowed[None, :, :], scores, masked)


def attend_fwd(queries, key_rows, value_rows, doc_start):
    seq_length, head_count, head_width = queries.shape
    block_rows = min(512, seq_length)
    scaling = head_width ** (-0.5)
    out_blocks = []
    total_blocks = []
    for begin_row in range(0, seq_length, block_rows):
        end_row = begin_row + block_rows
        scores = masked_scores(queries, key_rows, doc_start, begin_row, end_row, scaling)
        largest = jnp.max(scores, axis=-1, keepdims=True)
        log_total = largest + jnp.log(jnp.sum(jnp.exp(scores - largest), axis=-1, keepdims=True))
        attn_prob = jnp.exp(scores - log_total).astype(bf16)
        out_blocks.append(contract("hqk,khd->qhd", attn_prob, value_rows[:end_row]).astype(bf16))
        total_blocks.append(log_total[..., 0])
    return (jnp.concatenate(out_blocks, axis=0), jnp.concatenate(total_blocks, axis=1))


def attend_bwd(queries, key_rows, value_rows, outputs, log_totals, grad_result, doc_start):
    seq_length, head_count, head_width = queries.shape
    block_rows = min(512, seq_length)
    scaling = head_width ** (-0.5)
    carried = jnp.sum(grad_result.astype(f32) * outputs.astype(f32), axis=-1).T
    grad_query = []
    grad_key = jnp.zeros((seq_length, head_count, head_width), f32)
    grad_value = jnp.zeros((seq_length, head_count, head_width), f32)
    for begin_row in range(0, seq_length, block_rows):
        end_row = begin_row + block_rows
        scores = masked_scores(queries, key_rows, doc_start, begin_row, end_row, scaling)
        attn_prob = jnp.exp(scores - log_totals[:, begin_row:end_row, None])
        prob_half = attn_prob.astype(bf16)
        grad_rows = grad_result[begin_row:end_row]
        grad_value = grad_value.at[:end_row].add(contract("hqk,qhd->khd", prob_half, grad_rows))
        grad_prob = contract("qhd,khd->hqk", grad_rows, value_rows[:end_row])
        grad_score = (
            attn_prob * (grad_prob - carried[:, begin_row:end_row, None]) * scaling
        ).astype(bf16)
        grad_query.append(contract("hqk,khd->qhd", grad_score, key_rows[:end_row]))
        grad_key = grad_key.at[:end_row].add(
            contract("hqk,qhd->khd", grad_score, queries[begin_row:end_row])
        )
    return (
        jnp.concatenate(grad_query, axis=0).astype(bf16),
        grad_key.astype(bf16),
        grad_value.astype(bf16),
    )


def swap(array, mask):
    groups = lax.axis_size("seq")
    return lax.ppermute(array, "seq", [(i, i ^ mask) for i in range(groups)])


def partner_blocks(block):
    half = block.shape[0] // 2
    got = {0: block}
    got[2] = swap(block, 2)
    got[4] = swap(block, 4)
    got[1] = swap(block, 1)
    via_x = swap(got[4][:half], 2)
    via_y = swap(got[2][half:], 4)
    got[3] = swap(got[2], 1)
    got[5] = swap(got[4], 1)
    got[6] = jnp.concatenate([via_x, via_y], axis=0)
    got[7] = swap(got[6], 1)
    return [got[j] for j in range(8)]


def gather_seq(block, axis):
    if lax.axis_size("seq") != 8 or block.shape[0] % 2:
        return lax.all_gather(block, "seq", axis=axis, tiled=True)
    me = lax.axis_index("seq")
    width = block.shape[axis]
    shape = list(block.shape)
    shape[axis] = width * 8
    whole = jnp.zeros(shape, block.dtype)
    for j, part in enumerate(partner_blocks(block)):
        whole = lax.dynamic_update_slice_in_dim(whole, part, (me ^ j) * width, axis)
    return whole


def reduce_seq(partial, axis):
    groups = lax.axis_size("seq")
    width = partial.shape[axis] // groups
    if groups != 8 or partial.shape[0] % 2:
        return lax.psum_scatter(partial, "seq", scatter_dimension=axis, tiled=True).astype(f32)
    me = lax.axis_index("seq")
    half = partial.shape[0] // 2

    def piece(j):
        return lax.dynamic_slice_in_dim(partial, (me ^ j) * width, width, axis)

    got = swap(jnp.stack([piece(j) for j in (1, 3, 5, 7)]), 1)
    held = {j: piece(j).astype(f32) + got[j // 2].astype(f32) for j in (0, 2, 4, 6)}
    first = {j: held[j][:half] for j in held}
    second = {j: held[j][half:] for j in held}
    sent_x = swap(jnp.stack([first[2].astype(bf16), first[6].astype(bf16)]), 2)
    sent_y = swap(jnp.stack([second[4].astype(bf16), second[6].astype(bf16)]), 4)
    last_y = swap((first[4] + sent_x[1].astype(f32)).astype(bf16), 4)
    last_x = swap((second[2] + sent_y[1].astype(f32)).astype(bf16), 2)
    own_first = first[0] + sent_x[0].astype(f32) + last_y.astype(f32)
    own_second = second[0] + sent_y[0].astype(f32) + last_x.astype(f32)
    return jnp.concatenate([own_first, own_second], axis=0)


def line_step(array, step):
    size = lax.axis_size("fsdp")
    return lax.ppermute(
        array, "fsdp", [(i, i + step) for i in range(size) if 0 <= i + step < size]
    )


def gather_line(block):
    size = lax.axis_size("fsdp")
    if size != 4:
        return lax.all_gather(block, "fsdp", axis=0, tiled=False)
    me = lax.axis_index("fsdp")
    below, above = [block], [block]
    for _ in range(size - 1):
        below.append(line_step(below[-1], 1))
        above.append(line_step(above[-1], -1))
    whole = jnp.zeros((size,) + block.shape, block.dtype)
    whole = lax.dynamic_update_index_in_dim(whole, block, me, 0)
    for k in range(1, size):
        part = below[k] + above[size - k]
        whole = lax.dynamic_update_index_in_dim(whole, part, lax.rem(me - k + size, size), 0)
    return whole


def reduce_line(partial):
    size = lax.axis_size("fsdp")
    if size != 4:
        return lax.psum_scatter(
            partial.astype(bf16), "fsdp", scatter_dimension=0, tiled=False
        ).astype(f32)
    me = lax.axis_index("fsdp")

    def entry(k):
        return lax.dynamic_index_in_dim(
            partial, lax.rem(me + k + size, size), 0, keepdims=False
        ).astype(f32)

    up, down = entry(size - 1), entry(1 - size)
    for k in range(size - 2, -1, -1):
        got_up = line_step(up.astype(bf16), 1).astype(f32)
        got_down = line_step(down.astype(bf16), -1).astype(f32)
        if k:
            up, down = entry(k) + got_up, entry(-k) + got_down
    return entry(0) + got_up + got_down


def spread(blocks):
    return lax.all_to_all(blocks, "seq", split_axis=0, concat_axis=0, tiled=True)


def sum_everywhere(vector):
    groups, size = lax.axis_size("seq"), lax.axis_size("fsdp")
    if groups != 8 or size != 4:
        return lax.psum(vector, ("fsdp", "seq"))
    for mask in (1, 2, 4):
        vector = vector + swap(vector, mask)
    for mask in (1, 2):
        vector = vector + lax.ppermute(vector, "fsdp", [(i, i ^ mask) for i in range(size)])
    return vector


def body(
    block_input,
    positions,
    cotangent,
    attention_gain,
    query_weight,
    key_weight,
    value_weight,
    query_gain,
    key_gain,
    output_weight,
    feedforward_gain,
    gate_weight,
    up_weight,
    down_weight,
):
    seq_count, span, width = block_input.shape
    groups = lax.axis_size("seq")
    size = lax.axis_size("fsdp")
    me = lax.axis_index("seq")
    length = span * groups
    rows = seq_count * length
    own_rows = seq_count * span
    shard = query_weight.shape[0]
    heads = H // groups
    kv_heads = max(1, KV // groups)
    copies = max(1, groups // KV)
    q_cols, k_cols = heads * HD, kv_heads * HD
    qkv_cols = q_cols + 2 * k_cols
    part = gate_weight.shape[1] // (groups * size)
    hidden_cols = part * size

    x_full = gather_seq(block_input, 1)

    def columns(weight, col_copies):
        shaped = weight.reshape(shard, -1, 1, HD)
        shaped = jnp.broadcast_to(shaped, (shard, shaped.shape[1], col_copies, HD))
        return shaped.reshape(shard, groups, -1)

    packed = jnp.concatenate(
        [
            columns(query_weight, 1),
            columns(key_weight, copies),
            columns(value_weight, copies),
        ],
        axis=2,
    ).transpose(1, 0, 2)
    gains = jnp.concatenate([attention_gain, feedforward_gain])
    gain_rows = jnp.zeros((16, qkv_cols), bf16).at[0, : 2 * shard].set(gains)
    packed = jnp.concatenate(
        [packed, jnp.broadcast_to(gain_rows[None], (groups, 16, qkv_cols))], axis=1
    )
    packed = gather_line(spread(packed))
    w_qkv = packed[:, :, :shard, :].reshape(width, qkv_cols)
    gain_one = packed[:, :, shard, :shard].reshape(width).astype(f32)
    gain_two = packed[:, :, shard, shard : 2 * shard].reshape(width).astype(f32)

    out_full = lax.all_gather(output_weight, ("fsdp", "seq"), axis=0, tiled=True)

    def ff_columns(weight):
        shaped = weight.reshape(shard, size, groups, part)
        return shaped.transpose(2, 0, 1, 3).reshape(groups, shard, hidden_cols)

    w_gate_up = gather_line(
        spread(jnp.concatenate([ff_columns(gate_weight), ff_columns(up_weight)], axis=2))
    ).reshape(width, 2 * hidden_cols)
    w_gate = w_gate_up[:, :hidden_cols]
    w_up = w_gate_up[:, hidden_cols:]
    w_down = gather_line(down_weight).reshape(hidden_cols, width)

    cot_full = gather_seq(cotangent, 1).reshape(rows, width)

    residual_in = x_full.reshape(rows, width).astype(f32)
    factor_one = inv_rms(residual_in)
    normed_in = (residual_in * factor_one * gain_one).astype(bf16)
    qkv_raw = matmul(normed_in, w_qkv)
    query_raw = qkv_raw[:, :q_cols]
    key_raw = qkv_raw[:, q_cols : q_cols + k_cols]
    value_rows = qkv_raw[:, q_cols + k_cols :].astype(bf16)
    cosine, sine = rope_tables(positions.reshape(rows), HD)
    query_scale = query_gain.astype(f32)
    key_scale = key_gain.astype(f32)

    def query_side(raw_rows, gain_row):
        return head_prep(raw_rows, gain_row, cosine, sine, heads)

    def key_side(raw_rows, gain_row):
        return head_prep(raw_rows, gain_row, cosine, sine, kv_heads)

    def head_view(packed_rows):
        shaped = packed_rows.reshape(seq_count, length, -1, HD)
        return jnp.repeat(shaped, heads // shaped.shape[2], axis=2)

    queries = query_side(query_raw, query_scale).astype(bf16).reshape(seq_count, length, heads, HD)
    keys = head_view(key_side(key_raw, key_scale).astype(bf16))
    values = head_view(value_rows)
    doc_start = jnp.arange(length, dtype=jnp.int32)[None, :] - positions
    outputs, log_totals = jax.vmap(attend_fwd)(queries, keys, values, doc_start)

    attn_full = gather_seq(outputs.reshape(seq_count, length, q_cols), 2)
    attn_rows = attn_full.reshape(rows, width)
    residual_mid = residual_in + matmul(attn_rows, out_full)
    factor_two = inv_rms(residual_mid)
    normed_mid = (residual_mid * factor_two * gain_two).astype(bf16)

    def own(array):
        shaped = array.reshape(seq_count, length, -1)
        return lax.dynamic_slice_in_dim(shaped, me * span, span, 1).reshape(own_rows, -1)

    gate_rows = matmul(normed_mid, w_gate)
    up_rows = matmul(normed_mid, w_up)
    sigma = jax.nn.sigmoid(gate_rows)
    hidden = (gate_rows * sigma * up_rows).astype(bf16)
    grad_hidden = matmul_nt(cot_full, w_down)
    grad_gate = (grad_hidden * up_rows * sigma * (1.0 + gate_rows * (1.0 - sigma))).astype(bf16)
    grad_up = (grad_hidden * gate_rows * sigma).astype(bf16)
    grad_normed_part = (matmul_nt(grad_gate, w_gate) + matmul_nt(grad_up, w_up)).astype(bf16)
    grad_normed_mid = reduce_seq(grad_normed_part.reshape(seq_count, length, width), 1)
    grad_normed_mid = grad_normed_mid.reshape(own_rows, width)

    residual_own = own(residual_mid)
    cot_rows = cotangent.reshape(own_rows, width).astype(f32)
    grad_mid = cot_rows + norm_bwd(residual_own, own(factor_two), gain_two, grad_normed_mid)
    grad_mid_half = grad_mid.astype(bf16)
    grad_attn_out = matmul_nt(grad_mid_half, out_full).astype(bf16)
    grad_heads = lax.all_to_all(
        grad_attn_out.reshape(seq_count, span, width), "seq", split_axis=2, concat_axis=1, tiled=True
    )

    grad_query_heads, grad_key_heads, grad_value_heads = jax.vmap(attend_bwd)(
        queries,
        keys,
        values,
        outputs,
        log_totals,
        grad_heads.reshape(seq_count, length, heads, HD),
        doc_start,
    )

    def fold(packed_rows):
        shaped = packed_rows.reshape(rows, kv_heads, -1, HD).astype(f32)
        return jnp.sum(shaped, axis=2).reshape(rows, k_cols)

    _, query_back = jax.vjp(query_side, query_raw, query_scale)
    grad_query_raw, query_gain_term = query_back(grad_query_heads.reshape(rows, q_cols).astype(f32))
    _, key_back = jax.vjp(key_side, key_raw, key_scale)
    grad_key_raw, key_gain_term = key_back(fold(grad_key_heads))
    grad_qkv = jnp.concatenate(
        [
            grad_query_raw.astype(bf16),
            grad_key_raw.astype(bf16),
            fold(grad_value_heads).astype(bf16),
        ],
        axis=1,
    )
    grad_in_part = matmul_nt(grad_qkv, w_qkv).astype(bf16)
    grad_normed_in = reduce_seq(grad_in_part.reshape(seq_count, length, width), 1)
    grad_normed_in = grad_normed_in.reshape(own_rows, width)
    own_in = block_input.reshape(own_rows, width).astype(f32)
    input_grad = (
        (grad_mid + norm_bwd(own_in, inv_rms(own_in), gain_one, grad_normed_in))
        .astype(bf16)
        .reshape(seq_count, span, width)
    )

    result_part = matmul(hidden, w_down).astype(bf16).reshape(seq_count, length, width)
    block_output = (
        (residual_own + reduce_seq(result_part, 1).reshape(own_rows, width))
        .astype(bf16)
        .reshape(seq_count, span, width)
    )

    down_grad = reduce_line(matmul_tn(hidden, cot_full).reshape(size, part, width))
    gate_up_term = matmul_tn(normed_mid, jnp.concatenate([grad_gate, grad_up], axis=1))
    gate_up_term = reduce_line(gate_up_term.reshape(size, groups * shard, 2 * hidden_cols))
    gate_up_home = spread(gate_up_term.astype(bf16).reshape(groups, shard, 2 * hidden_cols))

    def ff_home(columns_home):
        shaped = columns_home.astype(f32).reshape(groups, shard, size, part)
        return shaped.transpose(1, 2, 0, 3).reshape(shard, groups * size * part)

    gate_grad = ff_home(gate_up_home[:, :, :hidden_cols])
    up_grad = ff_home(gate_up_home[:, :, hidden_cols:])

    output_term = matmul_tn(own(attn_rows), grad_mid_half).astype(bf16)
    output_grad = lax.psum_scatter(
        output_term, ("fsdp", "seq"), scatter_dimension=0, tiled=True
    ).astype(f32)

    qkv_term = reduce_line(matmul_tn(normed_in, grad_qkv).reshape(size, groups * shard, qkv_cols))
    qkv_home = spread(qkv_term.astype(bf16).reshape(groups, shard, qkv_cols)).astype(f32)

    def home(block, col_copies):
        shaped = block.transpose(1, 0, 2).reshape(shard, -1, col_copies, HD)
        return jnp.sum(shaped, axis=2).reshape(shard, -1)

    query_grad = home(qkv_home[:, :, :q_cols], 1)
    key_grad = home(qkv_home[:, :, q_cols : q_cols + k_cols], copies)
    value_grad = home(qkv_home[:, :, q_cols + k_cols :], copies)

    def weighted(weight, grad):
        return jnp.sum(weight.astype(f32) * grad, axis=1)

    gain_one_grad = (
        weighted(query_weight, query_grad)
        + weighted(key_weight, key_grad)
        + weighted(value_weight, value_grad)
    ) / attention_gain.astype(f32)
    gain_two_grad = (
        weighted(gate_weight, gate_grad) + weighted(up_weight, up_grad)
    ) / feedforward_gain.astype(f32)

    head_gains = sum_everywhere(jnp.concatenate([query_gain_term, key_gain_term])[None])[0]
    return (
        block_output,
        input_grad,
        gain_one_grad,
        query_grad,
        key_grad,
        value_grad,
        head_gains[:HD],
        head_gains[HD:],
        output_grad,
        gain_two_grad,
        gate_grad,
        up_grad,
        down_grad,
    )


def solution(mesh):
    shards = P(("fsdp", "seq"), None)
    vector = P(("fsdp", "seq"))
    tokens = P("fsdp", "seq", None)
    return jax.shard_map(
        body,
        mesh=mesh,
        in_specs=(
            tokens,
            P("fsdp", None),
            tokens,
            vector,
            shards,
            shards,
            shards,
            P(),
            P(),
            shards,
            vector,
            shards,
            shards,
            shards,
        ),
        out_specs=(
            tokens,
            tokens,
            vector,
            shards,
            shards,
            shards,
            P(),
            P(),
            shards,
            vector,
            shards,
            shards,
            shards,
        ),
        check_vma=False,
    )
```

time: 1820 us -> 792 us (0.44)
  waiting for transfers between devices: 1300 us -> 182 us
  blocking collectives: 152 us -> 0 us
  starting transfers between devices: 18.2 us -> 160 us
  other arithmetic: 49.9 us -> 134 us
  local copies, waits for them, and re-layouts: 92.4 us -> 134 us
  matrix products: 182 us -> 152 us
    reduce_scatter x6 -> x0, waiting for transfers between devices: 841 us -> none  [the longest x1 213 us: body(): lax.psum_scatter(up_term, ('fsdp', 'seq'), scatter_dimension=0, tiled=True)]
    all_gather x6 -> x0, waiting for transfers between devices: 292 us -> none  [the longest x1 74 us: body(): lax.all_gather(down_weight, ('fsdp', 'seq'), axis=0, tiled=True)]
    ppermute x0 -> x80, starting transfers between devices: none -> 140 us  [the longest x36 107 us: line_step(): lax.ppermute(array, 'fsdp', [(i, i + step) for i in range(size) if 0 <= i...]
    unnamed x2 -> x0, blocking collectives: 81.7 us -> none
    ppermute x0 -> x80, waiting for transfers between devices: none -> 81 us  [the longest x42 41 us: swap(): return lax.ppermute(array, 'seq', [(i, i ^ mask) for i in range(groups)])]
    all_to_all x4 -> x0, blocking collectives: 70.7 us -> none  [the longest x1 19.2 us: body(): lax.all_to_all(grad_attn_out.reshape(seq_count, span_rows, H * HD), 'seq'...]
    reduce_scatter x1, waiting for transfers between devices: 139 us -> 90 us  [body(): lax.psum_scatter(output_term, ('fsdp', 'seq'), scatter_dimension=0, tiled...]
    dot_general x39 -> x32, matrix products: 182 us -> 152 us  [the longest x18 52.7 us: contract(): return jnp.einsum(formula, left, right, preferred_element_type=f32)]
  transfers between devices with their start and end apart: 18 -> 87, of which waited for: 15 -> 24; matrix products, arithmetic and copies ran while one was open for 13% -> 41% of each run, Pallas kernels for 0% -> 0%
where the time goes in v1:
time: 792 us; the launch traced here: 779 us
  waiting for transfers between devices  182 us (23%)
  starting transfers between devices  160 us (20%)
  matrix products  152 us (19%)
  local copies, waits for them, and re-layouts  134 us (17%)
  other arithmetic  134 us (17%)
  between operations  17.2 us (2%)
    ppermute x36, starting transfers between devices, line_step(): lax.ppermute(array, 'fsdp', [(i, i + step) for i in range(size) if 0 <= i...  107 us
    reduce_scatter x1, waiting for transfers between devices, body(): lax.psum_scatter(output_term, ('fsdp', 'seq'), scatter_dimension=0, tiled...  90 us
    dot_general x18, matrix products, contract(): return jnp.einsum(formula, left, right, preferred_element_type=f32)  52.7 us
    ppermute x42, waiting for transfers between devices, swap(): return lax.ppermute(array, 'seq', [(i, i ^ mask) for i in range(groups)])  41 us
    ppermute x36, waiting for transfers between devices, line_step(): lax.ppermute(array, 'fsdp', [(i, i + step) for i in range(size) if 0 <= i...  40 us
    dot_general x5, matrix products, matmul(): return jnp.dot(left, right, preferred_element_type=f32)  39.3 us
    dot_general x5, matrix products, matmul_nt(): lax.dot_general(left, right, (((1,), (1,)), ((), ())), preferred_element_...  37.3 us
    dynamic_update_slice x24, local copies, waits for them, and re-layouts, gather_seq(): whole = lax.dynamic_update_slice_in_dim(whole, part, (me ^ j) * width, axis)  29.3 us
  transfers between devices with their start and end apart: 87, of which 24 were waited for; matrix products, arithmetic and copies ran while one was open for 41% of the time, Pallas kernels for 0%

profile of v1, /device:TPU:0, one launch (start us, length us, event | category | flops | bytes accessed | tf_op | source)
XLA Modules:
  0.0 778.8 jit_solution(14124845039403625754)
XLA Ops:
  8.6 6.3 collective-permute-start.28
  19.2 4.2 all-to-all-start
  39.5 4.2 all-to-all-start.1
  53.0 5.2 collective-permute-start.8
  60.9 5.9 collective-permute-start.32
  71.6 10.8 %collective-permute-done.12 = bf16[8,48,256]{2,1,0:T(8,128)(2,1)S(1)} collective-permute-done((bf16[8,48,256]{2,1,0:T(8,128)(2,1)}, bf16[8,48,256]{2,1,0:T(8,128)(2,1)S(1)}, u32[]{:S(2)}, u32[]{:S(2)}) %collective-permute-start.12) | collective-permute-done | bytes 196640 | tf_op jit(solution)/shard_map/ppermute | solution.py:182
  84.2 4.3 collective-permute-start.13
  110.2 4.1 collective-permute-start.33
  115.3 8.5 %collective-permute-done.42 = bf16[2,192,1024]{2,1,0:T(8,128)(2,1)} collective-permute-done((bf16[2,192,1024]{2,1,0:T(8,128)(2,1)S(1)}, bf16[2,192,1024]{2,1,0:T(8,128)(2,1)}, u32[]{:S(2)}, u32[]{:S(2)}) %collective-permute-start.42) | collective-permute-done | bytes 786464 | tf_op jit(solution)/shard_map/ppermute | solution.py:125
  139.2 4.6 collective-permute-start.22
  147.9 7.7 collective-permute-done.23
  158.0 5.8 collective-permute-start.26
  175.4 5.4 collective-permute-start.27
  219.6 3.7 exponential_reduce_fusion
  227.5 3.9 fusion.62
  236.6 6.9 fusion.4
  243.5 8.9 %copy.152 = bf16[1024,3072]{1,0:T(8,128)(2,1)} copy(bf16[1024,3072]{0,1:T(8,128)(2,1)} %bitcast.495) | data formatting | bytes 12582912 | tf_op jit(solution)/shard_map/dot_general | solution.py:30
  271.0 4.6 collective-permute-done.19
  284.2 10.9 %multiply_reduce_fusion = (f32[3072]{0:T(1024)S(1)}, f32[3072,1024]{1,0:T(8,128)S(1)}) fusion(bf16[3072,1024]{1,0:T(8,128)(2,1)} %bitcast.15, bf16[1024,1024]{1,0:T(8,128)(2,1)} %all-gather.2.cloned.1.call-done, bf16[2,1536,1024]{2,1,0:T(8,128)(2,1)} %copy-done.2), kind=kOutput, calls=%fused_computation.12 | convolution fusion | flops 6455030784 | bytes 27275264 | tf_op jit(solution)/shard_map/dot_general | solution.py:22
  299.7 6.0 fusion.70
  305.7 9.5 %fusion.12 = (bf16[576,3072]{1,0:T(8,128)(2,1)S(1)}, f32[3072,576]{0,1:T(8,128)}) fusion(f32[3072,576]{0,1:T(8,128)} %fusion.70, bf16[3072,1024]{1,0:T(8,128)(2,1)S(1)} %multiply_convert_fusion.1, bf16[1024,1152]{1,0:T(8,128)(2,1)S(1)} %bitcast.525), kind=kOutput, calls=%fused_computation.28 | convolution fusion | flops 3634495488 | bytes 25296896 | tf_op jit(solution)/shard_map/dot_general | solution.py:22
  315.2 11.0 %convolution_convert_fusion = bf16[3072,1024]{1,0:T(8,128)(2,1)} fusion(bf16[576,1024]{1,0:T(8,128)(2,1)} %bitcast.28, f32[3072,576]{0,1:T(8,128)} %get-tuple-element.212, f32[3072,576]{0,1:T(8,128)} %fusion.70), kind=kOutput, calls=%fused_computation.40 | convolution fusion | flops 3637641216 | bytes 21626880 | tf_op jit(solution)/shard_map/dot_general | solution.py:22
  326.2 11.4 %multiply_convert_fusion.3 = (bf16[3072,576]{0,1:T(8,128)(2,1)}, bf16[3072,576]{0,1:T(8,128)(2,1)}) fusion(f32[3072,576]{0,1:T(8,128)S(1)} %copy-done.134, f32[3072,576]{0,1:T(8,128)} %get-tuple-element.212, bf16[3072,1024]{1,0:T(8,128)(2,1)} %bitcast.47, bf16[576,1024]{1,0:T(8,128)(2,1)} %bitcast.28), kind=kOutput, calls=%fused_computation.34 | convolution fusion | flops 3646881792 | bytes 28704768 | tf_op jit(solution)/shard_map/dot_general | solution.py:26
  337.6 10.1 %fusion.68 = f32[3072,1024]{1,0:T(8,128)} fusion(bf16[3072,576]{0,1:T(8,128)(2,1)} %get-tuple-element.124, bf16[1024,1152]{1,0:T(8,128)(2,1)S(1)} %bitcast.526), kind=kOutput, calls=%fused_computation.156 | convolution fusion | flops 3623878656 | bytes 17432576 | tf_op jit(solution)/shard_map/dot_general | solution.py:26
  347.7 10.7 %fusion.8 = f32[1024,1152]{1,0:T(8,128)S(1)} fusion(bf16[3072,1024]{1,0:T(8,128)(2,1)S(1)} %multiply_convert_fusion.1, bf16[3072,576]{0,1:T(8,128)(2,1)} %get-tuple-element.123, bf16[3072,576]{0,1:T(8,128)(2,1)} %get-tuple-element.124), kind=kOutput, calls=%fused_computation.23 | convolution fusion | flops 7261913088 | bytes 18087936 | tf_op jit(solution)/shard_map/dot_general | solution.py:30
  358.4 11.4 %add_convert_fusion = bf16[3072,1024]{1,0:T(8,128)(2,1)S(1)} fusion(f32[3072,1024]{1,0:T(8,128)} %fusion.68, bf16[3072,576]{0,1:T(8,128)(2,1)} %get-tuple-element.123, bf16[1024,1152]{1,0:T(8,128)(2,1)S(1)} %bitcast.527), kind=kOutput, calls=%fused_computation.10 | convolution fusion | flops 3630170112 | bytes 23724032 | tf_op jit(solution)/shard_map/dot_general | solution.py:26
  378.8 5.9 fusion.173
  386.3 5.1 collective-permute-start.74
  396.2 5.2 collective-permute-start.69
  402.5 3.9 collective-permute-start.75
  410.7 8.9 %collective-permute-done.75 = bf16[144,1024]{1,0:T(8,128)(2,1)S(1)} collective-permute-done((bf16[144,1024]{1,0:T(8,128)(2,1)S(1)}, bf16[144,1024]{1,0:T(8,128)(2,1)S(1)}, u32[]{:S(2)}, u32[]{:S(2)}) %collective-permute-start.75) | collective-permute-done | bytes 294944 | tf_op jit(solution)/shard_map/ppermute | solution.py:182
  422.8 5.7 collective-permute-start.76
  431.2 4.6 collective-permute-start.70
  435.8 4.3 convert_add_fusion.4
  441.0 4.0 collective-permute-done.72
  448.8 8.4 %collective-permute-done.50 = bf16[2,1,192,1024]{3,2,1,0:T(8,128)(2,1)S(1)} collective-permute-done((bf16[2,1,192,1024]{3,2,1,0:T(8,128)(2,1)S(1)}, bf16[2,1,192,1024]{3,2,1,0:T(8,128)(2,1)S(1)}, u32[]{:S(2)}, u32[]{:S(2)}) %collective-permute-start.50) | collective-permute-done | bytes 786464 | tf_op jit(solution)/shard_map/ppermute | solution.py:125
  465.8 4.2 all-to-all-start.4
  496.2 5.7 all-to-all-done.2
  503.8 4.0 multiply_convert_fusion.6
  516.3 8.2 %multiply_convert_fusion = bf16[2,2,512,1536]{3,2,1,0:T(8,128)(2,1)S(1)} fusion(f32[2,2,512,1536]{3,2,1,0:T(8,128)} %copy-done.10, f32[2,2,512]{2,1,0:T(2,128)S(1)} %get-tuple-element.191, f32[2,2,512]{2,1,0:T(2,128)S(1)} %copy-done.118, pred[2,512,1536]{2,1,0:T(8,128)(4,1)S(1)} %copy-done.28, bf16[2,1536,64]{1,2,0:T(8,128)(2,1)S(1)} %bitcast.536, ...), kind=kOutput, calls=%fused_computation.9 | convolution fusion | flops 424673280 | bytes 21118976 | tf_op jit(solution)/shard_map/vmap(qhd,khd->hqk)/dot_general | solution.py:18
  552.9 5.0 fusion.51
  558.0 8.1 %fusion.52 = bf16[2,1536,64]{1,2,0:T(8,128)(2,1)} fusion(f32[2,1536,2,64]{1,3,2,0:T(8,128)S(1)} %fusion.51, bf16[2,1536,2,64]{1,3,2,0:T(8,128)(2,1)S(1)} %copy-done.49, f32[2,2,512,1536]{3,2,1,0:T(8,128)} %copy-done.10, f32[2,2,512]{2,1,0:T(2,128)S(1)} %copy-done.119, pred[2,512,1536]{2,1,0:T(8,128)(4,1)S(1)} %copy-done.29), kind=kOutput, calls=%fused_computation.124 | convolution fusion | flops 416219136 | bytes 16392192 | tf_op jit(solution)/shard_map/vmap(hqk,qhd->khd)/dot_general | solution.py:18
  595.8 4.6 collective-permute-start.58
  606.3 4.0 bitcast_convert_fusion
  620.9 4.7 collective-permute-done.62
  631.5 5.3 all-to-all-done.3
  643.9 7.2 convert_add_fusion
  659.6 90.0 %reduce-scatter.2.cloned.1.call-done = bf16[32,1024]{1,0:T(8,128)(2,1)} async-done(((bf16[1024,1024]{1,0:T(8,128)(2,1)}), bf16[32,1024]{1,0:T(8,128)(2,1)}) %reduce-scatter.2.cloned.1.call-update) | async-done | bytes 65552 | tf_op jit(solution)/shard_map/reduce_scatter | solution.py:426
  (688 shorter events, 368.8 us)
Async XLA Ops:
  7.2 52.4 %collective-permute-start.29 = (bf16[144,1024]{1,0:T(8,128)(2,1)}, bf16[144,1024]{1,0:T(8,128)(2,1)}, u32[]{:S(2)}, u32[]{:S(2)}) collective-permute-start(bf16[144,1024]{1,0:T(8,128)(2,1)} %param.45), channel_id=1, source_target_pairs={{8,0},{16,8},{24,16},{9,1},{17,9},{25,17},{10,2},{18,10},{26,18},{... | collective-permute-start | bytes 884744 | tf_op jit(solution)/shard_map/ppermute | solution.py:182
  8.6 52.3 %collective-permute-start.28 = (bf16[144,1024]{1,0:T(8,128)(2,1)}, bf16[144,1024]{1,0:T(8,128)(2,1)}, u32[]{:S(2)}, u32[]{:S(2)}) collective-permute-start(bf16[144,1024]{1,0:T(8,128)(2,1)} %param.45), channel_id=1, source_target_pairs={{0,8},{8,16},{16,24},{1,9},{9,17},{17,25},{2,10},{10,18},{18,26},{... | collective-permute-start | bytes 884744 | tf_op jit(solution)/shard_map/ppermute | solution.py:182
  19.2 20.3 %all-to-all-start = ((bf16[8,48,256]{2,1,0:T(8,128)(2,1)}), bf16[8,48,256]{2,1,0:T(8,128)(2,1)S(1)}, u32[]{:S(2)}, u32[]{:S(2)}) async-start(bf16[8,48,256]{2,1,0:T(8,128)(2,1)} %copy.110), calls=%async_computation | async-start | bytes 393216 | tf_op jit(solution)/shard_map/all_to_all | solution.py:227
  23.3 260.8 %all-gather.2.cloned.1.call-start = ((), (), s32[]{:S(2)}) async-start(), calls=%async_computation.6 | async-start | bytes 2162688 | tf_op jit(solution)/shard_map/all_gather | solution.py:298
  23.4 68.6 %collective-permute-start = (bf16[2,192,1024]{2,1,0:T(8,128)(2,1)}, bf16[2,192,1024]{2,1,0:T(8,128)(2,1)}, u32[]{:S(2)}, u32[]{:S(2)}) collective-permute-start(bf16[2,192,1024]{2,1,0:T(8,128)(2,1)} %param.32), channel_id=1, source_target_pairs={{0,1},{1,0},{2,3},{3,2},{4,5},{5,4},{6,7},{7,6},{8,9},{9,8},{10,11... | collective-permute-start | bytes 2359304 | tf_op jit(solution)/shard_map/ppermute | solution.py:125
  39.5 31.9 %all-to-all-start.1 = ((bf16[8,32,1152]{2,1,0:T(8,128)(2,1)}), bf16[8,32,1152]{2,1,0:T(8,128)(2,1)S(1)}, u32[]{:S(2)}, u32[]{:S(2)}) async-start(bf16[8,32,1152]{2,1,0:T(8,128)(2,1)} %pad_maximum_fusion.13), calls=%async_computation.1 | async-start | bytes 1179648 | tf_op jit(solution)/shard_map/all_to_all | solution.py:227
  59.6 30.0 %collective-permute-start.30 = (bf16[144,1024]{1,0:T(8,128)(2,1)}, bf16[144,1024]{1,0:T(8,128)(2,1)S(1)}, u32[]{:S(2)}, u32[]{:S(2)}) collective-permute-start(bf16[144,1024]{1,0:T(8,128)(2,1)} %collective-permute-done.29), channel_id=1, source_target_pairs={{8,0},{16,8},{24,16},{9,1},{17,9},{25,17},{10,2},{18,10},{26,18},{... | collective-permute-start | bytes 884744 | tf_op jit(solution)/shard_map/ppermute | solution.py:182
  60.9 30.2 %collective-permute-start.32 = (bf16[144,1024]{1,0:T(8,128)(2,1)}, bf16[144,1024]{1,0:T(8,128)(2,1)}, u32[]{:S(2)}, u32[]{:S(2)}) collective-permute-start(bf16[144,1024]{1,0:T(8,128)(2,1)} %collective-permute-done.28), channel_id=1, source_target_pairs={{0,8},{8,16},{16,24},{1,9},{9,17},{17,25},{2,10},{10,18},{18,26},{... | collective-permute-start | bytes 884744 | tf_op jit(solution)/shard_map/ppermute | solution.py:182
  82.5 20.6 %collective-permute-start.1 = (bf16[2,192,1024]{2,1,0:T(8,128)(2,1)S(1)}, bf16[2,192,1024]{2,1,0:T(8,128)(2,1)}, u32[]{:S(2)}, u32[]{:S(2)}) collective-permute-start(bf16[2,192,1024]{2,1,0:T(8,128)(2,1)S(1)} %copy-done.8), channel_id=1, source_target_pairs={{0,2},{1,3},{2,0},{3,1},{4,6},{5,7},{6,4},{7,5},{8,10},{9,11},{10,... | collective-permute-start | bytes 2359304 | tf_op jit(solution)/shard_map/ppermute | solution.py:125
  89.6 20.6 %collective-permute-start.3 = (bf16[2,192,1024]{2,1,0:T(8,128)(2,1)S(1)}, bf16[2,192,1024]{2,1,0:T(8,128)(2,1)}, u32[]{:S(2)}, u32[]{:S(2)}) collective-permute-start(bf16[2,192,1024]{2,1,0:T(8,128)(2,1)S(1)} %copy-done.8), channel_id=1, source_target_pairs={{0,4},{1,5},{2,6},{3,7},{4,0},{5,1},{6,2},{7,3},{8,12},{9,13},{10,... | collective-permute-start | bytes 2359304 | tf_op jit(solution)/shard_map/ppermute | solution.py:125
  91.1 34.3 %collective-permute-start.39 = (bf16[2,192,1024]{2,1,0:T(8,128)(2,1)S(1)}, bf16[2,192,1024]{2,1,0:T(8,128)(2,1)}, u32[]{:S(2)}, u32[]{:S(2)}) collective-permute-start(bf16[2,192,1024]{2,1,0:T(8,128)(2,1)S(1)} %copy-done.13), channel_id=1, source_target_pairs={{0,1},{1,0},{2,3},{3,2},{4,5},{5,4},{6,7},{7,6},{8,9},{9,8},{10,11... | collective-permute-start | bytes 2359304 | tf_op jit(solution)/shard_map/ppermute | solution.py:125
  91.6 37.3 %collective-permute-start.40 = (bf16[2,192,1024]{2,1,0:T(8,128)(2,1)S(1)}, bf16[2,192,1024]{2,1,0:T(8,128)(2,1)}, u32[]{:S(2)}, u32[]{:S(2)}) collective-permute-start(bf16[2,192,1024]{2,1,0:T(8,128)(2,1)S(1)} %copy-done.13), channel_id=1, source_target_pairs={{0,2},{1,3},{2,0},{3,1},{4,6},{5,7},{6,4},{7,5},{8,10},{9,11},{10,... | collective-permute-start | bytes 2359304 | tf_op jit(solution)/shard_map/ppermute | solution.py:125
  92.0 31.8 %collective-permute-start.42 = (bf16[2,192,1024]{2,1,0:T(8,128)(2,1)S(1)}, bf16[2,192,1024]{2,1,0:T(8,128)(2,1)}, u32[]{:S(2)}, u32[]{:S(2)}) collective-permute-start(bf16[2,192,1024]{2,1,0:T(8,128)(2,1)S(1)} %copy-done.13), channel_id=1, source_target_pairs={{0,4},{1,5},{2,6},{3,7},{4,0},{5,1},{6,2},{7,3},{8,12},{9,13},{10,... | collective-permute-start | bytes 2359304 | tf_op jit(solution)/shard_map/ppermute | solution.py:125
  103.1 29.8 %collective-permute-start.31 = (bf16[144,1024]{1,0:T(8,128)(2,1)S(1)}, bf16[144,1024]{1,0:T(8,128)(2,1)S(1)}, u32[]{:S(2)}, u32[]{:S(2)}) collective-permute-start(bf16[144,1024]{1,0:T(8,128)(2,1)S(1)} %collective-permute-done.30), channel_id=1, source_target_pairs={{8,0},{16,8},{24,16},{9,1},{17,9},{25,17},{10,2},{18,10},{26,18},{... | collective-permute-start | bytes 884744 | tf_op jit(solution)/shard_map/ppermute | solution.py:182
  110.2 26.0 %collective-permute-start.33 = (bf16[144,1024]{1,0:T(8,128)(2,1)}, bf16[144,1024]{1,0:T(8,128)(2,1)S(1)}, u32[]{:S(2)}, u32[]{:S(2)}) collective-permute-start(bf16[144,1024]{1,0:T(8,128)(2,1)} %collective-permute-done.32), channel_id=1, source_target_pairs={{0,8},{8,16},{16,24},{1,9},{9,17},{17,25},{2,10},{10,18},{18,26},{... | collective-permute-start | bytes 884744 | tf_op jit(solution)/shard_map/ppermute | solution.py:182
  136.2 21.9 %collective-permute-start.2 = (bf16[2,192,1024]{2,1,0:T(8,128)(2,1)}, bf16[2,192,1024]{2,1,0:T(8,128)(2,1)S(1)}, u32[]{:S(2)}, u32[]{:S(2)}) collective-permute-start(bf16[2,192,1024]{2,1,0:T(8,128)(2,1)} %collective-permute-done.1), channel_id=1, source_target_pairs={{0,1},{1,0},{2,3},{3,2},{4,5},{5,4},{6,7},{7,6},{8,9},{9,8},{10,11... | collective-permute-start | bytes 2359304 | tf_op jit(solution)/shard_map/ppermute | solution.py:125
  137.9 17.6 %collective-permute-start.23 = (bf16[8,32,1152]{2,1,0:T(8,128)(2,1)S(1)}, bf16[8,32,1152]{2,1,0:T(8,128)(2,1)S(1)}, u32[]{:S(2)}, u32[]{:S(2)}) collective-permute-start(bf16[8,32,1152]{2,1,0:T(8,128)(2,1)S(1)} %all-to-all-done.1), channel_id=1, source_target_pairs={{8,0},{16,8},{24,16},{9,1},{17,9},{25,17},{10,2},{18,10},{26,18},{... | collective-permute-start | bytes 1769480 | tf_op jit(solution)/shard_map/ppermute | solution.py:182
  139.2 17.5 %collective-permute-start.22 = (bf16[8,32,1152]{2,1,0:T(8,128)(2,1)S(1)}, bf16[8,32,1152]{2,1,0:T(8,128)(2,1)S(1)}, u32[]{:S(2)}, u32[]{:S(2)}) collective-permute-start(bf16[8,32,1152]{2,1,0:T(8,128)(2,1)S(1)} %all-to-all-done.1), channel_id=1, source_target_pairs={{0,8},{8,16},{16,24},{1,9},{9,17},{17,25},{2,10},{10,18},{18,26},{... | collective-permute-start | bytes 1769480 | tf_op jit(solution)/shard_map/ppermute | solution.py:182
  143.8 21.3 %collective-permute-start.4 = (bf16[2,192,1024]{2,1,0:T(8,128)(2,1)}, bf16[2,192,1024]{2,1,0:T(8,128)(2,1)S(1)}, u32[]{:S(2)}, u32[]{:S(2)}) collective-permute-start(bf16[2,192,1024]{2,1,0:T(8,128)(2,1)} %collective-permute-done.3), channel_id=1, source_target_pairs={{0,1},{1,0},{2,3},{3,2},{4,5},{5,4},{6,7},{7,6},{8,9},{9,8},{10,11... | collective-permute-start | bytes 2359304 | tf_op jit(solution)/shard_map/ppermute | solution.py:125
  145.7 19.7 %collective-permute-start.41 = (bf16[2,192,1024]{2,1,0:T(8,128)(2,1)}, bf16[2,192,1024]{2,1,0:T(8,128)(2,1)S(1)}, u32[]{:S(2)}, u32[]{:S(2)}) collective-permute-start(bf16[2,192,1024]{2,1,0:T(8,128)(2,1)} %collective-permute-done.40), channel_id=1, source_target_pairs={{0,1},{1,0},{2,3},{3,2},{4,5},{5,4},{6,7},{7,6},{8,9},{9,8},{10,11... | collective-permute-start | bytes 2359304 | tf_op jit(solution)/shard_map/ppermute | solution.py:125
  156.7 17.4 %collective-permute-start.24 = (bf16[8,32,1152]{2,1,0:T(8,128)(2,1)S(1)}, bf16[8,32,1152]{2,1,0:T(8,128)(2,1)}, u32[]{:S(2)}, u32[]{:S(2)}) collective-permute-start(bf16[8,32,1152]{2,1,0:T(8,128)(2,1)S(1)} %collective-permute-done.23), channel_id=1, source_target_pairs={{8,0},{16,8},{24,16},{9,1},{17,9},{25,17},{10,2},{18,10},{26,18},{... | collective-permute-start | bytes 1769480 | tf_op jit(solution)/shard_map/ppermute | solution.py:182
  158.0 17.4 %collective-permute-start.26 = (bf16[8,32,1152]{2,1,0:T(8,128)(2,1)S(1)}, bf16[8,32,1152]{2,1,0:T(8,128)(2,1)}, u32[]{:S(2)}, u32[]{:S(2)}) collective-permute-start(bf16[8,32,1152]{2,1,0:T(8,128)(2,1)S(1)} %collective-permute-done.22), channel_id=1, source_target_pairs={{0,8},{8,16},{16,24},{1,9},{9,17},{17,25},{2,10},{10,18},{18,26},{... | collective-permute-start | bytes 1769480 | tf_op jit(solution)/shard_map/ppermute | solution.py:182
  165.4 87.0 %collective-permute-start.46 = (bf16[2,192,1024]{2,1,0:T(8,128)(2,1)}, bf16[2,192,1024]{2,1,0:T(8,128)(2,1)}, u32[]{:S(2)}, u32[]{:S(2)}) collective-permute-start(bf16[2,192,1024]{2,1,0:T(8,128)(2,1)} %constant_dynamic-update-slice_fusion.28), channel_id=1, source_target_pairs={{0,1},{1,0},{2,3},{3,2},{4,5},{5,4},{6,7},{7,6},{8,9},{9,8},{10,11... | collective-permute-start | bytes 2359304 | tf_op jit(solution)/shard_map/ppermute | solution.py:125
  174.1 84.9 %collective-permute-start.25 = (bf16[8,32,1152]{2,1,0:T(8,128)(2,1)}, bf16[8,32,1152]{2,1,0:T(8,128)(2,1)}, u32[]{:S(2)}, u32[]{:S(2)}) collective-permute-start(bf16[8,32,1152]{2,1,0:T(8,128)(2,1)} %collective-permute-done.24), channel_id=1, source_target_pairs={{8,0},{16,8},{24,16},{9,1},{17,9},{25,17},{10,2},{18,10},{26,18},{... | collective-permute-start | bytes 1769480 | tf_op jit(solution)/shard_map/ppermute | solution.py:182
  175.4 86.3 %collective-permute-start.27 = (bf16[8,32,1152]{2,1,0:T(8,128)(2,1)}, bf16[8,32,1152]{2,1,0:T(8,128)(2,1)}, u32[]{:S(2)}, u32[]{:S(2)}) collective-permute-start(bf16[8,32,1152]{2,1,0:T(8,128)(2,1)} %collective-permute-done.26), channel_id=1, source_target_pairs={{0,8},{8,16},{16,24},{1,9},{9,17},{17,25},{2,10},{10,18},{18,26},{... | collective-permute-start | bytes 1769480 | tf_op jit(solution)/shard_map/ppermute | solution.py:182
  234.7 28.3 %collective-permute-start.17 = (bf16[2,1536,128]{2,1,0:T(8,128)(2,1)}, bf16[2,1536,128]{2,1,0:T(8,128)(2,1)}, u32[]{:S(2)}, u32[]{:S(2)}) collective-permute-start(bf16[2,1536,128]{2,1,0:T(8,128)(2,1)} %copy.121), channel_id=1, source_target_pairs={{0,4},{1,5},{2,6},{3,7},{4,0},{5,1},{6,2},{7,3},{8,12},{9,13},{10,... | collective-permute-start | bytes 2359304 | tf_op jit(solution)/shard_map/ppermute | solution.py:125
  236.0 29.5 %collective-permute-start.15 = (bf16[2,1536,128]{2,1,0:T(8,128)(2,1)}, bf16[2,1536,128]{2,1,0:T(8,128)(2,1)}, u32[]{:S(2)}, u32[]{:S(2)}) collective-permute-start(bf16[2,1536,128]{2,1,0:T(8,128)(2,1)} %copy.121), channel_id=1, source_target_pairs={{0,2},{1,3},{2,0},{3,1},{4,6},{5,7},{6,4},{7,5},{8,10},{9,11},{10,... | collective-permute-start | bytes 2359304 | tf_op jit(solution)/shard_map/ppermute | solution.py:125
  374.3 61.5 %collective-permute-start.47 = (bf16[4,2,192,1024]{3,2,1,0:T(8,128)(2,1)}, bf16[4,2,192,1024]{3,2,1,0:T(8,128)(2,1)}, u32[]{:S(2)}, u32[]{:S(2)}) collective-permute-start(bf16[4,2,192,1024]{3,2,1,0:T(8,128)(2,1)} %pad_maximum_fusion.1), channel_id=1, source_target_pairs={{0,1},{1,0},{2,3},{3,2},{4,5},{5,4},{6,7},{7,6},{8,9},{9,8},{10,11... | collective-permute-start | bytes 9437192 | tf_op jit(solution)/shard_map/ppermute | solution.py:125
  375.7 19.2 %collective-permute-start.68 = (bf16[256,1152]{1,0:T(8,128)(2,1)S(1)}, bf16[256,1152]{1,0:T(8,128)(2,1)S(1)}, u32[]{:S(2)}, u32[]{:S(2)}) collective-permute-start(bf16[256,1152]{1,0:T(8,128)(2,1)S(1)} %get-tuple-element.151), channel_id=1, source_target_pairs={{0,8},{8,16},{16,24},{1,9},{9,17},{17,25},{2,10},{10,18},{18,26},{... | collective-permute-start | bytes 1769480 | tf_op jit(solution)/shard_map/ppermute | solution.py:182
  391.4 19.4 %collective-permute-start.77 = (bf16[144,1024]{1,0:T(8,128)(2,1)}, bf16[144,1024]{1,0:T(8,128)(2,1)}, u32[]{:S(2)}, u32[]{:S(2)}) collective-permute-start(bf16[144,1024]{1,0:T(8,128)(2,1)} %get-tuple-element.156), channel_id=1, source_target_pairs={{8,0},{16,8},{24,16},{9,1},{17,9},{25,17},{10,2},{18,10},{26,18},{... | collective-permute-start | bytes 884744 | tf_op jit(solution)/shard_map/ppermute | solution.py:182
  392.7 35.9 %collective-permute-start.71 = (bf16[256,1152]{1,0:T(8,128)(2,1)}, bf16[256,1152]{1,0:T(8,128)(2,1)}, u32[]{:S(2)}, u32[]{:S(2)}) collective-permute-start(bf16[256,1152]{1,0:T(8,128)(2,1)} %get-tuple-element.152), channel_id=1, source_target_pairs={{8,0},{16,8},{24,16},{9,1},{17,9},{25,17},{10,2},{18,10},{26,18},{... | collective-permute-start | bytes 1769480 | tf_op jit(solution)/shard_map/ppermute | solution.py:182
  396.2 32.3 %collective-permute-start.69 = (bf16[256,1152]{1,0:T(8,128)(2,1)S(1)}, bf16[256,1152]{1,0:T(8,128)(2,1)S(1)}, u32[]{:S(2)}, u32[]{:S(2)}) collective-permute-start(bf16[256,1152]{1,0:T(8,128)(2,1)S(1)} %fusion.55), channel_id=1, source_target_pairs={{0,8},{8,16},{16,24},{1,9},{9,17},{17,25},{2,10},{10,18},{18,26},{... | collective-permute-start | bytes 1769480 | tf_op jit(solution)/shard_map/ppermute | solution.py:182
  402.5 17.2 %collective-permute-start.75 = (bf16[144,1024]{1,0:T(8,128)(2,1)S(1)}, bf16[144,1024]{1,0:T(8,128)(2,1)S(1)}, u32[]{:S(2)}, u32[]{:S(2)}) collective-permute-start(bf16[144,1024]{1,0:T(8,128)(2,1)S(1)} %fusion.93), channel_id=1, source_target_pairs={{0,8},{8,16},{16,24},{1,9},{9,17},{17,25},{2,10},{10,18},{18,26},{... | collective-permute-start | bytes 884744 | tf_op jit(solution)/shard_map/ppermute | solution.py:182
  421.5 24.1 %collective-permute-start.78 = (bf16[144,1024]{1,0:T(8,128)(2,1)S(1)}, bf16[144,1024]{1,0:T(8,128)(2,1)S(1)}, u32[]{:S(2)}, u32[]{:S(2)}) collective-permute-start(bf16[144,1024]{1,0:T(8,128)(2,1)S(1)} %get-tuple-element.154), channel_id=1, source_target_pairs={{8,0},{16,8},{24,16},{9,1},{17,9},{25,17},{10,2},{18,10},{26,18},{... | collective-permute-start | bytes 884744 | tf_op jit(solution)/shard_map/ppermute | solution.py:182
  422.8 67.4 %collective-permute-start.76 = (bf16[144,1024]{1,0:T(8,128)(2,1)}, bf16[144,1024]{1,0:T(8,128)(2,1)}, u32[]{:S(2)}, u32[]{:S(2)}) collective-permute-start(bf16[144,1024]{1,0:T(8,128)(2,1)} %get-tuple-element.153), channel_id=1, source_target_pairs={{0,8},{8,16},{16,24},{1,9},{9,17},{17,25},{2,10},{10,18},{18,26},{... | collective-permute-start | bytes 884744 | tf_op jit(solution)/shard_map/ppermute | solution.py:182
  431.2 32.7 %collective-permute-start.70 = (bf16[256,1152]{1,0:T(8,128)(2,1)S(1)}, bf16[256,1152]{1,0:T(8,128)(2,1)S(1)}, u32[]{:S(2)}, u32[]{:S(2)}) collective-permute-start(bf16[256,1152]{1,0:T(8,128)(2,1)S(1)} %get-tuple-element.149), channel_id=1, source_target_pairs={{0,8},{8,16},{16,24},{1,9},{9,17},{17,25},{2,10},{10,18},{18,26},{... | collective-permute-start | bytes 1769480 | tf_op jit(solution)/shard_map/ppermute | solution.py:182
  445.0 17.5 %collective-permute-start.48 = (bf16[2,1,192,1024]{3,2,1,0:T(8,128)(2,1)S(1)}, bf16[2,1,192,1024]{3,2,1,0:T(8,128)(2,1)S(1)}, u32[]{:S(2)}, u32[]{:S(2)}) collective-permute-start(bf16[2,1,192,1024]{3,2,1,0:T(8,128)(2,1)S(1)} %pad_maximum_fusion.9), channel_id=1, source_target_pairs={{0,2},{1,3},{2,0},{3,1},{4,6},{5,7},{6,4},{7,5},{8,10},{9,11},{10,... | collective-permute-start | bytes 2359304 | tf_op jit(solution)/shard_map/ppermute | solution.py:125
  445.6 19.2 %collective-permute-start.73 = (bf16[256,1152]{1,0:T(8,128)(2,1)S(1)}, bf16[256,1152]{1,0:T(8,128)(2,1)S(1)}, u32[]{:S(2)}, u32[]{:S(2)}) collective-permute-start(bf16[256,1152]{1,0:T(8,128)(2,1)S(1)} %fusion.54), channel_id=1, source_target_pairs={{8,0},{16,8},{24,16},{9,1},{17,9},{25,17},{10,2},{18,10},{26,18},{... | collective-permute-start | bytes 1769480 | tf_op jit(solution)/shard_map/ppermute | solution.py:182
  457.2 33.0 %collective-permute-start.79 = (bf16[144,1024]{1,0:T(8,128)(2,1)}, bf16[144,1024]{1,0:T(8,128)(2,1)}, u32[]{:S(2)}, u32[]{:S(2)}) collective-permute-start(bf16[144,1024]{1,0:T(8,128)(2,1)} %fusion.92), channel_id=1, source_target_pairs={{8,0},{16,8},{24,16},{9,1},{17,9},{25,17},{10,2},{18,10},{26,18},{... | collective-permute-start | bytes 884744 | tf_op jit(solution)/shard_map/ppermute | solution.py:182
  483.0 18.9 %all-to-all-start.2 = ((bf16[2,192,1024]{1,0,2:T(2,128)(2,1)}), bf16[2,192,1024]{1,0,2:T(2,128)(2,1)S(1)}, u32[]{:S(2)}, u32[]{:S(2)}) async-start(bf16[2,192,1024]{1,0,2:T(2,128)(2,1)} %copy.127), calls=%async_computation.2 | async-start | bytes 2097152 | tf_op jit(solution)/shard_map/all_to_all | solution.py:366
  486.5 263.0 %reduce-scatter.2.cloned.1.call-start = ((), (), s32[]{:S(2)}) async-start(), calls=%async_computation.7 | async-start | bytes 2162688 | tf_op jit(solution)/shard_map/reduce_scatter | solution.py:426
  489.8 154.0 %collective-permute-start.34 = (bf16[4,2,192,1024]{3,2,1,0:T(8,128)(2,1)}, bf16[4,2,192,1024]{3,2,1,0:T(8,128)(2,1)}, u32[]{:S(2)}, u32[]{:S(2)}) collective-permute-start(bf16[4,2,192,1024]{3,2,1,0:T(8,128)(2,1)} %pad_maximum_fusion), channel_id=1, source_target_pairs={{0,1},{1,0},{2,3},{3,2},{4,5},{5,4},{6,7},{7,6},{8,9},{9,8},{10,11... | collective-permute-start | bytes 9437192 | tf_op jit(solution)/shard_map/ppermute | solution.py:125
  543.0 39.1 %collective-permute-start.63 = (f32[1,128]{1,0:T(1,128)}, f32[1,128]{1,0:T(1,128)}, u32[]{:S(2)}, u32[]{:S(2)}) collective-permute-start(f32[1,128]{1,0:T(1,128)} %maximum_bitcast_fusion.2), channel_id=1, source_target_pairs={{0,1},{1,0},{2,3},{3,2},{4,5},{5,4},{6,7},{7,6},{8,9},{9,8},{10,11... | collective-permute-start | bytes 1544 | tf_op jit(solution)/shard_map/ppermute | solution.py:125
  575.4 68.5 %collective-permute-start.52 = (bf16[4,2,192,1024]{3,2,1,0:T(8,128)(2,1)}, bf16[4,2,192,1024]{3,2,1,0:T(8,128)(2,1)}, u32[]{:S(2)}, u32[]{:S(2)}) collective-permute-start(bf16[4,2,192,1024]{3,2,1,0:T(8,128)(2,1)} %pad_maximum_fusion.2), channel_id=1, source_target_pairs={{0,1},{1,0},{2,3},{3,2},{4,5},{5,4},{6,7},{7,6},{8,9},{9,8},{10,11... | collective-permute-start | bytes 9437192 | tf_op jit(solution)/shard_map/ppermute | solution.py:125
  652.4 98.9 %collective-permute-start.55 = (bf16[2,1,192,1024]{3,2,1,0:T(8,128)(2,1)}, bf16[2,1,192,1024]{3,2,1,0:T(8,128)(2,1)}, u32[]{:S(2)}, u32[]{:S(2)}) collective-permute-start(bf16[2,1,192,1024]{3,2,1,0:T(8,128)(2,1)} %pad_maximum_fusion.12), channel_id=1, source_target_pairs={{0,4},{1,5},{2,6},{3,7},{4,0},{5,1},{6,2},{7,3},{8,12},{9,13},{10,... | collective-permute-start | bytes 2359304 | tf_op jit(solution)/shard_map/ppermute | solution.py:125
  654.2 98.5 %collective-permute-start.53 = (bf16[2,1,192,1024]{3,2,1,0:T(8,128)(2,1)}, bf16[2,1,192,1024]{3,2,1,0:T(8,128)(2,1)}, u32[]{:S(2)}, u32[]{:S(2)}) collective-permute-start(bf16[2,1,192,1024]{3,2,1,0:T(8,128)(2,1)} %pad_maximum_fusion.11), channel_id=1, source_target_pairs={{0,2},{1,3},{2,0},{3,1},{4,6},{5,7},{6,4},{7,5},{8,10},{9,11},{10,... | collective-permute-start | bytes 2359304 | tf_op jit(solution)/shard_map/ppermute | solution.py:125
  655.9 98.3 %collective-permute-start.37 = (bf16[2,1,192,1024]{3,2,1,0:T(8,128)(2,1)}, bf16[2,1,192,1024]{3,2,1,0:T(8,128)(2,1)}, u32[]{:S(2)}, u32[]{:S(2)}) collective-permute-start(bf16[2,1,192,1024]{3,2,1,0:T(8,128)(2,1)} %pad_maximum_fusion.8), channel_id=1, source_target_pairs={{0,4},{1,5},{2,6},{3,7},{4,0},{5,1},{6,2},{7,3},{8,12},{9,13},{10,... | collective-permute-start | bytes 2359304 | tf_op jit(solution)/shard_map/ppermute | solution.py:125
  658.2 99.2 %collective-permute-start.35 = (bf16[2,1,192,1024]{3,2,1,0:T(8,128)(2,1)}, bf16[2,1,192,1024]{3,2,1,0:T(8,128)(2,1)}, u32[]{:S(2)}, u32[]{:S(2)}) collective-permute-start(bf16[2,1,192,1024]{3,2,1,0:T(8,128)(2,1)} %pad_maximum_fusion.7), channel_id=1, source_target_pairs={{0,2},{1,3},{2,0},{3,1},{4,6},{5,7},{6,4},{7,5},{8,10},{9,11},{10,... | collective-permute-start | bytes 2359304 | tf_op jit(solution)/shard_map/ppermute | solution.py:125
  (184 other events, 1848.9 us)
Sparse Core Ops, SparseCore 0:
  27.0 58.4 all-gather.1
  610.4 139.0 reduce-scatter.1

commit v2 on v1

--- a/solution.py
+++ b/solution.py
@@ -1,6 +1,10 @@
+import functools
+
 import jax
 import jax.numpy as jnp
 from jax import lax
+from jax.experimental import pallas as pl
+from jax.experimental.pallas import tpu as pltpu
 from jax.sharding import PartitionSpec as P
 
 H = 16
@@ -238,7 +242,586 @@
     return vector
 
 
-def body(
+exact = lax.Precision.HIGHEST
+
+
+def dot_nt(left, right, precision=None):
+    return lax.dot_general(left, right, (((1,), (1,)), ((), ())), precision=precision, preferred_element_type=f32)
+
+
+def dot_tn(left, right):
+    return lax.dot_general(left, right, (((0,), (0,)), ((), ())), preferred_element_type=f32)
+
+
+def head_mean():
+    row = lax.broadcasted_iota(jnp.int32, (128, 128), 0) // HD
+    col = lax.broadcasted_iota(jnp.int32, (128, 128), 1) // HD
+    return jnp.where(row == col, 1.0 / HD, 0.0).astype(f32)
+
+
+def lane_index(rows):
+    return lax.broadcasted_iota(jnp.int32, (rows, 128), 1)
+
+
+def half_turn(array, back):
+    low = (lane_index(array.shape[0]) % HD) < HD // 2
+    ahead = pltpu.roll(array, 128 - HD // 2, 1)
+    behind = pltpu.roll(array, HD // 2, 1)
+    return jnp.where(low, ahead, -behind) if back else jnp.where(low, -ahead, behind)
+
+
+def attn_fwd_kernel(block, q_ref, kv_ref, start_ref, out_ref, lse_ref):
+    step = pl.program_id(1)
+    steps = kv_ref.shape[1] // block
+    lanes = lane_index(block)
+
+    for at in range(steps):
+        end = (at + 1) * block
+
+        @pl.when(step == at)
+        def _(at=at, end=end):
+            k = kv_ref[0, :end, :HD]
+            v = kv_ref[0, :end, HD:]
+            q_index = at * block + lax.broadcasted_iota(jnp.int32, (block, end), 0)
+            k_index = lax.broadcasted_iota(jnp.int32, (block, end), 1)
+            allowed = (k_index <= q_index) & (k_index >= start_ref[0][:, :1])
+            outs, totals = [], []
+            for head in range(2):
+                q = q_ref[0, :, head * HD : (head + 1) * HD] * jnp.array(HD ** -0.5, bf16)
+                scores = jnp.where(allowed, dot_nt(q, k), masked)
+                largest = jnp.max(scores, axis=-1, keepdims=True)
+                weights = jnp.exp(scores - largest)
+                total = jnp.sum(weights, axis=-1, keepdims=True)
+                out = jnp.dot(weights.astype(bf16), v, preferred_element_type=f32) / total
+                outs.append(out.astype(bf16))
+                totals.append(largest + jnp.log(total))
+            out_ref[0] = jnp.concatenate(outs, axis=1)
+            lse_ref[0] = jnp.where(lanes < HD, totals[0], totals[1])
+
+
+def attn_fwd(q, kv, starts, span):
+    seqs, length, _ = q.shape
+    block = 2 * span
+    rows = lambda b, i: (b, i, 0)
+    whole = lambda b, i: (b, 0, 0)
+    return pl.pallas_call(
+        functools.partial(attn_fwd_kernel, block),
+        grid=(seqs, length // block),
+        in_specs=[
+            pl.BlockSpec((1, block, 128), rows),
+            pl.BlockSpec((1, length, 128), whole),
+            pl.BlockSpec((1, block, 128), rows),
+        ],
+        out_specs=[pl.BlockSpec((1, block, 128), rows), pl.BlockSpec((1, block, 128), rows)],
+        out_shape=[
+            jax.ShapeDtypeStruct((seqs, length, 128), bf16),
+            jax.ShapeDtypeStruct((seqs, length, 128), f32),
+        ],
+        compiler_params=pltpu.CompilerParams(vmem_limit_bytes=48 << 20),
+        cost_estimate=pl.CostEstimate(flops=seqs * length * length * 256, bytes_accessed=seqs * length * 1792, transcendentals=seqs * length * length),
+        name="attn_fwd",
+    )(q, kv, starts)
+
+
+def attn_bwd_kernel(block, q_ref, kv_ref, do_ref, o_ref, lse_ref, start_ref, *refs):
+    dq_ref, dkv_ref, dk_acc, dv_acc = refs[-4:]
+    step = pl.program_id(1)
+    steps = kv_ref.shape[1] // block
+
+    @pl.when(step == 0)
+    def _():
+        dk_acc[...] = jnp.zeros_like(dk_acc)
+        dv_acc[...] = jnp.zeros_like(dv_acc)
+
+    for at in range(steps):
+        end = (at + 1) * block
+
+        @pl.when(step == at)
+        def _(at=at, end=end):
+            k = kv_ref[0, :end, :HD]
+            v = kv_ref[0, :end, HD:]
+            k_index = lax.broadcasted_iota(jnp.int32, (end, block), 0)
+            q_index = at * block + lax.broadcasted_iota(jnp.int32, (end, block), 1)
+            allowed = (k_index <= q_index) & (k_index >= start_ref[0, 0:1, :])
+            do_rows = do_ref[...].reshape(block, 128)
+            product = do_rows.astype(f32) * o_ref[0].astype(f32)
+            dqs = []
+            for head in range(2):
+                cut = slice(head * HD, (head + 1) * HD)
+                q = q_ref[0, :, cut] * jnp.array(HD ** -0.5, bf16)
+                do = do_rows[:, cut]
+                delta = dot_nt(jnp.ones((8, HD), f32), product[:, cut], exact)[0:1, :]
+                scores = jnp.where(allowed, dot_nt(k, q), masked)
+                prob = jnp.exp(scores - lse_ref[0, head : head + 1, :])
+                dv_acc[:end, :] += jnp.dot(prob.astype(bf16), do, preferred_element_type=f32)
+                dscore = (prob * (dot_nt(v, do) - delta)).astype(bf16)
+                dk_acc[:end, :] += jnp.dot(dscore, q, preferred_element_type=f32)
+                dqs.append(dot_tn(dscore, k) * (HD ** -0.5))
+            dq_ref[0] = jnp.concatenate(dqs, axis=1)
+
+    @pl.when(step == steps - 1)
+    def _():
+        dkv_ref[0] = jnp.concatenate([dk_acc[...], dv_acc[...]], axis=1)
+
+
+def attn_bwd(q, kv, do, out, lse, starts, span, earlier):
+    seqs, length, _ = q.shape
+    block = 2 * span
+    rows = lambda b, i: (b, i, 0)
+    cols = lambda b, i: (b, 0, i)
+    whole = lambda b, i: (b, 0, 0)
+    return pl.pallas_call(
+        functools.partial(attn_bwd_kernel, block),
+        grid=(seqs, length // block),
+        in_specs=[
+            pl.BlockSpec((1, block, 128), rows),
+            pl.BlockSpec((1, length, 128), whole),
+            pl.BlockSpec((2, 1, span, 128), lambda b, i: (i, b, 0, 0)),
+            pl.BlockSpec((1, block, 128), rows),
+            pl.BlockSpec((1, 8, block), cols),
+            pl.BlockSpec((1, 8, block), cols),
+        ]
+        + [pl.BlockSpec(memory_space=pl.ANY)] * len(earlier),
+        out_specs=[pl.BlockSpec((1, block, 128), rows), pl.BlockSpec((1, length, 128), whole)],
+        out_shape=[
+            jax.ShapeDtypeStruct((seqs, length, 128), f32),
+            jax.ShapeDtypeStruct((seqs, length, 128), f32),
+        ],
+        scratch_shapes=[pltpu.VMEM((length, HD), f32), pltpu.VMEM((length, HD), f32)],
+        compiler_params=pltpu.CompilerParams(vmem_limit_bytes=56 << 20),
+        cost_estimate=pl.CostEstimate(flops=seqs * length * length * 640, bytes_accessed=seqs * length * 2560, transcendentals=seqs * length * length),
+        name="attn_bwd",
+    )(q, kv, do, out, lse, starts, *earlier)
+
+
+def any_space(count):
+    return [pl.BlockSpec(memory_space=pl.ANY)] * count
+
+
+def pack_kernel(groups, part, gate_ref, up_ref, out_ref):
+    size = gate_ref.shape[1] // (groups * part)
+    for at, ref in ((0, gate_ref), (size * part, up_ref)):
+        whole = ref[...].astype(f32)
+        for g in range(groups):
+            cuts = [whole[:, (f * groups + g) * part : (f * groups + g + 1) * part] for f in range(size)]
+            out_ref[g, :, at : at + size * part] = jnp.concatenate(cuts, axis=1).astype(bf16)
+
+
+def pack_columns(gate, up, groups, part):
+    shard, total = gate.shape
+    return pl.pallas_call(
+        functools.partial(pack_kernel, groups, part),
+        out_shape=jax.ShapeDtypeStruct((groups, shard, 2 * total // groups), bf16),
+        name="pack",
+    )(gate, up)
+
+
+def unpack_kernel(part, home_ref, gate_w_ref, up_w_ref, gate_ref, up_ref, sum_ref):
+    groups, _, shard, hidden = home_ref.shape
+    size = hidden // part
+    for which, ref in ((0, gate_ref), (1, up_ref)):
+        rows = [home_ref[g, which].astype(f32) for g in range(groups)]
+        cuts = [rows[g][:, f * part : (f + 1) * part] for f in range(size) for g in range(groups)]
+        ref[...] = jnp.concatenate(cuts, axis=1)
+    total = jnp.sum(gate_w_ref[...].astype(f32) * gate_ref[...], axis=1, keepdims=True)
+    total += jnp.sum(up_w_ref[...].astype(f32) * up_ref[...], axis=1, keepdims=True)
+    sum_ref[...] = jnp.broadcast_to(total, sum_ref.shape)
+
+
+def unpack_columns(home, gate_w, up_w, part):
+    shape = gate_w.shape
+    return pl.pallas_call(
+        functools.partial(unpack_kernel, part),
+        out_shape=[
+            jax.ShapeDtypeStruct(shape, f32),
+            jax.ShapeDtypeStruct(shape, f32),
+            jax.ShapeDtypeStruct((shape[0], 128), f32),
+        ],
+        name="unpack",
+    )(home, gate_w, up_w)
+
+
+def unpack_heads_kernel(home_ref, q_w_ref, k_w_ref, v_w_ref, q_ref, k_ref, v_ref, sum_ref):
+    blocks = [home_ref[g].astype(f32) for g in range(home_ref.shape[0])]
+    q_ref[...] = jnp.concatenate([block[:, : 2 * HD] for block in blocks], axis=1)
+    k_ref[...] = jnp.concatenate([block[:, 2 * HD : 3 * HD] for block in blocks], axis=1)
+    v_ref[...] = jnp.concatenate([block[:, 3 * HD :] for block in blocks], axis=1)
+    total = 0.0
+    for weight, grad in ((q_w_ref, q_ref), (k_w_ref, k_ref), (v_w_ref, v_ref)):
+        total += jnp.sum(weight[...].astype(f32) * grad[...], axis=1, keepdims=True)
+    sum_ref[...] = jnp.broadcast_to(total, sum_ref.shape)
+
+
+def unpack_heads(home, q_w, k_w, v_w):
+    return pl.pallas_call(
+        unpack_heads_kernel,
+        out_shape=[jax.ShapeDtypeStruct(w.shape, f32) for w in (q_w, k_w, v_w)]
+        + [jax.ShapeDtypeStruct((q_w.shape[0], 128), f32)],
+        name="unpack_heads",
+    )(home, q_w, k_w, v_w)
+
+
+def qkv_fwd_kernel(at_ref, *refs):
+    x_refs, w_refs = refs[:8], refs[8:12]
+    gain_ref, scale_ref, cos_ref, sin_ref, x_out, nm_ref, raw_ref, q_ref, kv_ref, w_ref = refs[12:]
+    step = pl.program_id(0)
+    shard = w_ref.shape[0] // 32
+
+    @pl.when(step == 0)
+    def _():
+        for m in range(4):
+            for g in range(8):
+                row = pl.multiple_of(((at_ref[1] ^ m) * 8 + g) * shard, shard)
+                w_ref[pl.ds(row, shard), :] = w_refs[m][g, :shard, :]
+
+    for j in range(8):
+
+        @pl.when(step == j)
+        def _(j=j):
+            x_out[...] = x_refs[j][...]
+
+    x = x_out[...].reshape(-1, x_out.shape[-1]).astype(f32)
+    factor = lax.rsqrt(jnp.mean(x * x, axis=-1, keepdims=True) + eps)
+    nm = (x * factor * gain_ref[...]).astype(bf16)
+    nm_ref[...] = nm.reshape(nm_ref.shape)
+    raw = jnp.dot(nm, w_ref[...], preferred_element_type=f32)
+    raw_ref[...] = raw.reshape(raw_ref.shape)
+    cos = cos_ref[...].reshape(-1, 128)
+    sin = sin_ref[...].reshape(-1, 128)
+    mean = head_mean()
+
+    def prepared(part, scale):
+        inv = lax.rsqrt(jnp.dot(part * part, mean, precision=exact, preferred_element_type=f32) + eps)
+        normed = part * inv * scale
+        return normed * cos + half_turn(normed, False) * sin
+
+    q = prepared(raw[:, :128], scale_ref[0:1, :])
+    kv = prepared(raw[:, 128:], scale_ref[1:2, :])
+    kv = jnp.where(lane_index(kv.shape[0]) < HD, kv, raw[:, 128:])
+    q_ref[...] = q.astype(bf16).reshape(q_ref.shape)
+    kv_ref[...] = kv.astype(bf16).reshape(kv_ref.shape)
+
+
+def qkv_fwd(at, x_blocks, w_blocks, gain, scales, cosine, sine, earlier):
+    seqs, span, width = x_blocks[0].shape
+    length = 8 * span
+    home = lambda j, m: (0, m[0] ^ j, 0)
+    fixed = lambda j, m: (0, 0)
+    once = dict(pipeline_mode=pl.Buffered(1))
+
+    def kernel(at_ref, *refs):
+        qkv_fwd_kernel(at_ref, *refs[:16], *refs[16 + len(earlier) :])
+
+    return pl.pallas_call(
+        kernel,
+        grid_spec=pltpu.PrefetchScalarGridSpec(
+            num_scalar_prefetch=1,
+            grid=(8,),
+            in_specs=[pl.BlockSpec((seqs, span, width), lambda j, m: (0, 0, 0), **once)] * 8
+            + [pl.BlockSpec(w_blocks[0].shape, lambda j, m: (0, 0, 0), **once)] * 4
+            + [
+                pl.BlockSpec((1, width), fixed, **once),
+                pl.BlockSpec((8, 128), fixed, **once),
+                pl.BlockSpec((seqs, span, 128), home),
+                pl.BlockSpec((seqs, span, 128), home),
+            ]
+            + any_space(len(earlier)),
+            out_specs=[
+                pl.BlockSpec((seqs, span, width), home),
+                pl.BlockSpec((seqs, span, width), home),
+                pl.BlockSpec((seqs, span, 256), home),
+                pl.BlockSpec((seqs, span, 128), home),
+                pl.BlockSpec((seqs, span, 128), home),
+                pl.BlockSpec((width, 256), fixed),
+            ],
+        ),
+        out_shape=[
+            jax.ShapeDtypeStruct((seqs, length, width), bf16),
+            jax.ShapeDtypeStruct((seqs, length, width), bf16),
+            jax.ShapeDtypeStruct((seqs, length, 256), f32),
+            jax.ShapeDtypeStruct((seqs, length, 128), bf16),
+            jax.ShapeDtypeStruct((seqs, length, 128), bf16),
+            jax.ShapeDtypeStruct((width, 256), bf16),
+        ],
+        compiler_params=pltpu.CompilerParams(vmem_limit_bytes=40 << 20),
+        cost_estimate=pl.CostEstimate(flops=16 * seqs * length * width * 256, bytes_accessed=seqs * length * width * 6, transcendentals=0),
+        name="qkv_fwd",
+    )(at, *x_blocks, *w_blocks, gain, scales, cosine, sine, *earlier)
+
+
+def halves_spec(seqs, span, width):
+    return pl.BlockSpec((1, seqs, span, width), lambda t, m: ((m[0] ^ t) >> 1, 0, 0, 0))
+
+
+def store_halves(me, step, value, even_ref, odd_ref):
+    odd = ((me ^ step) & 1) == 1
+
+    @pl.when(odd)
+    def _():
+        odd_ref[...] = value.reshape(odd_ref.shape)
+
+    @pl.when(jnp.logical_not(odd))
+    def _():
+        even_ref[...] = value.reshape(even_ref.shape)
+
+
+def ffn_kernel(hidden, padded, at_ref, *refs):
+    parts, wgu_refs, wd_refs = refs[:8], refs[8:12], refs[12:16]
+    (x_ref, cot_ref, wo_ref, gain_ref, attn_ref, mid_ref, nm_ref, hid_ref, grads_ref) = refs[16:25]
+    gnm_even, gnm_odd, out_even, out_odd, wgu, wd = refs[25:]
+    step = pl.program_id(0)
+
+    @pl.when(step == 0)
+    def _():
+        rows = wgu.shape[0] // 4
+        part = hidden // 4
+        wgu[...] = jnp.zeros_like(wgu)
+        wd[hidden:, :] = jnp.zeros((padded - hidden, wd.shape[1]), bf16)
+        for m in range(4):
+            from_f = at_ref[1] ^ m
+            block = wgu_refs[m][...].reshape(rows, 2 * hidden)
+            at = pl.ds(pl.multiple_of(from_f * rows, rows), rows)
+            wgu[at, :hidden] = block[:, :hidden]
+            wgu[at, padded : padded + hidden] = block[:, hidden:]
+            wd[pl.ds(pl.multiple_of(from_f * part, 16), part), :] = wd_refs[m][...]
+
+    tile = attn_ref.shape[0] * attn_ref.shape[1]
+    width = wo_ref.shape[0]
+    for j in range(8):
+        at = pl.multiple_of((at_ref[0] ^ j) * 128, 128)
+        attn_ref[:, :, pl.ds(at, 128)] = parts[j][...]
+    attn = attn_ref[...].reshape(tile, width)
+    mid = x_ref[...].reshape(tile, width).astype(f32) + jnp.dot(attn, wo_ref[...], preferred_element_type=f32)
+    mid_ref[...] = mid.reshape(mid_ref.shape)
+    factor = lax.rsqrt(jnp.mean(mid * mid, axis=-1, keepdims=True) + eps)
+    nm = (mid * factor * gain_ref[...]).astype(bf16)
+    nm_ref[...] = nm.reshape(nm_ref.shape)
+    both = jnp.dot(nm, wgu[...], preferred_element_type=f32)
+    gate, up = both[:, :padded], both[:, padded:]
+    sigma = jax.nn.sigmoid(gate)
+    hid = (gate * sigma * up).astype(bf16)
+    hid_ref[...] = hid.reshape(hid_ref.shape)
+    grad_hidden = dot_nt(cot_ref[...].reshape(tile, width), wd[...])
+    grad_gate = (grad_hidden * up * sigma * (1.0 + gate * (1.0 - sigma))).astype(bf16)
+    grad_up = (grad_hidden * gate * sigma).astype(bf16)
+    grads = jnp.concatenate([grad_gate, grad_up], axis=1)
+    grads_ref[...] = grads.reshape(grads_ref.shape)
+    store_halves(at_ref[0], step, dot_nt(grads, wgu[...]).astype(bf16), gnm_even, gnm_odd)
+    out = jnp.dot(hid, wd[...], preferred_element_type=f32).astype(bf16)
+    store_halves(at_ref[0], step, out, out_even, out_odd)
+
+
+def ffn(at, parts, wgu_blocks, wd_blocks, x, cot, w_out, gain):
+    seqs, length, width = x.shape
+    span = length // 8
+    hidden = 4 * wd_blocks[0].shape[0]
+    padded = -(-hidden // 128) * 128
+    home = lambda t, m: (0, t, 0)
+    fixed = lambda t, m: (0, 0)
+    once = dict(pipeline_mode=pl.Buffered(1))
+    tokens = lambda cols: pl.BlockSpec((seqs, span, cols), home)
+    shape = lambda cols, kind: jax.ShapeDtypeStruct((seqs, length, cols), kind)
+    half = jax.ShapeDtypeStruct((4, seqs, span, width), bf16)
+    return pl.pallas_call(
+        functools.partial(ffn_kernel, hidden, padded),
+        grid_spec=pltpu.PrefetchScalarGridSpec(
+            num_scalar_prefetch=1,
+            grid=(8,),
+            in_specs=[tokens(128)] * 8
+            + [pl.BlockSpec(wgu_blocks[0].shape, lambda t, m: (0, 0, 0), **once)] * 4
+            + [pl.BlockSpec(wd_blocks[0].shape, fixed, **once)] * 4
+            + [
+                tokens(width),
+                tokens(width),
+                pl.BlockSpec((width, width), fixed, **once),
+                pl.BlockSpec((1, width), fixed, **once),
+            ],
+            out_specs=[tokens(width), tokens(width), tokens(width), tokens(padded), tokens(2 * padded)]
+            + [halves_spec(seqs, span, width)] * 4,
+            scratch_shapes=[pltpu.VMEM((width, 2 * padded), bf16), pltpu.VMEM((padded, width), bf16)],
+        ),
+        out_shape=[shape(width, bf16), shape(width, f32), shape(width, bf16), shape(padded, bf16), shape(2 * padded, bf16)]
+        + [half] * 4,
+        compiler_params=pltpu.CompilerParams(vmem_limit_bytes=60 << 20),
+        cost_estimate=pl.CostEstimate(flops=seqs * length * width * (2 * width + 12 * padded), bytes_accessed=seqs * length * width * 20, transcendentals=seqs * length * padded),
+        name="ffn",
+    )(at, *parts, *wgu_blocks, *wd_blocks, x, cot, w_out, gain)
+
+
+def product_kernel(cuts, left_ref, right_ref, *refs):
+    out_ref, total = refs[-2:]
+    step = pl.program_id(0)
+    value = dot_tn(left_ref[...], right_ref[...])
+
+    @pl.when(step == 0)
+    def _():
+        total[...] = value
+
+    @pl.when(step > 0)
+    def _():
+        total[...] += value
+
+    @pl.when(step == pl.num_programs(0) - 1)
+    def _():
+        for i, (begin, end) in enumerate(cuts):
+            out_ref[i] = total[: out_ref.shape[1], begin:end].astype(bf16)
+
+
+def product(left, right, out_rows, cuts, earlier=()):
+    rows = left.shape[0]
+    tile = 512
+    at = lambda i: (i, 0)
+    return pl.pallas_call(
+        functools.partial(product_kernel, cuts),
+        grid=(rows // tile,),
+        in_specs=[pl.BlockSpec((tile, left.shape[1]), at), pl.BlockSpec((tile, right.shape[1]), at)]
+        + any_space(len(earlier)),
+        out_specs=pl.BlockSpec((len(cuts), out_rows, cuts[0][1] - cuts[0][0]), lambda i: (0, 0, 0)),
+        out_shape=jax.ShapeDtypeStruct((len(cuts), out_rows, cuts[0][1] - cuts[0][0]), bf16),
+        scratch_shapes=[pltpu.VMEM((left.shape[1], right.shape[1]), f32)],
+        compiler_params=pltpu.CompilerParams(vmem_limit_bytes=48 << 20),
+        cost_estimate=pl.CostEstimate(flops=2 * rows * left.shape[1] * right.shape[1], bytes_accessed=2 * rows * (left.shape[1] + right.shape[1]), transcendentals=0),
+        name="product",
+    )(left, right, *earlier)
+
+
+def mid_kernel(at_ref, mid_ref, cot_ref, gain_ref, wo_ref, even_ref, got_ref, sent_x, sent_y, last_x, last_y, grad_ref, half_ref, out_ref):
+    seqs, span, width = cot_ref.shape
+    grad_nm = even_ref[0].astype(f32) + got_ref[0].astype(f32)
+    more = [sent_x[0].astype(f32) + last_y[...].astype(f32), sent_y[0].astype(f32) + last_x[...].astype(f32)]
+    grad_nm = (grad_nm + jnp.concatenate(more, axis=0)).reshape(seqs * span, width)
+    mid = mid_ref[...].reshape(seqs * span, width)
+    factor = lax.rsqrt(jnp.mean(mid * mid, axis=-1, keepdims=True) + eps)
+    normed = mid * factor
+    scaled = grad_nm * gain_ref[...]
+    grad = cot_ref[...].reshape(seqs * span, width).astype(f32) + factor * (
+        scaled - normed * jnp.mean(scaled * normed, axis=-1, keepdims=True)
+    )
+    grad_ref[...] = grad
+    half = grad.astype(bf16)
+    half_ref[...] = half
+    out = dot_nt(half, wo_ref[...]).astype(bf16)
+    for g in range(8):
+        out_ref[g] = out[:, g * 128 : (g + 1) * 128].reshape(seqs, span, 128)
+
+
+def mid_bwd(at, mid, cot, gain, w_out, even, stages):
+    seqs, span, width = cot.shape
+    got, sent_x, sent_y, last_x, last_y = stages
+    half = seqs // 2
+    first = lambda *s: pl.BlockSpec((1,) + s, lambda i, m: (0,) * (len(s) + 1))
+    full = lambda *s: pl.BlockSpec(s, lambda i, m: (0,) * len(s))
+    rows = seqs * span
+    return pl.pallas_call(
+        mid_kernel,
+        grid_spec=pltpu.PrefetchScalarGridSpec(
+            num_scalar_prefetch=1,
+            grid=(1,),
+            in_specs=[
+                pl.BlockSpec((seqs, span, width), lambda i, m: (0, m[0], 0)),
+                full(seqs, span, width),
+                full(1, width),
+                full(width, width),
+                first(seqs, span, width),
+                first(seqs, span, width),
+                first(half, span, width),
+                first(half, span, width),
+                full(half, span, width),
+                full(half, span, width),
+            ],
+            out_specs=[full(rows, width), full(rows, width), full(8, seqs, span, 128)],
+        ),
+        out_shape=[
+            jax.ShapeDtypeStruct((rows, width), f32),
+            jax.ShapeDtypeStruct((rows, width), bf16),
+            jax.ShapeDtypeStruct((8, seqs, span, 128), bf16),
+        ],
+        compiler_params=pltpu.CompilerParams(vmem_limit_bytes=40 << 20),
+        cost_estimate=pl.CostEstimate(flops=2 * rows * width * width, bytes_accessed=rows * width * 20, transcendentals=0),
+        name="mid_bwd",
+    )(at, mid, cot, gain, w_out, even, got, sent_x, sent_y, last_x, last_y)
+
+
+def qkv_bwd_kernel(at_ref, dq_ref, dkv_ref, raw_ref, nm_ref, w_ref, scale_ref, cos_ref, sin_ref, *refs):
+    even_ref, odd_ref, dw_ref, dscale_ref, dw_acc = refs[-5:]
+    step = pl.program_id(0)
+    seqs, span, width = nm_ref.shape
+    tile = seqs * span
+
+    @pl.when(step == 0)
+    def _():
+        dw_acc[...] = jnp.zeros_like(dw_acc)
+        dscale_ref[...] = jnp.zeros_like(dscale_ref)
+
+    cos, sin = cos_ref[...].reshape(tile, 128), sin_ref[...].reshape(tile, 128)
+    mean = head_mean()
+
+    def average(array):
+        return jnp.dot(array, mean, precision=exact, preferred_element_type=f32)
+
+    def back(raw, grad, scale):
+        inv = lax.rsqrt(average(raw * raw) + eps)
+        normed = raw * inv
+        turned = grad * cos + half_turn(grad * sin, True)
+        grad_normed = turned * scale
+        grad_raw = inv * (grad_normed - normed * average(grad_normed * normed))
+        return grad_raw, jnp.sum(turned * normed, axis=0, keepdims=True)
+
+    raw = raw_ref[...].reshape(tile, 256)
+    grad_kv = dkv_ref[...].reshape(tile, 128)
+    dq, q_scale = back(raw[:, :128], dq_ref[...].reshape(tile, 128), scale_ref[0:1, :])
+    dkv, k_scale = back(raw[:, 128:], grad_kv, scale_ref[1:2, :])
+    dkv = jnp.where(lane_index(tile) < HD, dkv, grad_kv)
+    grad = jnp.concatenate([dq.astype(bf16), dkv.astype(bf16)], axis=1)
+    dscale_ref[0:1, :] += q_scale
+    dscale_ref[1:2, :] += k_scale
+    store_halves(at_ref[0], step, dot_nt(grad, w_ref[...]).astype(bf16), even_ref, odd_ref)
+    dw_acc[...] += dot_tn(nm_ref[...].reshape(tile, width), grad)
+
+    @pl.when(step == pl.num_programs(0) - 1)
+    def _():
+        dw_ref[...] = dw_acc[...].astype(bf16)
+
+
+def qkv_bwd(at, dq, dkv, raw, nm, w_qkv, scales, cosine, sine, earlier):
+    seqs, length, width = nm.shape
+    span = length // 8
+    tokens = lambda cols: pl.BlockSpec((seqs, span, cols), lambda t, m: (0, t, 0))
+    fixed = lambda t, m: (0, 0)
+    half = jax.ShapeDtypeStruct((4, seqs, span, width), bf16)
+    return pl.pallas_call(
+        qkv_bwd_kernel,
+        grid_spec=pltpu.PrefetchScalarGridSpec(
+            num_scalar_prefetch=1,
+            grid=(8,),
+            in_specs=[
+                tokens(128),
+                tokens(128),
+                tokens(256),
+                tokens(width),
+                pl.BlockSpec((width, 256), fixed),
+                pl.BlockSpec((8, 128), fixed),
+                tokens(128),
+                tokens(128),
+            ]
+            + any_space(len(earlier)),
+            out_specs=[halves_spec(seqs, span, width)] * 2
+            + [pl.BlockSpec((width, 256), fixed), pl.BlockSpec((8, 128), fixed)],
+            scratch_shapes=[pltpu.VMEM((width, 256), f32)],
+        ),
+        out_shape=[
+            half,
+            half,
+            jax.ShapeDtypeStruct((width, 256), bf16),
+            jax.ShapeDtypeStruct((8, 128), f32),
+        ],
+        compiler_params=pltpu.CompilerParams(vmem_limit_bytes=48 << 20),
+        cost_estimate=pl.CostEstimate(flops=16 * seqs * length * width * 256, bytes_accessed=seqs * length * width * 6, transcendentals=0),
+        name="qkv_bwd",
+    )(at, dq, dkv, raw, nm, w_qkv, scales, cosine, sine, *earlier)
+
+
+def plain_body(
     block_input,
     positions,
     cotangent,
@@ -460,6 +1043,223 @@
         value_grad,
         head_gains[:HD],
         head_gains[HD:],
+        output_grad,
+        gain_two_grad,
+        gate_grad,
+        up_grad,
+        down_grad,
+    )
+
+
+def after(array, earlier):
+    first = earlier.reshape(-1)[0] if earlier.ndim == 1 else earlier[(0,) * earlier.ndim]
+    return array + jnp.minimum(jnp.abs(first), 0).astype(array.dtype)
+
+
+def swap_line(array, mask):
+    size = lax.axis_size("fsdp")
+    return lax.ppermute(array, "fsdp", [(i, i ^ mask) for i in range(size)])
+
+
+def line_blocks(block):
+    return [block] + [swap_line(block, m) for m in (1, 2, 3)]
+
+
+def line_parts(block_of):
+    me = lax.axis_index("fsdp")
+    return [swap_line(block_of(me ^ m), m) for m in (1, 2, 3)]
+
+
+def add_up(own, others):
+    total = own.astype(f32)
+    for other in others:
+        total = total + other.astype(f32)
+    return total
+
+
+def reduce_stages(even, odd):
+    half = even.shape[1] // 2
+    got = swap(odd, 1)
+
+    def held(i, low):
+        cut = slice(0, half) if low else slice(half, None)
+        return even[i, cut].astype(f32) + got[i, cut].astype(f32)
+
+    sent_x = swap(jnp.stack([held(1, True), held(3, True)]).astype(bf16), 2)
+    sent_y = swap(jnp.stack([held(2, False), held(3, False)]).astype(bf16), 4)
+    last_y = swap((held(2, True) + sent_x[1].astype(f32)).astype(bf16), 4)
+    last_x = swap((held(1, False) + sent_y[1].astype(f32)).astype(bf16), 2)
+    return got, sent_x, sent_y, last_x, last_y
+
+
+def own_sum(even, stages):
+    got, sent_x, sent_y, last_x, last_y = stages
+    low = sent_x[0].astype(f32) + last_y.astype(f32)
+    high = sent_y[0].astype(f32) + last_x.astype(f32)
+    return even[0].astype(f32) + got[0].astype(f32) + jnp.concatenate([low, high], axis=0)
+
+
+def body(
+    block_input,
+    positions,
+    cotangent,
+    attention_gain,
+    query_weight,
+    key_weight,
+    value_weight,
+    query_gain,
+    key_gain,
+    output_weight,
+    feedforward_gain,
+    gate_weight,
+    up_weight,
+    down_weight,
+):
+    seqs, span, width = block_input.shape
+    groups = lax.axis_size("seq")
+    size = lax.axis_size("fsdp")
+    if not (groups == 8 and size == 4 and seqs % 2 == 0 and span % 64 == 0):
+        return plain_body(
+            block_input,
+            positions,
+            cotangent,
+            attention_gain,
+            query_weight,
+            key_weight,
+            value_weight,
+            query_gain,
+            key_gain,
+            output_weight,
+            feedforward_gain,
+            gate_weight,
+            up_weight,
+            down_weight,
+        )
+    me = lax.axis_index("seq")
+    me_line = lax.axis_index("fsdp")
+    at = jnp.stack([me, me_line]).astype(jnp.int32)
+    length = span * groups
+    rows = seqs * length
+    own_rows = seqs * span
+    shard = query_weight.shape[0]
+    part = gate_weight.shape[1] // (groups * size)
+    hidden_cols = part * size
+    padded = -(-hidden_cols // 128) * 128
+
+    x_blocks = partner_blocks(block_input)
+    packed = jnp.concatenate(
+        [
+            query_weight.reshape(shard, groups, 2 * HD),
+            key_weight.reshape(shard, groups, HD),
+            value_weight.reshape(shard, groups, HD),
+        ],
+        axis=2,
+    ).transpose(1, 0, 2)
+    gains = jnp.concatenate([attention_gain, feedforward_gain])
+    gain_rows = jnp.zeros((16, 4 * HD), bf16).at[0, : 2 * shard].set(gains)
+    packed = jnp.concatenate(
+        [packed, jnp.broadcast_to(gain_rows[None], (groups, 16, 4 * HD))], axis=1
+    )
+    qkv_blocks = line_blocks(spread(packed))
+    gains = jnp.stack([block[:, shard, : 2 * shard] for block in qkv_blocks])
+    gains = jnp.take(gains, me_line ^ jnp.arange(size), axis=0).astype(f32)
+    gain_one = gains[:, :, :shard].reshape(1, width)
+    gain_two = gains[:, :, shard:].reshape(1, width)
+
+    down_blocks = line_blocks(down_weight)
+    gate_up = spread(after(pack_columns(gate_weight, up_weight, groups, part), x_blocks[6]))
+    gate_up_blocks = line_blocks(gate_up)
+    w_out = lax.all_gather(output_weight, ("fsdp", "seq"), axis=0, tiled=True)
+    cot_full = lax.all_gather(cotangent, "seq", axis=1, tiled=True)
+
+    inverse = rope_base ** (-(jnp.arange(HD // 2, dtype=f32) * 2.0) / HD)
+    angles = positions.astype(f32)[:, :, None] * jnp.tile(inverse, 4)[None, None, :]
+    cosine, sine = jnp.cos(angles), jnp.sin(angles)
+    scales = jnp.concatenate(
+        [jnp.tile(query_gain, 2)[None], jnp.tile(key_gain, 2)[None], jnp.zeros((6, 128), bf16)]
+    ).astype(f32)
+    starts = jnp.arange(length, dtype=jnp.int32)[None, :] - positions
+    x_full, normed_in, qkv_raw, q_rows, kv_rows, w_qkv = qkv_fwd(
+        at, x_blocks, qkv_blocks, gain_one, scales, cosine, sine, [gate_up]
+    )
+    starts_wide = jnp.broadcast_to(starts[:, :, None], (seqs, length, 128))
+    outputs, totals = attn_fwd(q_rows, kv_rows, starts_wide, span)
+
+    attn_rows, residual_mid, normed_mid, hidden, ff_grads, gnm_even, gnm_odd, out_even, out_odd = ffn(
+        at, partner_blocks(outputs), gate_up_blocks, down_blocks, x_full, cot_full, w_out, gain_two
+    )
+    flat = lambda array: array.reshape(rows, -1)
+
+    mid_stages = reduce_stages(gnm_even, gnm_odd)
+    down_term = product(flat(hidden), flat(cot_full), hidden_cols, ((0, width),), [mid_stages[0]])[0]
+    cuts = ((0, hidden_cols), (padded, padded + hidden_cols))
+    gate_up_term = product(flat(normed_mid), flat(ff_grads), width, cuts, [down_term])
+    grad_mid, grad_mid_half, grad_attn_out = mid_bwd(
+        at, residual_mid, cotangent, gain_two, w_out, gnm_even, mid_stages
+    )
+    grad_heads = spread(grad_attn_out)
+
+    def block_rows(term, f, count):
+        return lax.dynamic_slice_in_dim(term, f * count, count, term.ndim - 2)
+
+    down_parts = line_parts(lambda f: block_rows(down_term, f, part))
+    gate_up_parts = line_parts(lambda f: block_rows(gate_up_term, f, groups * shard))
+    out_stages = reduce_stages(out_even, after(out_odd, grad_mid_half))
+
+    totals_row = jnp.stack([totals[:, :, 0], totals[:, :, HD]], axis=1)
+    totals_row = jnp.concatenate([totals_row, jnp.zeros((seqs, 6, length), f32)], axis=1)
+    starts_row = jnp.broadcast_to(starts[:, None, :], (seqs, 8, length))
+    grad_q, grad_kv = attn_bwd(
+        q_rows, kv_rows, grad_heads, outputs, totals_row, starts_row, span, [gate_up_term, out_stages[0]]
+    )
+    gin_even, gin_odd, qkv_term, head_gains = qkv_bwd(
+        at, grad_q, grad_kv, qkv_raw, normed_in, w_qkv, scales, cosine, sine,
+        [out_stages[1], out_stages[2]] + down_parts + gate_up_parts,
+    )
+    in_stages = reduce_stages(gin_even, gin_odd)
+    own_in = block_input.reshape(own_rows, width).astype(f32)
+    grad_normed_in = own_sum(gin_even, in_stages).reshape(own_rows, width)
+    input_grad = (
+        (grad_mid + norm_bwd(own_in, inv_rms(own_in), gain_one, grad_normed_in))
+        .astype(bf16)
+        .reshape(seqs, span, width)
+    )
+
+    residual_own = lax.dynamic_slice_in_dim(residual_mid, me * span, span, 1)
+    block_output = (residual_own + own_sum(out_even, out_stages)).astype(bf16)
+
+    down_grad = add_up(block_rows(down_term, me_line, part), down_parts)
+    gate_up_sum = add_up(block_rows(gate_up_term, me_line, groups * shard), gate_up_parts)
+    gate_up_sum = gate_up_sum.astype(bf16).reshape(2, groups, shard, hidden_cols).transpose(1, 0, 2, 3)
+    gate_grad, up_grad, gain_two_sum = unpack_columns(spread(gate_up_sum), gate_weight, up_weight, part)
+
+    attn_own = lax.dynamic_slice_in_dim(attn_rows, me * span, span, 1).reshape(own_rows, width)
+    output_term = matmul_tn(attn_own, grad_mid_half).astype(bf16)
+    output_term = reduce_seq(output_term.reshape(size, groups * shard, width), 1).astype(bf16)
+    output_grad = add_up(
+        lax.dynamic_index_in_dim(output_term, me_line, 0, keepdims=False),
+        line_parts(lambda f: lax.dynamic_index_in_dim(output_term, f, 0, keepdims=False)),
+    )
+
+    qkv_parts = line_parts(lambda f: block_rows(qkv_term, f, groups * shard))
+    qkv_sum = add_up(block_rows(qkv_term, me_line, groups * shard), qkv_parts).astype(bf16)
+    query_grad, key_grad, value_grad, gain_one_sum = unpack_heads(
+        spread(qkv_sum.reshape(groups, shard, 4 * HD)), query_weight, key_weight, value_weight
+    )
+
+    gain_one_grad = gain_one_sum[:, 0] / attention_gain.astype(f32)
+    gain_two_grad = gain_two_sum[:, 0] / feedforward_gain.astype(f32)
+
+    head_gains = sum_everywhere(head_gains)
+    return (
+        block_output,
+        input_grad,
+        gain_one_grad,
+        query_grad,
+        key_grad,
+        value_grad,
+        head_gains[0, :HD] + head_gains[0, HD:],
+        head_gains[1, :HD],
         output_grad,
         gain_two_grad,
         gate_grad,

time: 792 us -> 630 us (0.80)
  Pallas kernels: 0 us -> 167 us
  matrix products: 152 us -> 1.29 us
  local copies, waits for them, and re-layouts: 134 us -> 51.2 us
  other arithmetic: 134 us -> 57.1 us
  starting transfers between devices: 160 us -> 99.1 us
  waiting for transfers between devices: 182 us -> 232 us
    pallas_call x0 -> x11, Pallas kernels: none -> 167 us  [the longest x1 51.9 us: ffn(): pl.pallas_call(functools.partial(ffn_kernel, hidden, padded), grid_spec=p...]
    dot_general x28 -> x0, matrix products: 129 us -> none  [the longest x18 52.7 us: contract(): return jnp.einsum(formula, left, right, preferred_element_type=f32)]
    ppermute x36 -> x21, waiting for transfers between devices: 40 us -> 131 us  [swap_line(): return lax.ppermute(array, 'fsdp', [(i, i ^ mask) for i in range(size)])]
    reduce_scatter x1 -> x0, waiting for transfers between devices: 90 us -> none  [body(): lax.psum_scatter(output_term, ('fsdp', 'seq'), scatter_dimension=0, tiled...]
    ppermute x36 -> x21, starting transfers between devices: 107 us -> 44.9 us  [swap_line(): return lax.ppermute(array, 'fsdp', [(i, i ^ mask) for i in range(size)])]
    ppermute x42 -> x39, waiting for transfers between devices: 41 us -> 73.2 us  [swap(): return lax.ppermute(array, 'seq', [(i, i ^ mask) for i in range(groups)])]
    dynamic_update_slice x27 -> x0, local copies, waits for them, and re-layouts: 30.1 us -> none  [the longest x24 29.3 us: gather_seq(): whole = lax.dynamic_update_slice_in_dim(whole, part, (me ^ j) * width, axis)]
    convert_element_type x22 -> x8, other arithmetic: 31.8 us -> 10.3 us  [the longest x3 4.77 us: reduce_stages(): last_y = swap((held(2, True) + sent_x[1].astype(f32)).astype(bf16), 4)]
  transfers between devices with their start and end apart: 87 -> 69, of which waited for: 24 -> 28; matrix products, arithmetic and copies ran while one was open for 41% -> 13% of each run, Pallas kernels for 0% -> 18%
where the time goes in v2:
time: 630 us; the launch traced here: 625 us
  waiting for transfers between devices  232 us (37%)
  Pallas kernels  167 us (27%)
  starting transfers between devices  99.1 us (16%)
  other arithmetic  57.1 us (9%)
  local copies, waits for them, and re-layouts  51.2 us (8%)
  between operations  16.8 us (3%)
    ppermute x21, waiting for transfers between devices, swap_line(): return lax.ppermute(array, 'fsdp', [(i, i ^ mask) for i in range(size)])  131 us
    ppermute x39, waiting for transfers between devices, swap(): return lax.ppermute(array, 'seq', [(i, i ^ mask) for i in range(groups)])  73.2 us
    pallas_call x1, Pallas kernels, ffn(): pl.pallas_call(functools.partial(ffn_kernel, hidden, padded), grid_spec=p...  51.9 us
    ppermute x21, starting transfers between devices, swap_line(): return lax.ppermute(array, 'fsdp', [(i, i ^ mask) for i in range(size)])  44.9 us
    ppermute x39, starting transfers between devices, swap(): return lax.ppermute(array, 'seq', [(i, i ^ mask) for i in range(groups)])  32 us
    pallas_call x1, Pallas kernels, attn_bwd(): pl.pallas_call(functools.partial(attn_bwd_kernel, block), grid=(seqs, len...  27 us
    pallas_call x2, Pallas kernels, product(): pl.pallas_call(functools.partial(product_kernel, cuts), grid=(rows // til...  23.6 us
    all_to_all x5, waiting for transfers between devices, spread(): lax.all_to_all(blocks, 'seq', split_axis=0, concat_axis=0, tiled=True)  21.2 us
  transfers between devices with their start and end apart: 69, of which 28 were waited for; matrix products, arithmetic and copies ran while one was open for 13% of the time, Pallas kernels for 18%

profile of v2, /device:TPU:0, one launch (start us, length us, event | category | flops | bytes accessed | tf_op | source)
XLA Modules:
  0.0 624.6 jit_solution(3961836024795030777)
XLA Ops:
  8.7 3.0 collective-permute-start.3
  17.4 3.4 all-to-all-start
  21.0 6.9 %multiply_sine_fusion = (f32[2,1536,128]{2,1,0:T(8,128)S(1)}, f32[2,1536,128]{2,1,0:T(8,128)}) fusion(f32[128]{0:T(128)S(1)} %mul.134, f32[2,1536]{1,0:T(2,128)S(1)} %get-tuple-element.142), kind=kLoop, calls=%fused_computation.1 | loop fusion | flops 393216 | bytes 3158528 | tf_op jit(solution)/shard_map/sin | solution.py:1177
  27.8 2.7 collective-permute-done.3.refs_4_
  37.9 2.7 pack.1
  40.7 3.6 collective-permute-start.10
  45.2 6.3 %collective-permute-done.10.refs_11_ = bf16[8,48,256]{2,1,0:T(8,128)(2,1)S(1)} collective-permute-done((bf16[8,48,256]{2,1,0:T(8,128)(2,1)S(1)}, bf16[8,48,256]{2,1,0:T(8,128)(2,1)S(1)}, u32[]{:S(2)}, u32[]{:S(2)}) %collective-permute-start.10) | collective-permute-done | bytes 196640 | tf_op jit(solution)/shard_map/ppermute | solution.py:1061
  51.5 9.8 %collective-permute-done.9.refs_10_ = bf16[8,48,256]{2,1,0:T(8,128)(2,1)S(1)} collective-permute-done((bf16[8,48,256]{2,1,0:T(8,128)(2,1)S(1)}, bf16[8,48,256]{2,1,0:T(8,128)(2,1)S(1)}, u32[]{:S(2)}, u32[]{:S(2)}) %collective-permute-start.9) | collective-permute-done | bytes 196640 | tf_op jit(solution)/shard_map/ppermute | solution.py:1061
  68.3 3.8 all-to-all-start.1
  73.0 9.5 %all-to-all-done.1.refs_16_.refs_8_ = bf16[8,32,1152]{2,1,0:T(8,128)(2,1)S(1)} async-done(((bf16[8,32,1152]{2,1,0:T(8,128)(2,1)}), bf16[8,32,1152]{2,1,0:T(8,128)(2,1)S(1)}, u32[]{:S(2)}, u32[]{:S(2)}) %all-to-all-start.1) | async-done | bytes 589856 | tf_op jit(solution)/shard_map/all_to_all | solution.py:231
  86.2 17.6 %qkv_fwd.1 = (bf16[2,1536,1024]{2,1,0:T(8,128)(2,1)}, bf16[2,1536,1024]{2,1,0:T(8,128)(2,1)}, f32[2,1536,256]{2,1,0:T(8,128)}, bf16[2,1536,128]{2,1,0:T(8,128)(2...) custom-call(s32[2]{0:T(128)S(1)} %pad_add_fusion.at_ref, bf16[2,192,1024]{2,1,0:T(8,128)(2,1)S(1)} %copy-done.3, ...), custom_call_target="tpu_custom_call" | custom-call | flops 12884901888 | bytes 18874368 | tf_op jit(solution)/shard_map/qkv_fwd/pallas_call | solution.py:515
  105.0 15.4 %attn_fwd.1 = (bf16[2,1536,128]{2,1,0:T(8,128)(2,1)S(1)}, f32[2,1536,128]{2,1,0:T(8,128)S(1)}) custom-call(bf16[2,1536,128]{2,1,0:T(8,128)(2,1)S(1)} %get-tuple-element.58.q_ref, bf16[2,1536,128]{2,1,0:T(8,128)(2,1)S(1)} %get-tuple-element.59.kv_ref, s32[2,1536,128]{2,1,0:T(8,128)S(1)} %broadcast_in_dim.46.start_ref), custom_call_target="tpu_custom_call" | custom-call | flops 1207959552 | bytes 5505024 | tf_op jit(solution)/shard_map/attn_fwd/pallas_call | solution.py:307
  121.9 16.1 %collective-permute-done.14.refs_4_ = bf16[2,1536,128]{2,1,0:T(8,128)(2,1)} collective-permute-done((bf16[2,1536,128]{2,1,0:T(8,128)(2,1)S(1)}, bf16[2,1536,128]{2,1,0:T(8,128)(2,1)}, u32[]{:S(2)}, u32[]{:S(2)}) %collective-permute-start.14) | collective-permute-done | bytes 786464 | tf_op jit(solution)/shard_map/ppermute | solution.py:129
  139.0 2.9 collective-permute-start.16
  156.1 47.3 %collective-permute-done.23.refs_14_ = bf16[144,1024]{1,0:T(8,128)(2,1)S(1)} collective-permute-done((bf16[144,1024]{1,0:T(8,128)(2,1)S(1)}, bf16[144,1024]{1,0:T(8,128)(2,1)S(1)}, u32[]{:S(2)}, u32[]{:S(2)}) %collective-permute-start.23) | collective-permute-done | bytes 294944 | tf_op jit(solution)/shard_map/ppermute | solution.py:1061
  204.5 16.3 %collective-permute-done.20.refs_10_ = bf16[8,32,1152]{2,1,0:T(8,128)(2,1)S(1)} collective-permute-done((bf16[8,32,1152]{2,1,0:T(8,128)(2,1)S(1)}, bf16[8,32,1152]{2,1,0:T(8,128)(2,1)S(1)}, u32[]{:S(2)}, u32[]{:S(2)}) %collective-permute-start.20) | collective-permute-done | bytes 589856 | tf_op jit(solution)/shard_map/ppermute | solution.py:1061
  222.3 12.3 %collective-permute-done.19.refs_9_ = bf16[8,32,1152]{2,1,0:T(8,128)(2,1)} collective-permute-done((bf16[8,32,1152]{2,1,0:T(8,128)(2,1)S(1)}, bf16[8,32,1152]{2,1,0:T(8,128)(2,1)}, u32[]{:S(2)}, u32[]{:S(2)}) %collective-permute-start.19) | collective-permute-done | bytes 589856 | tf_op jit(solution)/shard_map/ppermute | solution.py:1061
  235.8 51.9 %ffn.1 = (bf16[2,1536,1024]{2,1,0:T(8,128)(2,1)}, f32[2,1536,1024]{2,1,0:T(8,128)}, bf16[2,1536,1024]{2,1,0:T(8,128)(2,1)}, bf16[2,1536,640]{2,1,0:T(8,128)(2,1)...) custom-call(s32[2]{0:T(128)} %copy-done.23, ...), custom_call_target="tpu_custom_call" | custom-call | flops 30601641984 | bytes 62914560 | tf_op jit(solution)/shard_map/ffn/pallas_call | solution.py:625
  287.7 5.9 collective-permute-done.25.got_ref.refs_0_
  293.6 3.0 add_convert_fusion.16
  298.5 17.8 %collective-permute-done.26.sent_x = bf16[2,1,192,1024]{3,2,1,0:T(8,128)(2,1)S(1)} collective-permute-done((bf16[2,1,192,1024]{3,2,1,0:T(8,128)(2,1)S(1)}, bf16[2,1,192,1024]{3,2,1,0:T(8,128)(2,1)S(1)}, u32[]{:S(2)}, u32[]{:S(2)}) %collective-permute-start.26) | collective-permute-done | bytes 786464 | tf_op jit(solution)/shard_map/ppermute | solution.py:129
  323.4 3.1 copy.78
  332.3 4.4 mid_bwd.1
  341.0 9.0 %product.2 = bf16[1,576,1024]{2,1,0:T(8,128)(2,1)S(1)} custom-call(bf16[3072,640]{1,0:T(8,128)(2,1)} %bitcast.201, bf16[3072,1024]{1,0:T(8,128)(2,1)} %bitcast.198, bf16[4,2,192,1024]{3,2,1,0:T(8,128)(2,1)S(1)} %copy-done.2), custom_call_target="tpu_custom_call" | custom-call | flops 4026531840 | bytes 10223616 | tf_op jit(solution)/shard_map/product/pallas_call | solution.py:674
  350.0 14.7 %product.3.refs_0_ = bf16[2,1024,576]{2,1,0:T(8,128)(2,1)S(1)} custom-call(bf16[3072,1024]{1,0:T(8,128)(2,1)} %bitcast.200, bf16[3072,1280]{1,0:T(8,128)(2,1)} %bitcast.199, bf16[576,1024]{1,0:T(8,128)(2,1)S(1)} %bitcast.188), custom_call_target="tpu_custom_call" | custom-call | flops 8053063680 | bytes 14155776 | tf_op jit(solution)/shard_map/product/pallas_call | solution.py:674
  371.3 3.0 collective-permute-start.39
  378.1 21.3 %collective-permute-done.38 = bf16[2,256,576]{1,2,0:T(8,128)(2,1)S(1)} collective-permute-done((bf16[2,256,576]{1,2,0:T(8,128)(2,1)}, bf16[2,256,576]{1,2,0:T(8,128)(2,1)S(1)}, u32[]{:S(2)}, u32[]{:S(2)}) %collective-permute-start.38) | collective-permute-done | bytes 589856 | tf_op jit(solution)/shard_map/ppermute | solution.py:1061
  403.1 17.2 %collective-permute-done.39 = bf16[2,256,576]{1,2,0:T(8,128)(2,1)S(1)} collective-permute-done((bf16[2,256,576]{1,2,0:T(8,128)(2,1)}, bf16[2,256,576]{1,2,0:T(8,128)(2,1)S(1)}, u32[]{:S(2)}, u32[]{:S(2)}) %collective-permute-start.39) | collective-permute-done | bytes 589856 | tf_op jit(solution)/shard_map/ppermute | solution.py:1061
  422.4 17.4 %collective-permute-start.35 = (bf16[144,1024]{1,0:T(8,128)(2,1)}, bf16[144,1024]{1,0:T(8,128)(2,1)}, u32[]{:S(2)}, u32[]{:S(2)}) collective-permute-start(bf16[144,1024]{1,0:T(8,128)(2,1)} %get-tuple-element.126), channel_id=1, source_target_pairs={{0,8},{8,0},{16,24},{24,16},{1,9},{9,1},{17,25},{25,17},{2,10},{10... | collective-permute-start | bytes 884744 | tf_op jit(solution)/shard_map/ppermute | solution.py:1061
  441.2 4.2 all-to-all-start.2
  445.5 3.0 convert_add_fusion.8
  459.3 27.0 %attn_bwd.1 = (f32[2,1536,128]{2,1,0:T(8,128)}, f32[2,1536,128]{2,1,0:T(8,128)}) custom-call(bf16[2,1536,128]{2,1,0:T(8,128)(2,1)} %copy-done.30, bf16[2,1536,128]{2,1,0:T(8,128)(2,1)} %copy-done.31, bf16[8,2,192,128]{3,2,1,0:T(8,128)(2,1)} %all-to-all-done.2.do_ref, bf16[2,1536,128]{2,1,0:T(8,128)(2,1)} %copy-done.29, ...), custom_call_target="tpu_custom_call" | custom-call | flops 3019898880 | bytes 7864320 | tf_op jit(solution)/shard_map/attn_bwd/pallas_call | solution.py:373
  486.6 20.5 %qkv_bwd.1 = (bf16[4,2,192,1024]{3,2,1,0:T(8,128)(2,1)}, bf16[4,2,192,1024]{3,2,1,0:T(8,128)(2,1)}, bf16[1024,256]{1,0:T(8,128)(2,1)S(1)}, f32[8,128]{1,0:T(8,128)S(1)}) custom-call(s32[2]{0:T(128)S(1)} %copy-done.24, f32[2,1536,128]{2,1,0:T(8,128)} %get-tuple-element.74.dq_ref, f32[2,1536,128]{2,1,0:T(8,128)} %get-tuple-element.75.dkv_ref, ...), custom_call_target="tpu_custom_call" | custom-call | flops 12884901888 | bytes 18874368 | tf_op jit(solution)/shard_map/qkv_bwd/pallas_call | solution.py:792
  511.8 4.2 all-to-all-start.4
  523.6 4.0 all-to-all-done.4.home_ref
  533.1 3.2 collective-permute-start.60
  538.1 3.0 collective-permute-done.50
  546.8 2.7 collective-permute-start.48
  549.5 2.9 collective-permute-start.53
  554.4 4.6 collective-permute-done.53
  560.9 3.6 all-to-all-start.3
  565.1 6.3 %all-to-all-done.3.home_ref = bf16[8,32,256]{2,1,0:T(8,128)(2,1)S(1)} async-done(((bf16[8,32,256]{2,1,0:T(8,128)(2,1)}), bf16[8,32,256]{2,1,0:T(8,128)(2,1)S(1)}, u32[]{:S(2)}, u32[]{:S(2)}) %all-to-all-start.3) | async-done | bytes 131104 | tf_op jit(solution)/shard_map/all_to_all | solution.py:231
  580.7 14.6 %collective-permute-done.44 = bf16[2,1,192,1024]{3,2,1,0:T(8,128)(2,1)S(1)} collective-permute-done((bf16[2,1,192,1024]{3,2,1,0:T(8,128)(2,1)S(1)}, bf16[2,1,192,1024]{3,2,1,0:T(8,128)(2,1)S(1)}, u32[]{:S(2)}, u32[]{:S(2)}) %collective-permute-start.44) | collective-permute-done | bytes 786464 | tf_op jit(solution)/shard_map/ppermute | solution.py:129
  598.8 3.2 fusion.1
  602.2 2.5 convert_add_fusion
  606.7 4.3 collective-permute-done.45
  611.1 3.0 fusion.4
  614.2 3.3 fusion.9
  (362 shorter events, 139.5 us)
Async XLA Ops:
  7.2 227.5 %all-gather.5.cloned.1.call-start = ((), (), s32[]{:S(2)}) async-start(), calls=%async_computation.6 | async-start | bytes 2162688 | tf_op jit(solution)/shard_map/all_gather | solution.py:1172
  7.9 226.8 %all-gather.3.cloned.1.call-start = ((), (), s32[]{:S(2)}) async-start(), calls=%async_computation.5 | async-start | bytes 7077888 | tf_op jit(solution)/shard_map/all_gather | solution.py:1173
  8.7 21.9 %collective-permute-start.3 = (bf16[2,192,1024]{2,1,0:T(8,128)(2,1)}, bf16[2,192,1024]{2,1,0:T(8,128)(2,1)}, u32[]{:S(2)}, u32[]{:S(2)}) collective-permute-start(bf16[2,192,1024]{2,1,0:T(8,128)(2,1)} %refs_0_.1), channel_id=1, source_target_pairs={{0,4},{1,5},{2,6},{3,7},{4,0},{5,1},{6,2},{7,3},{8,12},{9,13},{10,... | collective-permute-start | bytes 2359304 | tf_op jit(solution)/shard_map/ppermute | solution.py:129
  11.7 22.6 %collective-permute-start.1 = (bf16[2,192,1024]{2,1,0:T(8,128)(2,1)}, bf16[2,192,1024]{2,1,0:T(8,128)(2,1)}, u32[]{:S(2)}, u32[]{:S(2)}) collective-permute-start(bf16[2,192,1024]{2,1,0:T(8,128)(2,1)} %refs_0_.1), channel_id=1, source_target_pairs={{0,2},{1,3},{2,0},{3,1},{4,6},{5,7},{6,4},{7,5},{8,10},{9,11},{10,... | collective-permute-start | bytes 2359304 | tf_op jit(solution)/shard_map/ppermute | solution.py:129
  17.4 23.3 %all-to-all-start = ((bf16[8,48,256]{2,1,0:T(8,128)(2,1)}), bf16[8,48,256]{2,1,0:T(8,128)(2,1)S(1)}, u32[]{:S(2)}, u32[]{:S(2)}) async-start(bf16[8,48,256]{2,1,0:T(8,128)(2,1)} %pad_maximum_fusion.10), calls=%async_computation | async-start | bytes 393216 | tf_op jit(solution)/shard_map/all_to_all | solution.py:231
  32.3 29.6 %collective-permute-start.5 = (bf16[1,192,1024]{2,1,0:T(8,128)(2,1)}, bf16[1,192,1024]{2,1,0:T(8,128)(2,1)}, u32[]{:S(2)}, u32[]{:S(2)}) collective-permute-start(bf16[1,192,1024]{2,1,0:T(8,128)(2,1)} %slice.362), channel_id=1, source_target_pairs={{0,2},{1,3},{2,0},{3,1},{4,6},{5,7},{6,4},{7,5},{8,10},{9,11},{10,... | collective-permute-start | bytes 1179656 | tf_op jit(solution)/shard_map/ppermute | solution.py:129
  36.1 29.5 %collective-permute-start.6 = (bf16[1,192,1024]{2,1,0:T(8,128)(2,1)}, bf16[1,192,1024]{2,1,0:T(8,128)(2,1)}, u32[]{:S(2)}, u32[]{:S(2)}) collective-permute-start(bf16[1,192,1024]{2,1,0:T(8,128)(2,1)} %slice.363), channel_id=1, source_target_pairs={{0,4},{1,5},{2,6},{3,7},{4,0},{5,1},{6,2},{7,3},{8,12},{9,13},{10,... | collective-permute-start | bytes 1179656 | tf_op jit(solution)/shard_map/ppermute | solution.py:129
  44.3 17.0 %collective-permute-start.9 = (bf16[8,48,256]{2,1,0:T(8,128)(2,1)S(1)}, bf16[8,48,256]{2,1,0:T(8,128)(2,1)S(1)}, u32[]{:S(2)}, u32[]{:S(2)}) collective-permute-start(bf16[8,48,256]{2,1,0:T(8,128)(2,1)S(1)} %all-to-all-done.refs_8_), channel_id=1, source_target_pairs={{0,16},{8,24},{16,0},{24,8},{1,17},{9,25},{17,1},{25,9},{2,18},{10... | collective-permute-start | bytes 589832 | tf_op jit(solution)/shard_map/ppermute | solution.py:1061
  44.3 17.0 %collective-permute-start.8 = (bf16[8,48,256]{2,1,0:T(8,128)(2,1)S(1)}, bf16[8,48,256]{2,1,0:T(8,128)(2,1)S(1)}, u32[]{:S(2)}, u32[]{:S(2)}) collective-permute-start(bf16[8,48,256]{2,1,0:T(8,128)(2,1)S(1)} %all-to-all-done.refs_8_), channel_id=1, source_target_pairs={{0,8},{8,0},{16,24},{24,16},{1,9},{9,1},{17,25},{25,17},{2,10},{10... | collective-permute-start | bytes 589832 | tf_op jit(solution)/shard_map/ppermute | solution.py:1061
  51.5 21.5 %collective-permute-start = (bf16[2,192,1024]{2,1,0:T(8,128)(2,1)S(1)}, bf16[2,192,1024]{2,1,0:T(8,128)(2,1)}, u32[]{:S(2)}, u32[]{:S(2)}) collective-permute-start(bf16[2,192,1024]{2,1,0:T(8,128)(2,1)S(1)} %copy-done.3), channel_id=1, source_target_pairs={{0,1},{1,0},{2,3},{3,2},{4,5},{5,4},{6,7},{7,6},{8,9},{9,8},{10,11... | collective-permute-start | bytes 2359304 | tf_op jit(solution)/shard_map/ppermute | solution.py:129
  67.3 15.2 %collective-permute-start.7 = (bf16[2,192,1024]{2,1,0:T(8,128)(2,1)}, bf16[2,192,1024]{2,1,0:T(8,128)(2,1)}, u32[]{:S(2)}, u32[]{:S(2)}) collective-permute-start(bf16[2,192,1024]{2,1,0:T(8,128)(2,1)} %constant_dynamic-update-slice_fusion.refs_6_), channel_id=1, source_target_pairs={{0,1},{1,0},{2,3},{3,2},{4,5},{5,4},{6,7},{7,6},{8,9},{9,8},{10,11... | collective-permute-start | bytes 2359304 | tf_op jit(solution)/shard_map/ppermute | solution.py:129
  68.3 14.2 %all-to-all-start.1 = ((bf16[8,32,1152]{2,1,0:T(8,128)(2,1)}), bf16[8,32,1152]{2,1,0:T(8,128)(2,1)S(1)}, u32[]{:S(2)}, u32[]{:S(2)}) async-start(bf16[8,32,1152]{2,1,0:T(8,128)(2,1)} %broadcast_add_fusion.1), calls=%async_computation.1 | async-start | bytes 1179648 | tf_op jit(solution)/shard_map/all_to_all | solution.py:231
  120.5 17.5 %collective-permute-start.14 = (bf16[2,1536,128]{2,1,0:T(8,128)(2,1)S(1)}, bf16[2,1536,128]{2,1,0:T(8,128)(2,1)}, u32[]{:S(2)}, u32[]{:S(2)}) collective-permute-start(bf16[2,1536,128]{2,1,0:T(8,128)(2,1)S(1)} %get-tuple-element.60.refs_0_.o_ref), channel_id=1, source_target_pairs={{0,4},{1,5},{2,6},{3,7},{4,0},{5,1},{6,2},{7,3},{8,12},{9,13},{10,... | collective-permute-start | bytes 2359304 | tf_op jit(solution)/shard_map/ppermute | solution.py:129
  121.2 20.7 %collective-permute-start.12 = (bf16[2,1536,128]{2,1,0:T(8,128)(2,1)S(1)}, bf16[2,1536,128]{2,1,0:T(8,128)(2,1)}, u32[]{:S(2)}, u32[]{:S(2)}) collective-permute-start(bf16[2,1536,128]{2,1,0:T(8,128)(2,1)S(1)} %get-tuple-element.60.refs_0_.o_ref), channel_id=1, source_target_pairs={{0,2},{1,3},{2,0},{3,1},{4,6},{5,7},{6,4},{7,5},{8,10},{9,11},{10,... | collective-permute-start | bytes 2359304 | tf_op jit(solution)/shard_map/ppermute | solution.py:129
  143.5 60.6 %collective-permute-start.21 = (bf16[8,32,1152]{2,1,0:T(8,128)(2,1)S(1)}, bf16[8,32,1152]{2,1,0:T(8,128)(2,1)S(1)}, u32[]{:S(2)}, u32[]{:S(2)}) collective-permute-start(bf16[8,32,1152]{2,1,0:T(8,128)(2,1)S(1)} %all-to-all-done.1.refs_16_.refs_8_), channel_id=1, source_target_pairs={{0,24},{8,16},{16,8},{24,0},{1,25},{9,17},{17,9},{25,1},{2,26},{10... | collective-permute-start | bytes 1769480 | tf_op jit(solution)/shard_map/ppermute | solution.py:1061
  145.5 58.0 %collective-permute-start.23 = (bf16[144,1024]{1,0:T(8,128)(2,1)S(1)}, bf16[144,1024]{1,0:T(8,128)(2,1)S(1)}, u32[]{:S(2)}, u32[]{:S(2)}) collective-permute-start(bf16[144,1024]{1,0:T(8,128)(2,1)S(1)} %copy-done.60), channel_id=1, source_target_pairs={{0,16},{8,24},{16,0},{24,8},{1,17},{9,25},{17,1},{25,9},{2,18},{10... | collective-permute-start | bytes 884744 | tf_op jit(solution)/shard_map/ppermute | solution.py:1061
  145.5 58.0 %collective-permute-start.22 = (bf16[144,1024]{1,0:T(8,128)(2,1)S(1)}, bf16[144,1024]{1,0:T(8,128)(2,1)S(1)}, u32[]{:S(2)}, u32[]{:S(2)}) collective-permute-start(bf16[144,1024]{1,0:T(8,128)(2,1)S(1)} %copy-done.60), channel_id=1, source_target_pairs={{0,8},{8,0},{16,24},{24,16},{1,9},{9,1},{17,25},{25,17},{2,10},{10... | collective-permute-start | bytes 884744 | tf_op jit(solution)/shard_map/ppermute | solution.py:1061
  150.4 53.6 %collective-permute-start.24 = (bf16[144,1024]{1,0:T(8,128)(2,1)S(1)}, bf16[144,1024]{1,0:T(8,128)(2,1)S(1)}, u32[]{:S(2)}, u32[]{:S(2)}) collective-permute-start(bf16[144,1024]{1,0:T(8,128)(2,1)S(1)} %copy-done.60), channel_id=1, source_target_pairs={{0,24},{8,16},{16,8},{24,0},{1,25},{9,17},{17,9},{25,1},{2,26},{10... | collective-permute-start | bytes 884744 | tf_op jit(solution)/shard_map/ppermute | solution.py:1061
  153.0 67.8 %collective-permute-start.20 = (bf16[8,32,1152]{2,1,0:T(8,128)(2,1)S(1)}, bf16[8,32,1152]{2,1,0:T(8,128)(2,1)S(1)}, u32[]{:S(2)}, u32[]{:S(2)}) collective-permute-start(bf16[8,32,1152]{2,1,0:T(8,128)(2,1)S(1)} %all-to-all-done.1.refs_16_.refs_8_), channel_id=1, source_target_pairs={{0,16},{8,24},{16,0},{24,8},{1,17},{9,25},{17,1},{25,9},{2,18},{10... | collective-permute-start | bytes 1769480 | tf_op jit(solution)/shard_map/ppermute | solution.py:1061
  203.5 31.1 %collective-permute-start.11 = (bf16[2,1536,128]{2,1,0:T(8,128)(2,1)S(1)}, bf16[2,1536,128]{2,1,0:T(8,128)(2,1)S(1)}, u32[]{:S(2)}, u32[]{:S(2)}) collective-permute-start(bf16[2,1536,128]{2,1,0:T(8,128)(2,1)S(1)} %get-tuple-element.60.refs_0_.o_ref), channel_id=1, source_target_pairs={{0,1},{1,0},{2,3},{3,2},{4,5},{5,4},{6,7},{7,6},{8,9},{9,8},{10,11... | collective-permute-start | bytes 2359304 | tf_op jit(solution)/shard_map/ppermute | solution.py:129
  203.5 31.1 %collective-permute-start.15 = (bf16[2,1536,128]{2,1,0:T(8,128)(2,1)}, bf16[2,1536,128]{2,1,0:T(8,128)(2,1)S(1)}, u32[]{:S(2)}, u32[]{:S(2)}) collective-permute-start(bf16[2,1536,128]{2,1,0:T(8,128)(2,1)} %collective-permute-done.14.refs_4_), channel_id=1, source_target_pairs={{0,1},{1,0},{2,3},{3,2},{4,5},{5,4},{6,7},{7,6},{8,9},{9,8},{10,11... | collective-permute-start | bytes 2359304 | tf_op jit(solution)/shard_map/ppermute | solution.py:129
  204.0 30.6 %collective-permute-start.13 = (bf16[2,1536,128]{2,1,0:T(8,128)(2,1)}, bf16[2,1536,128]{2,1,0:T(8,128)(2,1)}, u32[]{:S(2)}, u32[]{:S(2)}) collective-permute-start(bf16[2,1536,128]{2,1,0:T(8,128)(2,1)} %collective-permute-done.12.refs_2_), channel_id=1, source_target_pairs={{0,1},{1,0},{2,3},{3,2},{4,5},{5,4},{6,7},{7,6},{8,9},{9,8},{10,11... | collective-permute-start | bytes 2359304 | tf_op jit(solution)/shard_map/ppermute | solution.py:129
  204.1 30.5 %collective-permute-start.18 = (bf16[2,1536,128]{2,1,0:T(8,128)(2,1)}, bf16[2,1536,128]{2,1,0:T(8,128)(2,1)}, u32[]{:S(2)}, u32[]{:S(2)}) collective-permute-start(bf16[2,1536,128]{2,1,0:T(8,128)(2,1)} %constant_dynamic-update-slice_fusion.2.refs_6_), channel_id=1, source_target_pairs={{0,1},{1,0},{2,3},{3,2},{4,5},{5,4},{6,7},{7,6},{8,9},{9,8},{10,11... | collective-permute-start | bytes 2359304 | tf_op jit(solution)/shard_map/ppermute | solution.py:129
  220.8 13.8 %collective-permute-start.19 = (bf16[8,32,1152]{2,1,0:T(8,128)(2,1)S(1)}, bf16[8,32,1152]{2,1,0:T(8,128)(2,1)}, u32[]{:S(2)}, u32[]{:S(2)}) collective-permute-start(bf16[8,32,1152]{2,1,0:T(8,128)(2,1)S(1)} %all-to-all-done.1.refs_16_.refs_8_), channel_id=1, source_target_pairs={{0,8},{8,0},{16,24},{24,16},{1,9},{9,1},{17,25},{25,17},{2,10},{10... | collective-permute-start | bytes 1769480 | tf_op jit(solution)/shard_map/ppermute | solution.py:1061
  296.6 19.6 %collective-permute-start.26 = (bf16[2,1,192,1024]{3,2,1,0:T(8,128)(2,1)S(1)}, bf16[2,1,192,1024]{3,2,1,0:T(8,128)(2,1)S(1)}, u32[]{:S(2)}, u32[]{:S(2)}) collective-permute-start(bf16[2,1,192,1024]{3,2,1,0:T(8,128)(2,1)S(1)} %pad_maximum_fusion.2), channel_id=1, source_target_pairs={{0,2},{1,3},{2,0},{3,1},{4,6},{5,7},{6,4},{7,5},{8,10},{9,11},{10,... | collective-permute-start | bytes 2359304 | tf_op jit(solution)/shard_map/ppermute | solution.py:129
  297.2 19.4 %collective-permute-start.27 = (bf16[2,1,192,1024]{3,2,1,0:T(8,128)(2,1)S(1)}, bf16[2,1,192,1024]{3,2,1,0:T(8,128)(2,1)S(1)}, u32[]{:S(2)}, u32[]{:S(2)}) collective-permute-start(bf16[2,1,192,1024]{3,2,1,0:T(8,128)(2,1)S(1)} %pad_maximum_fusion.3), channel_id=1, source_target_pairs={{0,4},{1,5},{2,6},{3,7},{4,0},{5,1},{6,2},{7,3},{8,12},{9,13},{10,... | collective-permute-start | bytes 2359304 | tf_op jit(solution)/shard_map/ppermute | solution.py:129
  339.9 108.6 %collective-permute-start.30 = (bf16[4,2,192,1024]{3,2,1,0:T(8,128)(2,1)}, bf16[4,2,192,1024]{3,2,1,0:T(8,128)(2,1)}, u32[]{:S(2)}, u32[]{:S(2)}) collective-permute-start(bf16[4,2,192,1024]{3,2,1,0:T(8,128)(2,1)} %broadcast_add_fusion), channel_id=1, source_target_pairs={{0,1},{1,0},{2,3},{3,2},{4,5},{5,4},{6,7},{7,6},{8,9},{9,8},{10,11... | collective-permute-start | bytes 9437192 | tf_op jit(solution)/shard_map/ppermute | solution.py:129
  367.7 77.8 %collective-permute-start.54 = (bf16[4,4,32,1024]{3,2,1,0:T(8,128)(2,1)}, bf16[4,4,32,1024]{3,2,1,0:T(8,128)(2,1)}, u32[]{:S(2)}, u32[]{:S(2)}) collective-permute-start(bf16[4,4,32,1024]{3,2,1,0:T(8,128)(2,1)} %pad_maximum_fusion.1), channel_id=1, source_target_pairs={{0,1},{1,0},{2,3},{3,2},{4,5},{5,4},{6,7},{7,6},{8,9},{9,8},{10,11... | collective-permute-start | bytes 3145736 | tf_op jit(solution)/shard_map/ppermute | solution.py:129
  371.1 28.3 %collective-permute-start.38 = (bf16[2,256,576]{1,2,0:T(8,128)(2,1)}, bf16[2,256,576]{1,2,0:T(8,128)(2,1)S(1)}, u32[]{:S(2)}, u32[]{:S(2)}) collective-permute-start(bf16[2,256,576]{1,2,0:T(8,128)(2,1)} %copy.80), channel_id=1, source_target_pairs={{0,8},{8,0},{16,24},{24,16},{1,9},{9,1},{17,25},{25,17},{2,10},{10... | collective-permute-start | bytes 1769480 | tf_op jit(solution)/shard_map/ppermute | solution.py:1061
  371.3 48.9 %collective-permute-start.39 = (bf16[2,256,576]{1,2,0:T(8,128)(2,1)}, bf16[2,256,576]{1,2,0:T(8,128)(2,1)S(1)}, u32[]{:S(2)}, u32[]{:S(2)}) collective-permute-start(bf16[2,256,576]{1,2,0:T(8,128)(2,1)} %copy.81), channel_id=1, source_target_pairs={{0,16},{8,24},{16,0},{24,8},{1,17},{9,25},{17,1},{25,9},{2,18},{10... | collective-permute-start | bytes 1769480 | tf_op jit(solution)/shard_map/ppermute | solution.py:1061
  374.3 48.1 %collective-permute-start.40 = (bf16[2,256,576]{1,2,0:T(8,128)(2,1)S(1)}, bf16[2,256,576]{1,2,0:T(8,128)(2,1)}, u32[]{:S(2)}, u32[]{:S(2)}) collective-permute-start(bf16[2,256,576]{1,2,0:T(8,128)(2,1)S(1)} %copy-done.44), channel_id=1, source_target_pairs={{0,24},{8,16},{16,8},{24,0},{1,25},{9,17},{17,9},{25,1},{2,26},{10... | collective-permute-start | bytes 1769480 | tf_op jit(solution)/shard_map/ppermute | solution.py:1061
  400.2 86.1 %collective-permute-start.37 = (bf16[144,1024]{1,0:T(8,128)(2,1)}, bf16[144,1024]{1,0:T(8,128)(2,1)S(1)}, u32[]{:S(2)}, u32[]{:S(2)}) collective-permute-start(bf16[144,1024]{1,0:T(8,128)(2,1)} %get-tuple-element.124), channel_id=1, source_target_pairs={{0,24},{8,16},{16,8},{24,0},{1,25},{9,17},{17,9},{25,1},{2,26},{10... | collective-permute-start | bytes 884744 | tf_op jit(solution)/shard_map/ppermute | solution.py:1061
  421.1 65.4 %collective-permute-start.36 = (bf16[144,1024]{1,0:T(8,128)(2,1)}, bf16[144,1024]{1,0:T(8,128)(2,1)}, u32[]{:S(2)}, u32[]{:S(2)}) collective-permute-start(bf16[144,1024]{1,0:T(8,128)(2,1)} %get-tuple-element.125), channel_id=1, source_target_pairs={{0,16},{8,24},{16,0},{24,8},{1,17},{9,25},{17,1},{25,9},{2,18},{10... | collective-permute-start | bytes 884744 | tf_op jit(solution)/shard_map/ppermute | solution.py:1061
  422.4 64.1 %collective-permute-start.35 = (bf16[144,1024]{1,0:T(8,128)(2,1)}, bf16[144,1024]{1,0:T(8,128)(2,1)}, u32[]{:S(2)}, u32[]{:S(2)}) collective-permute-start(bf16[144,1024]{1,0:T(8,128)(2,1)} %get-tuple-element.126), channel_id=1, source_target_pairs={{0,8},{8,0},{16,24},{24,16},{1,9},{9,1},{17,25},{25,17},{2,10},{10... | collective-permute-start | bytes 884744 | tf_op jit(solution)/shard_map/ppermute | solution.py:1061
  441.2 17.4 %all-to-all-start.2 = ((bf16[8,2,192,128]{3,2,1,0:T(8,128)(2,1)}), bf16[8,2,192,128]{3,2,1,0:T(8,128)(2,1)}, u32[]{:S(2)}, u32[]{:S(2)}) async-start(bf16[8,2,192,128]{3,2,1,0:T(8,128)(2,1)} %copy-done.18), calls=%async_computation.2 | async-start | bytes 1572864 | tf_op jit(solution)/shard_map/all_to_all | solution.py:231
  451.5 35.0 %collective-permute-start.33 = (bf16[2,1,192,1024]{3,2,1,0:T(8,128)(2,1)}, bf16[2,1,192,1024]{3,2,1,0:T(8,128)(2,1)}, u32[]{:S(2)}, u32[]{:S(2)}) collective-permute-start(bf16[2,1,192,1024]{3,2,1,0:T(8,128)(2,1)} %pad_maximum_fusion.5), channel_id=1, source_target_pairs={{0,4},{1,5},{2,6},{3,7},{4,0},{5,1},{6,2},{7,3},{8,12},{9,13},{10,... | collective-permute-start | bytes 2359304 | tf_op jit(solution)/shard_map/ppermute | solution.py:129
  454.4 32.2 %collective-permute-start.31 = (bf16[2,1,192,1024]{3,2,1,0:T(8,128)(2,1)}, bf16[2,1,192,1024]{3,2,1,0:T(8,128)(2,1)}, u32[]{:S(2)}, u32[]{:S(2)}) collective-permute-start(bf16[2,1,192,1024]{3,2,1,0:T(8,128)(2,1)} %pad_maximum_fusion.4), channel_id=1, source_target_pairs={{0,2},{1,3},{2,0},{3,1},{4,6},{5,7},{6,4},{7,5},{8,10},{9,11},{10,... | collective-permute-start | bytes 2359304 | tf_op jit(solution)/shard_map/ppermute | solution.py:129
  486.3 29.7 %collective-permute-start.57 = (bf16[2,2,32,1024]{3,2,1,0:T(8,128)(2,1)}, bf16[2,2,32,1024]{3,2,1,0:T(8,128)(2,1)}, u32[]{:S(2)}, u32[]{:S(2)}) collective-permute-start(bf16[2,2,32,1024]{3,2,1,0:T(8,128)(2,1)} %pad_maximum_fusion.9), channel_id=1, source_target_pairs={{0,4},{1,5},{2,6},{3,7},{4,0},{5,1},{6,2},{7,3},{8,12},{9,13},{10,... | collective-permute-start | bytes 786440 | tf_op jit(solution)/shard_map/ppermute | solution.py:129
  507.0 66.7 %collective-permute-start.41 = (bf16[4,2,192,1024]{3,2,1,0:T(8,128)(2,1)}, bf16[4,2,192,1024]{3,2,1,0:T(8,128)(2,1)}, u32[]{:S(2)}, u32[]{:S(2)}) collective-permute-start(bf16[4,2,192,1024]{3,2,1,0:T(8,128)(2,1)} %get-tuple-element.80), channel_id=1, source_target_pairs={{0,1},{1,0},{2,3},{3,2},{4,5},{5,4},{6,7},{7,6},{8,9},{9,8},{10,11... | collective-permute-start | bytes 9437192 | tf_op jit(solution)/shard_map/ppermute | solution.py:129
  511.8 15.8 %all-to-all-start.4 = ((bf16[8,2,32,576]{3,2,1,0:T(8,128)(2,1)}), bf16[8,2,32,576]{3,2,1,0:T(8,128)(2,1)S(1)}, u32[]{:S(2)}, u32[]{:S(2)}) async-start(bf16[8,2,32,576]{3,2,1,0:T(8,128)(2,1)} %bitcast.183), calls=%async_computation.4 | async-start | bytes 1310720 | tf_op jit(solution)/shard_map/all_to_all | solution.py:231
  516.9 14.8 %collective-permute-start.58 = (bf16[2,32,1024]{2,1,0:T(8,128)(2,1)S(1)}, bf16[2,32,1024]{2,1,0:T(8,128)(2,1)S(1)}, u32[]{:S(2)}, u32[]{:S(2)}) collective-permute-start(bf16[2,32,1024]{2,1,0:T(8,128)(2,1)S(1)} %fusion.20), channel_id=1, source_target_pairs={{0,2},{1,3},{2,0},{3,1},{4,6},{5,7},{6,4},{7,5},{8,10},{9,11},{10,... | collective-permute-start | bytes 393224 | tf_op jit(solution)/shard_map/ppermute | solution.py:129
  520.0 11.8 %collective-permute-start.56 = (bf16[2,32,1024]{2,1,0:T(8,128)(2,1)S(1)}, bf16[2,32,1024]{2,1,0:T(8,128)(2,1)S(1)}, u32[]{:S(2)}, u32[]{:S(2)}) collective-permute-start(bf16[2,32,1024]{2,1,0:T(8,128)(2,1)S(1)} %fusion.23), channel_id=1, source_target_pairs={{0,4},{1,5},{2,6},{3,7},{4,0},{5,1},{6,2},{7,3},{8,12},{9,13},{10,... | collective-permute-start | bytes 393224 | tf_op jit(solution)/shard_map/ppermute | solution.py:129
  544.8 14.8 %collective-permute-start.46 = (bf16[256,256]{1,0:T(8,128)(2,1)S(1)}, bf16[256,256]{1,0:T(8,128)(2,1)S(1)}, u32[]{:S(2)}, u32[]{:S(2)}) collective-permute-start(bf16[256,256]{1,0:T(8,128)(2,1)S(1)} %get-tuple-element.129), channel_id=1, source_target_pairs={{0,8},{8,0},{16,24},{24,16},{1,9},{9,1},{17,25},{25,17},{2,10},{10... | collective-permute-start | bytes 393224 | tf_op jit(solution)/shard_map/ppermute | solution.py:1061
  546.8 13.3 %collective-permute-start.48 = (bf16[256,256]{1,0:T(8,128)(2,1)S(1)}, bf16[256,256]{1,0:T(8,128)(2,1)S(1)}, u32[]{:S(2)}, u32[]{:S(2)}) collective-permute-start(bf16[256,256]{1,0:T(8,128)(2,1)S(1)} %get-tuple-element.130), channel_id=1, source_target_pairs={{0,24},{8,16},{16,8},{24,0},{1,25},{9,17},{17,9},{25,1},{2,26},{10... | collective-permute-start | bytes 393224 | tf_op jit(solution)/shard_map/ppermute | solution.py:1061
  559.0 19.2 %collective-permute-start.32 = (bf16[1,192,1024]{2,1,0:T(8,128)(2,1)S(1)}, bf16[1,192,1024]{2,1,0:T(8,128)(2,1)S(1)}, u32[]{:S(2)}, u32[]{:S(2)}) collective-permute-start(bf16[1,192,1024]{2,1,0:T(8,128)(2,1)S(1)} %get-tuple-element.97), channel_id=1, source_target_pairs={{0,4},{1,5},{2,6},{3,7},{4,0},{5,1},{6,2},{7,3},{8,12},{9,13},{10,... | collective-permute-start | bytes 1179656 | tf_op jit(solution)/shard_map/ppermute | solution.py:129
  559.6 20.0 %collective-permute-start.34 = (bf16[1,192,1024]{2,1,0:T(8,128)(2,1)S(1)}, bf16[1,192,1024]{2,1,0:T(8,128)(2,1)S(1)}, u32[]{:S(2)}, u32[]{:S(2)}) collective-permute-start(bf16[1,192,1024]{2,1,0:T(8,128)(2,1)S(1)} %get-tuple-element.98), channel_id=1, source_target_pairs={{0,2},{1,3},{2,0},{3,1},{4,6},{5,7},{6,4},{7,5},{8,10},{9,11},{10,... | collective-permute-start | bytes 1179656 | tf_op jit(solution)/shard_map/ppermute | solution.py:129
  576.4 19.0 %collective-permute-start.44 = (bf16[2,1,192,1024]{3,2,1,0:T(8,128)(2,1)S(1)}, bf16[2,1,192,1024]{3,2,1,0:T(8,128)(2,1)S(1)}, u32[]{:S(2)}, u32[]{:S(2)}) collective-permute-start(bf16[2,1,192,1024]{3,2,1,0:T(8,128)(2,1)S(1)} %pad_maximum_fusion.7), channel_id=1, source_target_pairs={{0,4},{1,5},{2,6},{3,7},{4,0},{5,1},{6,2},{7,3},{8,12},{9,13},{10,... | collective-permute-start | bytes 2359304 | tf_op jit(solution)/shard_map/ppermute | solution.py:129
  577.1 18.7 %collective-permute-start.42 = (bf16[2,1,192,1024]{3,2,1,0:T(8,128)(2,1)S(1)}, bf16[2,1,192,1024]{3,2,1,0:T(8,128)(2,1)S(1)}, u32[]{:S(2)}, u32[]{:S(2)}) collective-permute-start(bf16[2,1,192,1024]{3,2,1,0:T(8,128)(2,1)S(1)} %pad_maximum_fusion.6), channel_id=1, source_target_pairs={{0,2},{1,3},{2,0},{3,1},{4,6},{5,7},{6,4},{7,5},{8,10},{9,11},{10,... | collective-permute-start | bytes 2359304 | tf_op jit(solution)/shard_map/ppermute | solution.py:129
  (89 other events, 1170.2 us)
Sparse Core Ops, SparseCore 0:
  10.9 65.6 all-gather.4
  78.5 44.7 all-gather.2

commit v3 on v2

--- a/solution.py
+++ b/solution.py
@@ -130,17 +130,10 @@
 
 
 def partner_blocks(block):
-    half = block.shape[0] // 2
-    got = {0: block}
-    got[2] = swap(block, 2)
-    got[4] = swap(block, 4)
-    got[1] = swap(block, 1)
-    via_x = swap(got[4][:half], 2)
-    via_y = swap(got[2][half:], 4)
-    got[3] = swap(got[2], 1)
-    got[5] = swap(got[4], 1)
-    got[6] = jnp.concatenate([via_x, via_y], axis=0)
-    got[7] = swap(got[6], 1)
+    got = {0: block, 2: swap(block, 2), 4: swap(block, 4)}
+    got[6] = swap(got[4], 2)
+    for mask in (0, 2, 4, 6):
+        got[mask + 1] = swap(got[mask], 1)
     return [got[j] for j in range(8)]
 
 
@@ -256,7 +249,14 @@
 def head_mean():
     row = lax.broadcasted_iota(jnp.int32, (128, 128), 0) // HD
     col = lax.broadcasted_iota(jnp.int32, (128, 128), 1) // HD
-    return jnp.where(row == col, 1.0 / HD, 0.0).astype(f32)
+    return jnp.where(row == col, 1.0 / HD, 0.0).astype(bf16)
+
+
+def head_average(array):
+    high = array.astype(bf16)
+    low = (array - high.astype(f32)).astype(bf16)
+    mean = head_mean()
+    return jnp.dot(high, mean, preferred_element_type=f32) + jnp.dot(low, mean, preferred_element_type=f32)
 
 
 def lane_index(rows):
@@ -270,7 +270,8 @@
     return jnp.where(low, ahead, -behind) if back else jnp.where(low, -ahead, behind)
 
 
-def attn_fwd_kernel(block, q_ref, kv_ref, start_ref, out_ref, lse_ref):
+def attn_fwd_kernel(block, q_ref, kv_ref, start_ref, *refs):
+    out_ref, lse_ref = refs[-2:]
     step = pl.program_id(1)
     steps = kv_ref.shape[1] // block
     lanes = lane_index(block)
@@ -299,7 +300,7 @@
             lse_ref[0] = jnp.where(lanes < HD, totals[0], totals[1])
 
 
-def attn_fwd(q, kv, starts, span):
+def attn_fwd(q, kv, starts, span, earlier):
     seqs, length, _ = q.shape
     block = 2 * span
     rows = lambda b, i: (b, i, 0)
@@ -311,7 +312,8 @@
             pl.BlockSpec((1, block, 128), rows),
             pl.BlockSpec((1, length, 128), whole),
             pl.BlockSpec((1, block, 128), rows),
-        ],
+        ]
+        + [pl.BlockSpec(memory_space=pl.ANY)] * len(earlier),
         out_specs=[pl.BlockSpec((1, block, 128), rows), pl.BlockSpec((1, block, 128), rows)],
         out_shape=[
             jax.ShapeDtypeStruct((seqs, length, 128), bf16),
@@ -320,7 +322,7 @@
         compiler_params=pltpu.CompilerParams(vmem_limit_bytes=48 << 20),
         cost_estimate=pl.CostEstimate(flops=seqs * length * length * 256, bytes_accessed=seqs * length * 1792, transcendentals=seqs * length * length),
         name="attn_fwd",
-    )(q, kv, starts)
+    )(q, kv, starts, *earlier)
 
 
 def attn_bwd_kernel(block, q_ref, kv_ref, do_ref, o_ref, lse_ref, start_ref, *refs):
@@ -398,25 +400,33 @@
     return [pl.BlockSpec(memory_space=pl.ANY)] * count
 
 
-def pack_kernel(groups, part, gate_ref, up_ref, out_ref):
+def pack_kernel(groups, part, gate_ref, up_ref, q_ref, k_ref, v_ref, gain_ref, out_ref):
     size = gate_ref.shape[1] // (groups * part)
-    for at, ref in ((0, gate_ref), (size * part, up_ref)):
+    hidden = size * part
+    for at, ref in ((0, gate_ref), (hidden, up_ref)):
         whole = ref[...].astype(f32)
         for g in range(groups):
             cuts = [whole[:, (f * groups + g) * part : (f * groups + g + 1) * part] for f in range(size)]
-            out_ref[g, :, at : at + size * part] = jnp.concatenate(cuts, axis=1).astype(bf16)
-
-
-def pack_columns(gate, up, groups, part):
+            out_ref[g, :, at : at + hidden] = jnp.concatenate(cuts, axis=1).astype(bf16)
+    k, v = k_ref[...].astype(f32), v_ref[...].astype(f32)
+    for g in range(groups):
+        at = slice(g * HD, (g + 1) * HD)
+        out_ref[g, :, 2 * hidden : 2 * hidden + 128] = q_ref[:, g * 128 : (g + 1) * 128]
+        both = jnp.concatenate([k[:, at], v[:, at]], axis=1)
+        out_ref[g, :, 2 * hidden + 128 : 2 * hidden + 256] = both.astype(bf16)
+        out_ref[g, :, 2 * hidden + 256 :] = gain_ref[...]
+
+
+def pack_columns(gate, up, query, key, value, gains, groups, part):
     shard, total = gate.shape
     return pl.pallas_call(
         functools.partial(pack_kernel, groups, part),
-        out_shape=jax.ShapeDtypeStruct((groups, shard, 2 * total // groups), bf16),
+        out_shape=jax.ShapeDtypeStruct((groups, shard, 2 * total // groups + 384), bf16),
         name="pack",
-    )(gate, up)
-
-
-def unpack_kernel(part, home_ref, gate_w_ref, up_w_ref, gate_ref, up_ref, sum_ref):
+    )(gate, up, query, key, value, gains)
+
+
+def unpack_kernel(part, home_ref, gate_w_ref, up_w_ref, _, gate_ref, up_ref, sum_ref):
     groups, _, shard, hidden = home_ref.shape
     size = hidden // part
     for which, ref in ((0, gate_ref), (1, up_ref)):
@@ -428,35 +438,38 @@
     sum_ref[...] = jnp.broadcast_to(total, sum_ref.shape)
 
 
-def unpack_columns(home, gate_w, up_w, part):
+def unpack_columns(home, gate_w, up_w, part, earlier):
     shape = gate_w.shape
     return pl.pallas_call(
         functools.partial(unpack_kernel, part),
+        in_specs=[pl.BlockSpec(memory_space=pltpu.VMEM)] * 3 + any_space(1),
         out_shape=[
             jax.ShapeDtypeStruct(shape, f32),
             jax.ShapeDtypeStruct(shape, f32),
             jax.ShapeDtypeStruct((shape[0], 128), f32),
         ],
         name="unpack",
-    )(home, gate_w, up_w)
-
-
-def unpack_heads_kernel(home_ref, q_w_ref, k_w_ref, v_w_ref, q_ref, k_ref, v_ref, sum_ref):
-    blocks = [home_ref[g].astype(f32) for g in range(home_ref.shape[0])]
-    q_ref[...] = jnp.concatenate([block[:, : 2 * HD] for block in blocks], axis=1)
-    k_ref[...] = jnp.concatenate([block[:, 2 * HD : 3 * HD] for block in blocks], axis=1)
-    v_ref[...] = jnp.concatenate([block[:, 3 * HD :] for block in blocks], axis=1)
+    )(home, gate_w, up_w, earlier)
+
+
+def unpack_heads_kernel(home_ref, q_w_ref, k_w_ref, v_w_ref, q_ref, k_ref, v_ref, sum_ref, gain_ref):
+    groups, shard = home_ref.shape[0], q_ref.shape[0]
+    blocks = [home_ref[g].astype(f32) for g in range(groups)]
+    q_ref[...] = jnp.concatenate([block[:shard, : 2 * HD] for block in blocks], axis=1)
+    k_ref[...] = jnp.concatenate([block[:shard, 2 * HD : 3 * HD] for block in blocks], axis=1)
+    v_ref[...] = jnp.concatenate([block[:shard, 3 * HD :] for block in blocks], axis=1)
     total = 0.0
     for weight, grad in ((q_w_ref, q_ref), (k_w_ref, k_ref), (v_w_ref, v_ref)):
         total += jnp.sum(weight[...].astype(f32) * grad[...], axis=1, keepdims=True)
     sum_ref[...] = jnp.broadcast_to(total, sum_ref.shape)
+    gain_ref[...] = sum(block[shard : shard + 8] for block in blocks)
 
 
 def unpack_heads(home, q_w, k_w, v_w):
     return pl.pallas_call(
         unpack_heads_kernel,
         out_shape=[jax.ShapeDtypeStruct(w.shape, f32) for w in (q_w, k_w, v_w)]
-        + [jax.ShapeDtypeStruct((q_w.shape[0], 128), f32)],
+        + [jax.ShapeDtypeStruct((q_w.shape[0], 128), f32), jax.ShapeDtypeStruct((8, home.shape[2]), f32)],
         name="unpack_heads",
     )(home, q_w, k_w, v_w)
 
@@ -472,7 +485,7 @@
         for m in range(4):
             for g in range(8):
                 row = pl.multiple_of(((at_ref[1] ^ m) * 8 + g) * shard, shard)
-                w_ref[pl.ds(row, shard), :] = w_refs[m][g, :shard, :]
+                w_ref[pl.ds(row, shard), :] = w_refs[m][g, :, :256]
 
     for j in range(8):
 
@@ -488,10 +501,9 @@
     raw_ref[...] = raw.reshape(raw_ref.shape)
     cos = cos_ref[...].reshape(-1, 128)
     sin = sin_ref[...].reshape(-1, 128)
-    mean = head_mean()
 
     def prepared(part, scale):
-        inv = lax.rsqrt(jnp.dot(part * part, mean, precision=exact, preferred_element_type=f32) + eps)
+        inv = lax.rsqrt(head_average(part * part) + eps)
         normed = part * inv * scale
         return normed * cos + half_turn(normed, False) * sin
 
@@ -566,24 +578,30 @@
 
 
 def ffn_kernel(hidden, padded, at_ref, *refs):
-    parts, wgu_refs, wd_refs = refs[:8], refs[8:12], refs[12:16]
-    (x_ref, cot_ref, wo_ref, gain_ref, attn_ref, mid_ref, nm_ref, hid_ref, grads_ref) = refs[16:25]
-    gnm_even, gnm_odd, out_even, out_odd, wgu, wd = refs[25:]
+    parts, cot_refs, wd_parts = refs[:8], refs[8:16], refs[16]
+    (x_ref, wo_parts, wgu_ref, gain_ref, attn_ref, mid_ref, nm_ref, hid_ref, grads_ref) = refs[17:26]
+    gnm_even, gnm_odd, out_even, out_odd, cot_ref, wo_ref, wgu, wd = refs[26:]
     step = pl.program_id(0)
 
     @pl.when(step == 0)
     def _():
-        rows = wgu.shape[0] // 4
-        part = hidden // 4
+        shard = wo_parts.shape[2]
+        part = wd_parts.shape[1] - shard
         wgu[...] = jnp.zeros_like(wgu)
+        wgu[:, :hidden] = wgu_ref[:, :hidden]
+        wgu[:, padded : padded + hidden] = wgu_ref[:, hidden:]
         wd[hidden:, :] = jnp.zeros((padded - hidden, wd.shape[1]), bf16)
-        for m in range(4):
-            from_f = at_ref[1] ^ m
-            block = wgu_refs[m][...].reshape(rows, 2 * hidden)
-            at = pl.ds(pl.multiple_of(from_f * rows, rows), rows)
-            wgu[at, :hidden] = block[:, :hidden]
-            wgu[at, padded : padded + hidden] = block[:, hidden:]
-            wd[pl.ds(pl.multiple_of(from_f * part, 16), part), :] = wd_refs[m][...]
+        for f in range(wd_parts.shape[0]):
+            wd[f * part : (f + 1) * part, :] = wd_parts[f, :part, :]
+            for g in range(8):
+                row = (f * 8 + g) * shard
+                wo_ref[row : row + shard, :] = wo_parts[g, f]
+
+    for j in range(8):
+
+        @pl.when((at_ref[0] ^ step) == j)
+        def _(j=j):
+            cot_ref[...] = cot_refs[j][...]
 
     tile = attn_ref.shape[0] * attn_ref.shape[1]
     width = wo_ref.shape[0]
@@ -611,10 +629,10 @@
     store_halves(at_ref[0], step, out, out_even, out_odd)
 
 
-def ffn(at, parts, wgu_blocks, wd_blocks, x, cot, w_out, gain):
+def ffn(at, parts, cot_blocks, wd_parts, x, wo_parts, w_gate_up, gain):
     seqs, length, width = x.shape
     span = length // 8
-    hidden = 4 * wd_blocks[0].shape[0]
+    hidden = w_gate_up.shape[1] // 2
     padded = -(-hidden // 128) * 128
     home = lambda t, m: (0, t, 0)
     fixed = lambda t, m: (0, 0)
@@ -628,24 +646,26 @@
             num_scalar_prefetch=1,
             grid=(8,),
             in_specs=[tokens(128)] * 8
-            + [pl.BlockSpec(wgu_blocks[0].shape, lambda t, m: (0, 0, 0), **once)] * 4
-            + [pl.BlockSpec(wd_blocks[0].shape, fixed, **once)] * 4
+            + [pl.BlockSpec((seqs, span, width), lambda t, m: (0, 0, 0), **once)] * 8
+            + [pl.BlockSpec(wd_parts.shape, lambda t, m: (0, 0, 0), **once)]
             + [
                 tokens(width),
-                tokens(width),
-                pl.BlockSpec((width, width), fixed, **once),
+                pl.BlockSpec(wo_parts.shape, lambda t, m: (0, 0, 0, 0), **once),
+                pl.BlockSpec((width, 2 * hidden), fixed, **once),
                 pl.BlockSpec((1, width), fixed, **once),
             ],
             out_specs=[tokens(width), tokens(width), tokens(width), tokens(padded), tokens(2 * padded)]
-            + [halves_spec(seqs, span, width)] * 4,
+            + [halves_spec(seqs, span, width)] * 4
+            + [tokens(width), pl.BlockSpec((width, width), fixed)],
             scratch_shapes=[pltpu.VMEM((width, 2 * padded), bf16), pltpu.VMEM((padded, width), bf16)],
         ),
         out_shape=[shape(width, bf16), shape(width, f32), shape(width, bf16), shape(padded, bf16), shape(2 * padded, bf16)]
-        + [half] * 4,
+        + [half] * 4
+        + [shape(width, bf16), jax.ShapeDtypeStruct((width, width), bf16)],
         compiler_params=pltpu.CompilerParams(vmem_limit_bytes=60 << 20),
         cost_estimate=pl.CostEstimate(flops=seqs * length * width * (2 * width + 12 * padded), bytes_accessed=seqs * length * width * 20, transcendentals=seqs * length * padded),
         name="ffn",
-    )(at, *parts, *wgu_blocks, *wd_blocks, x, cot, w_out, gain)
+    )(at, *parts, *cot_blocks, wd_parts, x, wo_parts, w_gate_up, gain)
 
 
 def product_kernel(cuts, left_ref, right_ref, *refs):
@@ -663,12 +683,17 @@
 
     @pl.when(step == pl.num_programs(0) - 1)
     def _():
-        for i, (begin, end) in enumerate(cuts):
-            out_ref[i] = total[: out_ref.shape[1], begin:end].astype(bf16)
-
-
-def product(left, right, out_rows, cuts, earlier=()):
+        size, blocks, _, count, _ = out_ref.shape
+        for f in range(size):
+            for g in range(blocks):
+                row = (f * blocks + g) * count
+                for i, (begin, end) in enumerate(cuts):
+                    out_ref[f, g, i] = total[row : row + count, begin:end].astype(bf16)
+
+
+def product(left, right, split, cuts, earlier=()):
     rows = left.shape[0]
+    shape = (split[0], split[1], len(cuts), split[2], cuts[0][1] - cuts[0][0])
     tile = 512
     at = lambda i: (i, 0)
     return pl.pallas_call(
@@ -676,8 +701,8 @@
         grid=(rows // tile,),
         in_specs=[pl.BlockSpec((tile, left.shape[1]), at), pl.BlockSpec((tile, right.shape[1]), at)]
         + any_space(len(earlier)),
-        out_specs=pl.BlockSpec((len(cuts), out_rows, cuts[0][1] - cuts[0][0]), lambda i: (0, 0, 0)),
-        out_shape=jax.ShapeDtypeStruct((len(cuts), out_rows, cuts[0][1] - cuts[0][0]), bf16),
+        out_specs=pl.BlockSpec(shape, lambda i: (0, 0, 0, 0, 0)),
+        out_shape=jax.ShapeDtypeStruct(shape, bf16),
         scratch_shapes=[pltpu.VMEM((left.shape[1], right.shape[1]), f32)],
         compiler_params=pltpu.CompilerParams(vmem_limit_bytes=48 << 20),
         cost_estimate=pl.CostEstimate(flops=2 * rows * left.shape[1] * right.shape[1], bytes_accessed=2 * rows * (left.shape[1] + right.shape[1]), transcendentals=0),
@@ -685,11 +710,13 @@
     )(left, right, *earlier)
 
 
-def mid_kernel(at_ref, mid_ref, cot_ref, gain_ref, wo_ref, even_ref, got_ref, sent_x, sent_y, last_x, last_y, grad_ref, half_ref, out_ref):
+def mid_kernel(at_ref, mid_ref, cot_ref, gain_ref, wo_ref, even_ref, got_ref, *refs):
+    grad_ref, half_ref, out_ref = refs[-3:]
     seqs, span, width = cot_ref.shape
     grad_nm = even_ref[0].astype(f32) + got_ref[0].astype(f32)
-    more = [sent_x[0].astype(f32) + last_y[...].astype(f32), sent_y[0].astype(f32) + last_x[...].astype(f32)]
-    grad_nm = (grad_nm + jnp.concatenate(more, axis=0)).reshape(seqs * span, width)
+    for part_ref in refs[:3]:
+        grad_nm += part_ref[...].astype(f32)
+    grad_nm = grad_nm.reshape(seqs * span, width)
     mid = mid_ref[...].reshape(seqs * span, width)
     factor = lax.rsqrt(jnp.mean(mid * mid, axis=-1, keepdims=True) + eps)
     normed = mid * factor
@@ -705,10 +732,8 @@
         out_ref[g] = out[:, g * 128 : (g + 1) * 128].reshape(seqs, span, 128)
 
 
-def mid_bwd(at, mid, cot, gain, w_out, even, stages):
+def mid_bwd(at, mid, cot, gain, w_out, even, stages, earlier):
     seqs, span, width = cot.shape
-    got, sent_x, sent_y, last_x, last_y = stages
-    half = seqs // 2
     first = lambda *s: pl.BlockSpec((1,) + s, lambda i, m: (0,) * (len(s) + 1))
     full = lambda *s: pl.BlockSpec(s, lambda i, m: (0,) * len(s))
     rows = seqs * span
@@ -724,11 +749,11 @@
                 full(width, width),
                 first(seqs, span, width),
                 first(seqs, span, width),
-                first(half, span, width),
-                first(half, span, width),
-                full(half, span, width),
-                full(half, span, width),
-            ],
+                full(seqs, span, width),
+                full(seqs, span, width),
+                full(seqs, span, width),
+            ]
+            + any_space(len(earlier)),
             out_specs=[full(rows, width), full(rows, width), full(8, seqs, span, 128)],
         ),
         out_shape=[
@@ -739,7 +764,7 @@
         compiler_params=pltpu.CompilerParams(vmem_limit_bytes=40 << 20),
         cost_estimate=pl.CostEstimate(flops=2 * rows * width * width, bytes_accessed=rows * width * 20, transcendentals=0),
         name="mid_bwd",
-    )(at, mid, cot, gain, w_out, even, got, sent_x, sent_y, last_x, last_y)
+    )(at, mid, cot, gain, w_out, even, *stages, *earlier)
 
 
 def qkv_bwd_kernel(at_ref, dq_ref, dkv_ref, raw_ref, nm_ref, w_ref, scale_ref, cos_ref, sin_ref, *refs):
@@ -754,17 +779,12 @@
         dscale_ref[...] = jnp.zeros_like(dscale_ref)
 
     cos, sin = cos_ref[...].reshape(tile, 128), sin_ref[...].reshape(tile, 128)
-    mean = head_mean()
-
-    def average(array):
-        return jnp.dot(array, mean, precision=exact, preferred_element_type=f32)
-
     def back(raw, grad, scale):
-        inv = lax.rsqrt(average(raw * raw) + eps)
+        inv = lax.rsqrt(head_average(raw * raw) + eps)
         normed = raw * inv
         turned = grad * cos + half_turn(grad * sin, True)
         grad_normed = turned * scale
-        grad_raw = inv * (grad_normed - normed * average(grad_normed * normed))
+        grad_raw = inv * (grad_normed - normed * head_average(grad_normed * normed))
         return grad_raw, jnp.sum(turned * normed, axis=0, keepdims=True)
 
     raw = raw_ref[...].reshape(tile, 256)
@@ -1077,26 +1097,21 @@
     return total
 
 
-def reduce_stages(even, odd):
-    half = even.shape[1] // 2
+def reduce_stages(even, odd, earlier=None):
     got = swap(odd, 1)
 
-    def held(i, low):
-        cut = slice(0, half) if low else slice(half, None)
-        return even[i, cut].astype(f32) + got[i, cut].astype(f32)
-
-    sent_x = swap(jnp.stack([held(1, True), held(3, True)]).astype(bf16), 2)
-    sent_y = swap(jnp.stack([held(2, False), held(3, False)]).astype(bf16), 4)
-    last_y = swap((held(2, True) + sent_x[1].astype(f32)).astype(bf16), 4)
-    last_x = swap((held(1, False) + sent_y[1].astype(f32)).astype(bf16), 2)
-    return got, sent_x, sent_y, last_x, last_y
+    def sent(i):
+        total = even[i].astype(f32) + got[i].astype(f32)
+        return swap((total if earlier is None else after(total, earlier)).astype(bf16), 2 * i)
+
+    return got, sent(1), sent(2), sent(3)
 
 
 def own_sum(even, stages):
-    got, sent_x, sent_y, last_x, last_y = stages
-    low = sent_x[0].astype(f32) + last_y.astype(f32)
-    high = sent_y[0].astype(f32) + last_x.astype(f32)
-    return even[0].astype(f32) + got[0].astype(f32) + jnp.concatenate([low, high], axis=0)
+    total = even[0].astype(f32) + stages[0][0].astype(f32)
+    for part in stages[1:]:
+        total = total + part.astype(f32)
+    return total
 
 
 def body(
@@ -1146,31 +1161,33 @@
     hidden_cols = part * size
     padded = -(-hidden_cols // 128) * 128
 
+    gains = jnp.concatenate([attention_gain, feedforward_gain])
+    gains = jnp.zeros((shard, 128), bf16).at[0, : 2 * shard].set(gains)
+    packed = spread(
+        pack_columns(gate_weight, up_weight, query_weight, key_weight, value_weight, gains, groups, part)
+    )
     x_blocks = partner_blocks(block_input)
-    packed = jnp.concatenate(
-        [
-            query_weight.reshape(shard, groups, 2 * HD),
-            key_weight.reshape(shard, groups, HD),
-            value_weight.reshape(shard, groups, HD),
-        ],
-        axis=2,
-    ).transpose(1, 0, 2)
-    gains = jnp.concatenate([attention_gain, feedforward_gain])
-    gain_rows = jnp.zeros((16, 4 * HD), bf16).at[0, : 2 * shard].set(gains)
-    packed = jnp.concatenate(
-        [packed, jnp.broadcast_to(gain_rows[None], (groups, 16, 4 * HD))], axis=1
-    )
-    qkv_blocks = line_blocks(spread(packed))
-    gains = jnp.stack([block[:, shard, : 2 * shard] for block in qkv_blocks])
-    gains = jnp.take(gains, me_line ^ jnp.arange(size), axis=0).astype(f32)
+    qkv_blocks = line_blocks(packed[:, :, 2 * hidden_cols :])
+    gains = [block[:, 0, 256 : 256 + 2 * shard].astype(f32) for block in qkv_blocks]
+    gains = jnp.stack(
+        [sum(jnp.where((me_line ^ m) == f, gains[m], 0.0) for m in range(size)) for f in range(size)]
+    )
     gain_one = gains[:, :, :shard].reshape(1, width)
     gain_two = gains[:, :, shard:].reshape(1, width)
-
-    down_blocks = line_blocks(down_weight)
-    gate_up = spread(after(pack_columns(gate_weight, up_weight, groups, part), x_blocks[6]))
-    gate_up_blocks = line_blocks(gate_up)
-    w_out = lax.all_gather(output_weight, ("fsdp", "seq"), axis=0, tiled=True)
-    cot_full = lax.all_gather(cotangent, "seq", axis=1, tiled=True)
+    down_parts = lax.all_gather(
+        jnp.concatenate([down_weight, output_weight], axis=0), "fsdp", axis=0, tiled=False
+    )
+    wo_parts = lax.all_gather(down_parts[:, part:], "seq", axis=0, tiled=False)
+    w_gate_up = packed[:, :, : 2 * hidden_cols]
+    for block in qkv_blocks[1:]:
+        w_gate_up = after(w_gate_up, block)
+    w_gate_up = lax.all_gather(w_gate_up, "fsdp", axis=0, tiled=False).reshape(width, 2 * hidden_cols)
+    cot_blocks = {0: cotangent}
+    for mask in (2, 4):
+        cot_blocks[mask] = swap(after(cotangent, x_blocks[6]), mask)
+    cot_blocks[6] = swap(cot_blocks[2], 4)
+    for mask in (0, 2, 4, 6):
+        cot_blocks[mask + 1] = swap(cot_blocks[mask], 1)
 
     inverse = rope_base ** (-(jnp.arange(HD // 2, dtype=f32) * 2.0) / HD)
     angles = positions.astype(f32)[:, :, None] * jnp.tile(inverse, 4)[None, None, :]
@@ -1180,41 +1197,55 @@
     ).astype(f32)
     starts = jnp.arange(length, dtype=jnp.int32)[None, :] - positions
     x_full, normed_in, qkv_raw, q_rows, kv_rows, w_qkv = qkv_fwd(
-        at, x_blocks, qkv_blocks, gain_one, scales, cosine, sine, [gate_up]
+        at, x_blocks, qkv_blocks, gain_one, scales, cosine, sine, []
     )
     starts_wide = jnp.broadcast_to(starts[:, :, None], (seqs, length, 128))
-    outputs, totals = attn_fwd(q_rows, kv_rows, starts_wide, span)
-
-    attn_rows, residual_mid, normed_mid, hidden, ff_grads, gnm_even, gnm_odd, out_even, out_odd = ffn(
-        at, partner_blocks(outputs), gate_up_blocks, down_blocks, x_full, cot_full, w_out, gain_two
+    outputs, totals = attn_fwd(q_rows, kv_rows, starts_wide, span, [cot_blocks[2], cot_blocks[4]])
+
+    (attn_rows, residual_mid, normed_mid, hidden, ff_grads, gnm_even, gnm_odd, out_even, out_odd, cot_full, w_out) = ffn(
+        at,
+        partner_blocks(outputs),
+        [cot_blocks[j] for j in range(8)],
+        down_parts,
+        x_full,
+        wo_parts,
+        w_gate_up,
+        gain_two,
     )
     flat = lambda array: array.reshape(rows, -1)
 
     mid_stages = reduce_stages(gnm_even, gnm_odd)
-    down_term = product(flat(hidden), flat(cot_full), hidden_cols, ((0, width),), [mid_stages[0]])[0]
     cuts = ((0, hidden_cols), (padded, padded + hidden_cols))
-    gate_up_term = product(flat(normed_mid), flat(ff_grads), width, cuts, [down_term])
+    gate_up_term = product(flat(normed_mid), flat(ff_grads), (size, groups, shard), cuts)
+    waits = [mid_stages[0], gate_up_term]
+    down_term = product(flat(hidden), flat(cot_full), (size, 1, part), ((0, width),), waits)
     grad_mid, grad_mid_half, grad_attn_out = mid_bwd(
-        at, residual_mid, cotangent, gain_two, w_out, gnm_even, mid_stages
+        at, residual_mid, cotangent, gain_two, w_out, gnm_even, mid_stages, [down_term, gate_up_term]
     )
     grad_heads = spread(grad_attn_out)
 
     def block_rows(term, f, count):
         return lax.dynamic_slice_in_dim(term, f * count, count, term.ndim - 2)
 
-    down_parts = line_parts(lambda f: block_rows(down_term, f, part))
-    gate_up_parts = line_parts(lambda f: block_rows(gate_up_term, f, groups * shard))
-    out_stages = reduce_stages(out_even, after(out_odd, grad_mid_half))
+    gate_up_sum = lax.psum_scatter(gate_up_term, "fsdp", scatter_dimension=0, tiled=False)
+    down_sum = lax.psum_scatter(down_term, "fsdp", scatter_dimension=0, tiled=False)
+    attn_own = lax.dynamic_slice_in_dim(attn_rows, me * span, span, 1).reshape(own_rows, width)
+    output_term = matmul_tn(attn_own, grad_mid_half).astype(bf16)
+    output_term = output_term.reshape(size, groups, shard, width).transpose(1, 0, 2, 3)
+    output_term = lax.psum_scatter(output_term, "seq", scatter_dimension=0, tiled=False)
+    output_sum = lax.psum_scatter(output_term, "fsdp", scatter_dimension=0, tiled=False)
+    out_stages = reduce_stages(out_even, out_odd, grad_heads)
+    gate_up_home = spread(gate_up_sum)
 
     totals_row = jnp.stack([totals[:, :, 0], totals[:, :, HD]], axis=1)
     totals_row = jnp.concatenate([totals_row, jnp.zeros((seqs, 6, length), f32)], axis=1)
     starts_row = jnp.broadcast_to(starts[:, None, :], (seqs, 8, length))
     grad_q, grad_kv = attn_bwd(
-        q_rows, kv_rows, grad_heads, outputs, totals_row, starts_row, span, [gate_up_term, out_stages[0]]
+        q_rows, kv_rows, grad_heads, outputs, totals_row, starts_row, span, [out_stages[0]]
     )
     gin_even, gin_odd, qkv_term, head_gains = qkv_bwd(
         at, grad_q, grad_kv, qkv_raw, normed_in, w_qkv, scales, cosine, sine,
-        [out_stages[1], out_stages[2]] + down_parts + gate_up_parts,
+        [*out_stages[1:], gate_up_home, down_sum]
     )
     in_stages = reduce_stages(gin_even, gin_odd)
     own_in = block_input.reshape(own_rows, width).astype(f32)
@@ -1225,32 +1256,36 @@
         .reshape(seqs, span, width)
     )
 
+    def two_terms(array):
+        high = array.astype(bf16)
+        low = (array - high.astype(f32)).astype(bf16)
+        return jnp.concatenate([high, low, jnp.zeros((14, array.shape[1]), bf16)], axis=0)
+
+    gain_rows = two_terms(head_gains[:2].reshape(1, 256))
+
+    def sent_rows(f):
+        block = after(block_rows(qkv_term, f, groups * shard), in_stages[0])
+        return jnp.concatenate([block, gain_rows], axis=0)
+
+    qkv_parts = line_parts(sent_rows)
+    qkv_sum = add_up(sent_rows(me_line), qkv_parts)
+    gain_rows = two_terms(qkv_sum[-16:-15] + qkv_sum[-15:-14])
+    qkv_sum = qkv_sum[:-16].astype(bf16).reshape(groups, shard, 4 * HD)
+    gain_rows = jnp.broadcast_to(gain_rows[None], (groups, *gain_rows.shape))
+    query_grad, key_grad, value_grad, gain_one_sum, head_gains = unpack_heads(
+        spread(jnp.concatenate([qkv_sum, gain_rows], axis=1)), query_weight, key_weight, value_weight
+    )
+    head_gains = (head_gains[0] + head_gains[1]).reshape(2, 128)
+
     residual_own = lax.dynamic_slice_in_dim(residual_mid, me * span, span, 1)
-    block_output = (residual_own + own_sum(out_even, out_stages)).astype(bf16)
-
-    down_grad = add_up(block_rows(down_term, me_line, part), down_parts)
-    gate_up_sum = add_up(block_rows(gate_up_term, me_line, groups * shard), gate_up_parts)
-    gate_up_sum = gate_up_sum.astype(bf16).reshape(2, groups, shard, hidden_cols).transpose(1, 0, 2, 3)
-    gate_grad, up_grad, gain_two_sum = unpack_columns(spread(gate_up_sum), gate_weight, up_weight, part)
-
-    attn_own = lax.dynamic_slice_in_dim(attn_rows, me * span, span, 1).reshape(own_rows, width)
-    output_term = matmul_tn(attn_own, grad_mid_half).astype(bf16)
-    output_term = reduce_seq(output_term.reshape(size, groups * shard, width), 1).astype(bf16)
-    output_grad = add_up(
-        lax.dynamic_index_in_dim(output_term, me_line, 0, keepdims=False),
-        line_parts(lambda f: lax.dynamic_index_in_dim(output_term, f, 0, keepdims=False)),
-    )
-
-    qkv_parts = line_parts(lambda f: block_rows(qkv_term, f, groups * shard))
-    qkv_sum = add_up(block_rows(qkv_term, me_line, groups * shard), qkv_parts).astype(bf16)
-    query_grad, key_grad, value_grad, gain_one_sum = unpack_heads(
-        spread(qkv_sum.reshape(groups, shard, 4 * HD)), query_weight, key_weight, value_weight
-    )
+    block_output = after(residual_own + own_sum(out_even, out_stages), qkv_parts[0]).astype(bf16)
+    down_grad = after(down_sum.astype(f32), qkv_parts[0]).reshape(part, width)
+    output_grad = after(output_sum.astype(f32), qkv_parts[0])
+    gate_grad, up_grad, gain_two_sum = unpack_columns(gate_up_home, gate_weight, up_weight, part, qkv_parts[0])
 
     gain_one_grad = gain_one_sum[:, 0] / attention_gain.astype(f32)
     gain_two_grad = gain_two_sum[:, 0] / feedforward_gain.astype(f32)
 
-    head_gains = sum_everywhere(head_gains)
     return (
         block_output,
         input_grad,

time: 630 us -> 506 us (0.80)
  waiting for transfers between devices: 232 us -> 163 us
  starting transfers between devices: 99.1 us -> 46.3 us
  blocking collectives: 0 us -> 17.7 us
  local copies, waits for them, and re-layouts: 51.2 us -> 37.1 us
  other arithmetic: 57.1 us -> 45.5 us
    ppermute x21 -> x6, waiting for transfers between devices: 131 us -> 29.7 us  [swap_line(): return lax.ppermute(array, 'fsdp', [(i, i ^ mask) for i in range(size)])]
    ppermute x21 -> x6, starting transfers between devices: 44.9 us -> 7.78 us  [swap_line(): return lax.ppermute(array, 'fsdp', [(i, i ^ mask) for i in range(size)])]
    ppermute x39 -> x33, waiting for transfers between devices: 73.2 us -> 94.9 us  [swap(): return lax.ppermute(array, 'seq', [(i, i ^ mask) for i in range(groups)])]
    all_to_all x0 -> x1, blocking collectives: none -> 17.7 us  [spread(): lax.all_to_all(blocks, 'seq', split_axis=0, concat_axis=0, tiled=True)]
    all_to_all x5 -> x3, waiting for transfers between devices: 21.2 us -> 38.1 us  [spread(): lax.all_to_all(blocks, 'seq', split_axis=0, concat_axis=0, tiled=True)]
    another operation x14 -> x2, other arithmetic: 13.6 us -> 0.76 us
    all_to_all x5 -> x3, starting transfers between devices: 19.2 us -> 10.5 us  [spread(): lax.all_to_all(blocks, 'seq', split_axis=0, concat_axis=0, tiled=True)]
    convert_element_type x9 -> x8, other arithmetic: 12.1 us -> 17.9 us  [the longest x3 13.9 us: sent(): (total if earlier is None else after(total, earlier)).astype(bf16)]
  transfers between devices with their start and end apart: 69 -> 49, of which waited for: 28 -> 20; matrix products, arithmetic and copies ran while one was open for 13% -> 12% of each run, Pallas kernels for 18% -> 20%
where the time goes in v3:
time: 506 us; the launch traced here: 501 us
  Pallas kernels  169 us (33%)
  waiting for transfers between devices  163 us (32%)
  starting transfers between devices  46.3 us (9%)
  other arithmetic  45.5 us (9%)
  local copies, waits for them, and re-layouts  37.1 us (7%)
  between operations  19.6 us (4%)
  blocking collectives  17.7 us (3%)
    ppermute x33, waiting for transfers between devices, swap(): return lax.ppermute(array, 'seq', [(i, i ^ mask) for i in range(groups)])  94.9 us
    pallas_call x1, Pallas kernels, ffn(): pl.pallas_call(functools.partial(ffn_kernel, hidden, padded), grid_spec=p...  55.2 us
    all_to_all x3, waiting for transfers between devices, spread(): lax.all_to_all(blocks, 'seq', split_axis=0, concat_axis=0, tiled=True)  38.1 us
    ppermute x6, waiting for transfers between devices, swap_line(): return lax.ppermute(array, 'fsdp', [(i, i ^ mask) for i in range(size)])  29.7 us
    ppermute x33, starting transfers between devices, swap(): return lax.ppermute(array, 'seq', [(i, i ^ mask) for i in range(groups)])  27.6 us
    pallas_call x1, Pallas kernels, attn_bwd(): pl.pallas_call(functools.partial(attn_bwd_kernel, block), grid=(seqs, len...  26.9 us
    pallas_call x2, Pallas kernels, product(): pl.pallas_call(functools.partial(product_kernel, cuts), grid=(rows // til...  26.5 us
    all_to_all x1, blocking collectives, spread(): lax.all_to_all(blocks, 'seq', split_axis=0, concat_axis=0, tiled=True)  17.7 us
  transfers between devices with their start and end apart: 49, of which 20 were waited for; matrix products, arithmetic and copies ran while one was open for 12% of the time, Pallas kernels for 20%

profile of v3, /device:TPU:0, one launch (start us, length us, event | category | flops | bytes accessed | tf_op | source)
XLA Modules:
  0.0 500.9 jit_solution(13142830602408624276)
XLA Ops:
  7.2 1.8 pad_maximum_fusion
  10.4 2.9 pack.1
  13.3 17.7 %all_to_all.20 = bf16[8,32,1536]{2,1,0:T(8,128)(2,1)S(1)} all-to-all(bf16[8,32,1536]{2,1,0:T(8,128)(2,1)} %pack.1), channel_id=1, replica_groups=mesh['fsdp'=4,'seq'=8] {'seq'}, dimensions={0} | all-to-all | bytes 1572864 | tf_op jit(solution)/shard_map/all_to_all | solution.py:224
  32.8 2.5 collective-permute-start.9
  35.4 14.9 %collective-permute-done.7 = bf16[8,32,384]{2,0,1:T(8,128)(2,1)S(1)} collective-permute-done((bf16[8,32,384]{2,0,1:T(8,128)(2,1)S(1)}, bf16[8,32,384]{2,0,1:T(8,128)(2,1)S(1)}, u32[]{:S(2)}, u32[]{:S(2)}) %collective-permute-start.7) | collective-permute-done | bytes 196640 | tf_op jit(solution)/shard_map/ppermute | solution.py:1081
  51.5 2.1 collective-permute-done.9.refs_11_
  54.8 9.5 %collective-permute-done.8.refs_10_ = bf16[8,32,384]{2,1,0:T(8,128)(2,1)S(1)} collective-permute-done((bf16[8,32,384]{2,1,0:T(8,128)(2,1)S(1)}, bf16[8,32,384]{2,1,0:T(8,128)(2,1)S(1)}, u32[]{:S(2)}, u32[]{:S(2)}) %collective-permute-start.8) | collective-permute-done | bytes 196640 | tf_op jit(solution)/shard_map/ppermute | solution.py:1081
  71.2 7.6 %multiply_sine_fusion = (f32[2,1536,128]{2,1,0:T(8,128)S(1)}, f32[2,1536,128]{2,1,0:T(8,128)}) fusion(f32[128]{0:T(128)S(1)} %mul.94, f32[2,1536]{1,0:T(2,128)} %get-tuple-element.127), kind=kLoop, calls=%fused_computation | loop fusion | flops 393216 | bytes 3158528 | tf_op jit(solution)/shard_map/sin | solution.py:1194
  78.8 7.0 %collective-permute-done.3.refs_4_ = bf16[2,192,1024]{2,1,0:T(8,128)(2,1)} collective-permute-done((bf16[2,192,1024]{2,1,0:T(8,128)(2,1)S(1)}, bf16[2,192,1024]{2,1,0:T(8,128)(2,1)}, u32[]{:S(2)}, u32[]{:S(2)}) %collective-permute-start.3) | collective-permute-done | bytes 786464 | tf_op jit(solution)/shard_map/ppermute | solution.py:129
  85.9 1.7 collective-permute-start.5
  91.0 13.7 %collective-permute-done.5.refs_6_ = bf16[2,192,1024]{2,1,0:T(8,128)(2,1)} collective-permute-done((bf16[2,192,1024]{2,1,0:T(8,128)(2,1)}, bf16[2,192,1024]{2,1,0:T(8,128)(2,1)}, u32[]{:S(2)}, u32[]{:S(2)}) %collective-permute-start.5) | collective-permute-done | bytes 786464 | tf_op jit(solution)/shard_map/ppermute | solution.py:129
  109.9 1.7 slice.237
  118.0 14.5 %qkv_fwd.1 = (bf16[2,1536,1024]{2,1,0:T(8,128)(2,1)}, bf16[2,1536,1024]{2,1,0:T(8,128)(2,1)}, f32[2,1536,256]{2,1,0:T(8,128)}, bf16[2,1536,128]{2,1,0:T(8,128)(2...) custom-call(s32[2]{0:T(128)S(1)} %pad_add_fusion.at_ref, bf16[2,192,1024]{2,1,0:T(8,128)(2,1)S(1)} %copy-done, ...), custom_call_target="tpu_custom_call" | custom-call | flops 12884901888 | bytes 18874368 | tf_op jit(solution)/shard_map/qkv_fwd/pallas_call | solution.py:527
  137.4 17.1 %attn_fwd.1 = (bf16[2,1536,128]{2,1,0:T(8,128)(2,1)}, f32[2,1536,128]{2,1,0:T(8,128)S(1)}) custom-call(bf16[2,1536,128]{2,1,0:T(8,128)(2,1)S(1)} %get-tuple-element.61.q_ref, bf16[2,1536,128]{2,1,0:T(8,128)(2,1)S(1)} %get-tuple-element.62.kv_ref, s32[2,1536,128]{2,1,0:T(8,128)} %broadcast_in_dim.50.start_ref, ...), custom_call_target="tpu_custom_call" | custom-call | flops 1207959552 | bytes 5505024 | tf_op jit(solution)/shard_map/attn_fwd/pallas_call | solution.py:308
  158.3 17.0 %collective-permute-done.15.refs_4_ = bf16[2,1536,128]{2,1,0:T(8,128)(2,1)} collective-permute-done((bf16[2,1536,128]{2,1,0:T(8,128)(2,1)}, bf16[2,1536,128]{2,1,0:T(8,128)(2,1)}, u32[]{:S(2)}, u32[]{:S(2)}) %collective-permute-start.15) | collective-permute-done | bytes 786464 | tf_op jit(solution)/shard_map/ppermute | solution.py:129
  176.8 13.7 %collective-permute-done.22.refs_14_ = bf16[2,192,1024]{2,1,0:T(8,128)(2,1)} collective-permute-done((bf16[2,192,1024]{2,1,0:T(8,128)(2,1)S(1)}, bf16[2,192,1024]{2,1,0:T(8,128)(2,1)}, u32[]{:S(2)}, u32[]{:S(2)}) %collective-permute-start.22) | collective-permute-done | bytes 786464 | tf_op jit(solution)/shard_map/ppermute | solution.py:129
  191.9 1.8 collective-permute-done.17.refs_6_
  196.6 55.2 %ffn.1 = (bf16[2,1536,1024]{2,1,0:T(8,128)(2,1)}, f32[2,1536,1024]{2,1,0:T(8,128)}, bf16[2,1536,1024]{2,1,0:T(8,128)(2,1)}, bf16[2,1536,640]{2,1,0:T(8,128)(2,1)...) custom-call(s32[2]{0:T(128)} %copy-done.13, ...), custom_call_target="tpu_custom_call" | custom-call | flops 30601641984 | bytes 62914560 | tf_op jit(solution)/shard_map/ffn/pallas_call | solution.py:643
  251.8 16.0 %product.2.refs_1_.refs_4_ = bf16[4,8,2,32,576]{4,3,2,1,0:T(8,128)(2,1)} custom-call(bf16[3072,1024]{1,0:T(8,128)(2,1)} %bitcast.137, bf16[3072,1280]{1,0:T(8,128)(2,1)} %bitcast.136), custom_call_target="tpu_custom_call" | custom-call | flops 8053063680 | bytes 14155776 | tf_op jit(solution)/shard_map/product/pallas_call | solution.py:699
  268.4 8.4 %collective-permute-done.25.refs_0_.got_ref = bf16[4,2,192,1024]{3,2,1,0:T(8,128)(2,1)S(1)} collective-permute-done((bf16[4,2,192,1024]{3,2,1,0:T(8,128)(2,1)}, bf16[4,2,192,1024]{3,2,1,0:T(8,128)(2,1)S(1)}, u32[]{:S(2)}, u32[]{:S(2)}) %collective-permute-start.25) | collective-permute-done | bytes 3145760 | tf_op jit(solution)/shard_map/ppermute | solution.py:129
  276.9 4.9 fusion.14
  281.8 2.1 collective-permute-start.28
  285.3 10.5 %product.3.refs_3_ = bf16[4,1,1,144,1024]{4,3,2,1,0:T(8,128)(2,1)} custom-call(bf16[3072,640]{1,0:T(8,128)(2,1)} %bitcast.116, bf16[3072,1024]{1,0:T(8,128)(2,1)} %bitcast.115, bf16[4,2,192,1024]{3,2,1,0:T(8,128)(2,1)} %copy-done.27, bf16[4,8,2,32,576]{4,3,2,1,0:T(8,128)(2,1)} %product.2.refs_1_.refs_4_), custom_call_target="tpu_custom_call" | custom-call | flops 4026531840 | bytes 10223616 | tf_op jit(solution)/shard_map/product/pallas_call | solution.py:699
  295.8 7.7 %collective-permute-done.28.refs_2_ = bf16[2,192,1024]{2,1,0:T(8,128)(2,1)} collective-permute-done((bf16[2,192,1024]{2,1,0:T(8,128)(2,1)}, bf16[2,192,1024]{2,1,0:T(8,128)(2,1)}, u32[]{:S(2)}, u32[]{:S(2)}) %collective-permute-start.28) | collective-permute-done | bytes 786464 | tf_op jit(solution)/shard_map/ppermute | solution.py:129
  303.4 16.0 %collective-permute-done.27.refs_1_ = bf16[2,192,1024]{2,1,0:T(8,128)(2,1)} collective-permute-done((bf16[2,192,1024]{2,1,0:T(8,128)(2,1)}, bf16[2,192,1024]{2,1,0:T(8,128)(2,1)}, u32[]{:S(2)}, u32[]{:S(2)}) %collective-permute-start.27) | collective-permute-done | bytes 786464 | tf_op jit(solution)/shard_map/ppermute | solution.py:129
  321.0 5.0 mid_bwd.1
  329.0 3.5 all-to-all-start.1
  335.2 9.9 %all-to-all-done.1.do_ref = bf16[8,2,192,128]{3,2,1,0:T(8,128)(2,1)S(1)} async-done(((bf16[8,2,192,128]{3,2,1,0:T(8,128)(2,1)}), bf16[8,2,192,128]{3,2,1,0:T(8,128)(2,1)S(1)}, u32[]{:S(2)}, u32[]{:S(2)}) %all-to-all-start.1) | async-done | bytes 786464 | tf_op jit(solution)/shard_map/all_to_all | solution.py:224
  346.3 4.5 fusion.15
  355.0 2.1 constant_dynamic-slice_fusion
  357.1 3.5 all-to-all-start.2
  360.7 2.7 convolution_convert_fusion
  366.3 26.9 %attn_bwd.1 = (f32[2,1536,128]{2,1,0:T(8,128)}, f32[2,1536,128]{2,1,0:T(8,128)}) custom-call(bf16[2,1536,128]{2,1,0:T(8,128)(2,1)} %copy-done.23, bf16[2,1536,128]{2,1,0:T(8,128)(2,1)} %copy-done.24, bf16[8,2,192,128]{3,2,1,0:T(8,128)(2,1)} %copy-done.29, bf16[2,1536,128]{2,1,0:T(8,128)(2,1)} %get-tuple-element.63.refs_0_.o_ref, ...), custom_call_target="tpu_custom_call" | custom-call | flops 3019898880 | bytes 7864320 | tf_op jit(solution)/shard_map/attn_bwd/pallas_call | solution.py:375
  393.2 7.1 %all-to-all-done.2.refs_3_.home_ref = bf16[8,2,32,576]{3,2,1,0:T(8,128)(2,1)S(1)} async-done(((bf16[8,2,32,576]{3,2,1,0:T(8,128)(2,1)}), bf16[8,2,32,576]{3,2,1,0:T(8,128)(2,1)S(1)}, u32[]{:S(2)}, u32[]{:S(2)}) %all-to-all-start.2) | async-done | bytes 589856 | tf_op jit(solution)/shard_map/all_to_all | solution.py:224
  404.0 16.7 %qkv_bwd.1 = (bf16[4,2,192,1024]{3,2,1,0:T(8,128)(2,1)}, bf16[4,2,192,1024]{3,2,1,0:T(8,128)(2,1)}, bf16[1024,256]{1,0:T(8,128)(2,1)S(1)}, f32[8,128]{1,0:T(8,128)S(1)}) custom-call(s32[2]{0:T(128)S(1)} %copy-done.14, f32[2,1536,128]{2,1,0:T(8,128)S(1)} %copy-done.22, f32[2,1536,128]{2,1,0:T(8,128)} %get-tuple-element.78.dkv_ref, ...), custom_call_target="tpu_custom_call" | custom-call | flops 12884901888 | bytes 18874368 | tf_op jit(solution)/shard_map/qkv_bwd/pallas_call | solution.py:812
  422.0 4.8 collective-permute-done.32
  429.2 3.1 collective-permute-start.33
  432.3 4.5 fusion.18
  436.8 1.7 collective-permute-start.34
  440.0 3.2 collective-permute-done.37
  443.2 1.9 collective-permute-start.35
  447.1 3.4 all-to-all-start.3
  451.4 2.5 unpack.1
  454.7 3.9 fusion.11
  460.6 21.2 %all-to-all-done.3.home_ref = bf16[8,48,256]{2,1,0:T(8,128)(2,1)S(1)} async-done(((bf16[8,48,256]{2,1,0:T(8,128)(2,1)}), bf16[8,48,256]{2,1,0:T(8,128)(2,1)S(1)}, u32[]{:S(2)}, u32[]{:S(2)}) %all-to-all-start.3) | async-done | bytes 196640 | tf_op jit(solution)/shard_map/all_to_all | solution.py:224
  482.5 1.7 unpack_heads.1
  486.9 4.1 multiply_reduce_fusion
  491.1 2.7 fusion.4
  (241 shorter events, 72.8 us)
Async XLA Ops:
  7.2 102.7 %all-gather.7.cloned.1.call-start = ((), (), s32[]{:S(2)}) async-start(), calls=%async_computation.12 | async-start | bytes 1802240 | tf_op jit(solution)/shard_map/all_gather | solution.py:1177
  9.0 186.4 %all-gather.11.cloned.1.call-start = ((), (), s32[]{:S(2)}) async-start(), calls=%async_computation.14 | async-start | bytes 2949120 | tf_op jit(solution)/shard_map/all_gather | solution.py:1184
  31.2 19.2 %collective-permute-start.7 = (bf16[8,32,384]{2,0,1:T(8,128)(2,1)S(1)}, bf16[8,32,384]{2,0,1:T(8,128)(2,1)S(1)}, u32[]{:S(2)}, u32[]{:S(2)}) collective-permute-start(bf16[8,32,384]{2,0,1:T(8,128)(2,1)S(1)} %copy.112), channel_id=1, source_target_pairs={{0,8},{8,0},{16,24},{24,16},{1,9},{9,1},{17,25},{25,17},{2,10},{10... | collective-permute-start | bytes 589832 | tf_op jit(solution)/shard_map/ppermute | solution.py:1081
  32.8 20.8 %collective-permute-start.9 = (bf16[8,32,384]{2,1,0:T(8,128)(2,1)S(1)}, bf16[8,32,384]{2,1,0:T(8,128)(2,1)S(1)}, u32[]{:S(2)}, u32[]{:S(2)}) collective-permute-start(bf16[8,32,384]{2,1,0:T(8,128)(2,1)S(1)} %slice.230.refs_8_), channel_id=1, source_target_pairs={{0,24},{8,16},{16,8},{24,0},{1,25},{9,17},{17,9},{25,1},{2,26},{10... | collective-permute-start | bytes 589832 | tf_op jit(solution)/shard_map/ppermute | solution.py:1081
  35.3 29.0 %collective-permute-start.8 = (bf16[8,32,384]{2,1,0:T(8,128)(2,1)S(1)}, bf16[8,32,384]{2,1,0:T(8,128)(2,1)S(1)}, u32[]{:S(2)}, u32[]{:S(2)}) collective-permute-start(bf16[8,32,384]{2,1,0:T(8,128)(2,1)S(1)} %slice.230.refs_8_), channel_id=1, source_target_pairs={{0,16},{8,24},{16,0},{24,8},{1,17},{9,25},{17,1},{25,9},{2,18},{10... | collective-permute-start | bytes 589832 | tf_op jit(solution)/shard_map/ppermute | solution.py:1081
  66.5 130.1 %all-gather.9.cloned.1.call-start = ((), (), s32[]{:S(2)}) async-start(), calls=%async_computation.13 | async-start | bytes 2359296 | tf_op jit(solution)/shard_map/all_gather | solution.py:1180
  66.5 19.3 %collective-permute-start.3 = (bf16[2,192,1024]{2,1,0:T(8,128)(2,1)S(1)}, bf16[2,192,1024]{2,1,0:T(8,128)(2,1)}, u32[]{:S(2)}, u32[]{:S(2)}) collective-permute-start(bf16[2,192,1024]{2,1,0:T(8,128)(2,1)S(1)} %copy-done), channel_id=1, source_target_pairs={{0,4},{1,5},{2,6},{3,7},{4,0},{5,1},{6,2},{7,3},{8,12},{9,13},{10,... | collective-permute-start | bytes 2359304 | tf_op jit(solution)/shard_map/ppermute | solution.py:129
  68.1 20.3 %collective-permute-start.1 = (bf16[2,192,1024]{2,1,0:T(8,128)(2,1)S(1)}, bf16[2,192,1024]{2,1,0:T(8,128)(2,1)}, u32[]{:S(2)}, u32[]{:S(2)}) collective-permute-start(bf16[2,192,1024]{2,1,0:T(8,128)(2,1)S(1)} %copy-done), channel_id=1, source_target_pairs={{0,2},{1,3},{2,0},{3,1},{4,6},{5,7},{6,4},{7,5},{8,10},{9,11},{10,... | collective-permute-start | bytes 2359304 | tf_op jit(solution)/shard_map/ppermute | solution.py:129
  69.5 42.3 %collective-permute-start = (bf16[2,192,1024]{2,1,0:T(8,128)(2,1)S(1)}, bf16[2,192,1024]{2,1,0:T(8,128)(2,1)}, u32[]{:S(2)}, u32[]{:S(2)}) collective-permute-start(bf16[2,192,1024]{2,1,0:T(8,128)(2,1)S(1)} %copy-done), channel_id=1, source_target_pairs={{0,1},{1,0},{2,3},{3,2},{4,5},{5,4},{6,7},{7,6},{8,9},{9,8},{10,11... | collective-permute-start | bytes 2359304 | tf_op jit(solution)/shard_map/ppermute | solution.py:129
  69.5 87.2 %collective-permute-start.19 = (bf16[2,192,1024]{2,1,0:T(8,128)(2,1)S(1)}, bf16[2,192,1024]{2,1,0:T(8,128)(2,1)}, u32[]{:S(2)}, u32[]{:S(2)}) collective-permute-start(bf16[2,192,1024]{2,1,0:T(8,128)(2,1)S(1)} %copy-done.1), channel_id=1, source_target_pairs={{0,1},{1,0},{2,3},{3,2},{4,5},{5,4},{6,7},{7,6},{8,9},{9,8},{10,11... | collective-permute-start | bytes 2359304 | tf_op jit(solution)/shard_map/ppermute | solution.py:129
  85.9 18.9 %collective-permute-start.5 = (bf16[2,192,1024]{2,1,0:T(8,128)(2,1)}, bf16[2,192,1024]{2,1,0:T(8,128)(2,1)}, u32[]{:S(2)}, u32[]{:S(2)}) collective-permute-start(bf16[2,192,1024]{2,1,0:T(8,128)(2,1)} %collective-permute-done.3.refs_4_), channel_id=1, source_target_pairs={{0,2},{1,3},{2,0},{3,1},{4,6},{5,7},{6,4},{7,5},{8,10},{9,11},{10,... | collective-permute-start | bytes 2359304 | tf_op jit(solution)/shard_map/ppermute | solution.py:129
  88.4 24.9 %collective-permute-start.4 = (bf16[2,192,1024]{2,1,0:T(8,128)(2,1)}, bf16[2,192,1024]{2,1,0:T(8,128)(2,1)}, u32[]{:S(2)}, u32[]{:S(2)}) collective-permute-start(bf16[2,192,1024]{2,1,0:T(8,128)(2,1)} %collective-permute-done.3.refs_4_), channel_id=1, source_target_pairs={{0,1},{1,0},{2,3},{3,2},{4,5},{5,4},{6,7},{7,6},{8,9},{9,8},{10,11... | collective-permute-start | bytes 2359304 | tf_op jit(solution)/shard_map/ppermute | solution.py:129
  88.4 26.4 %collective-permute-start.2 = (bf16[2,192,1024]{2,1,0:T(8,128)(2,1)}, bf16[2,192,1024]{2,1,0:T(8,128)(2,1)}, u32[]{:S(2)}, u32[]{:S(2)}) collective-permute-start(bf16[2,192,1024]{2,1,0:T(8,128)(2,1)} %collective-permute-done.1.refs_2_), channel_id=1, source_target_pairs={{0,1},{1,0},{2,3},{3,2},{4,5},{5,4},{6,7},{7,6},{8,9},{9,8},{10,11... | collective-permute-start | bytes 2359304 | tf_op jit(solution)/shard_map/ppermute | solution.py:129
  104.7 10.0 %collective-permute-start.6 = (bf16[2,192,1024]{2,1,0:T(8,128)(2,1)}, bf16[2,192,1024]{2,1,0:T(8,128)(2,1)}, u32[]{:S(2)}, u32[]{:S(2)}) collective-permute-start(bf16[2,192,1024]{2,1,0:T(8,128)(2,1)} %collective-permute-done.5.refs_6_), channel_id=1, source_target_pairs={{0,1},{1,0},{2,3},{3,2},{4,5},{5,4},{6,7},{7,6},{8,9},{9,8},{10,11... | collective-permute-start | bytes 2359304 | tf_op jit(solution)/shard_map/ppermute | solution.py:129
  111.6 245.6 %reduce-scatter.5.cloned.1.call-start = ((), (), s32[]{:S(2)}) async-start(), calls=%async_computation.8 | async-start | bytes 3276800 | tf_op jit(solution)/shard_map/reduce_scatter | solution.py:1230
  111.9 23.0 %collective-permute-start.11 = (bf16[2,192,1024]{2,1,0:T(8,128)(2,1)}, bf16[2,192,1024]{2,1,0:T(8,128)(2,1)S(1)}, u32[]{:S(2)}, u32[]{:S(2)}) collective-permute-start(bf16[2,192,1024]{2,1,0:T(8,128)(2,1)} %broadcast_add_fusion), channel_id=1, source_target_pairs={{0,4},{1,5},{2,6},{3,7},{4,0},{5,1},{6,2},{7,3},{8,12},{9,13},{10,... | collective-permute-start | bytes 2359304 | tf_op jit(solution)/shard_map/ppermute | solution.py:129
  113.3 22.7 %collective-permute-start.10 = (bf16[2,192,1024]{2,1,0:T(8,128)(2,1)}, bf16[2,192,1024]{2,1,0:T(8,128)(2,1)S(1)}, u32[]{:S(2)}, u32[]{:S(2)}) collective-permute-start(bf16[2,192,1024]{2,1,0:T(8,128)(2,1)} %broadcast_add_fusion), channel_id=1, source_target_pairs={{0,2},{1,3},{2,0},{3,1},{4,6},{5,7},{6,4},{7,5},{8,10},{9,11},{10,... | collective-permute-start | bytes 2359304 | tf_op jit(solution)/shard_map/ppermute | solution.py:129
  154.5 20.8 %collective-permute-start.15 = (bf16[2,1536,128]{2,1,0:T(8,128)(2,1)}, bf16[2,1536,128]{2,1,0:T(8,128)(2,1)}, u32[]{:S(2)}, u32[]{:S(2)}) collective-permute-start(bf16[2,1536,128]{2,1,0:T(8,128)(2,1)} %get-tuple-element.63.refs_0_.o_ref), channel_id=1, source_target_pairs={{0,4},{1,5},{2,6},{3,7},{4,0},{5,1},{6,2},{7,3},{8,12},{9,13},{10,... | collective-permute-start | bytes 2359304 | tf_op jit(solution)/shard_map/ppermute | solution.py:129
  155.2 21.6 %collective-permute-start.21 = (bf16[2,192,1024]{2,1,0:T(8,128)(2,1)S(1)}, bf16[2,192,1024]{2,1,0:T(8,128)(2,1)S(1)}, u32[]{:S(2)}, u32[]{:S(2)}) collective-permute-start(bf16[2,192,1024]{2,1,0:T(8,128)(2,1)S(1)} %collective-permute-done.11.refs_1_.refs_12_), channel_id=1, source_target_pairs={{0,1},{1,0},{2,3},{3,2},{4,5},{5,4},{6,7},{7,6},{8,9},{9,8},{10,11... | collective-permute-start | bytes 2359304 | tf_op jit(solution)/shard_map/ppermute | solution.py:129
  155.2 35.3 %collective-permute-start.22 = (bf16[2,192,1024]{2,1,0:T(8,128)(2,1)S(1)}, bf16[2,192,1024]{2,1,0:T(8,128)(2,1)}, u32[]{:S(2)}, u32[]{:S(2)}) collective-permute-start(bf16[2,192,1024]{2,1,0:T(8,128)(2,1)S(1)} %collective-permute-done.10.refs_0_.refs_10_), channel_id=1, source_target_pairs={{0,4},{1,5},{2,6},{3,7},{4,0},{5,1},{6,2},{7,3},{8,12},{9,13},{10,... | collective-permute-start | bytes 2359304 | tf_op jit(solution)/shard_map/ppermute | solution.py:129
  156.6 34.0 %collective-permute-start.20 = (bf16[2,192,1024]{2,1,0:T(8,128)(2,1)S(1)}, bf16[2,192,1024]{2,1,0:T(8,128)(2,1)S(1)}, u32[]{:S(2)}, u32[]{:S(2)}) collective-permute-start(bf16[2,192,1024]{2,1,0:T(8,128)(2,1)S(1)} %collective-permute-done.10.refs_0_.refs_10_), channel_id=1, source_target_pairs={{0,1},{1,0},{2,3},{3,2},{4,5},{5,4},{6,7},{7,6},{8,9},{9,8},{10,11... | collective-permute-start | bytes 2359304 | tf_op jit(solution)/shard_map/ppermute | solution.py:129
  156.8 34.6 %collective-permute-start.13 = (bf16[2,1536,128]{2,1,0:T(8,128)(2,1)}, bf16[2,1536,128]{2,1,0:T(8,128)(2,1)S(1)}, u32[]{:S(2)}, u32[]{:S(2)}) collective-permute-start(bf16[2,1536,128]{2,1,0:T(8,128)(2,1)} %get-tuple-element.63.refs_0_.o_ref), channel_id=1, source_target_pairs={{0,2},{1,3},{2,0},{3,1},{4,6},{5,7},{6,4},{7,5},{8,10},{9,11},{10,... | collective-permute-start | bytes 2359304 | tf_op jit(solution)/shard_map/ppermute | solution.py:129
  175.3 18.4 %collective-permute-start.17 = (bf16[2,1536,128]{2,1,0:T(8,128)(2,1)}, bf16[2,1536,128]{2,1,0:T(8,128)(2,1)}, u32[]{:S(2)}, u32[]{:S(2)}) collective-permute-start(bf16[2,1536,128]{2,1,0:T(8,128)(2,1)} %collective-permute-done.15.refs_4_), channel_id=1, source_target_pairs={{0,2},{1,3},{2,0},{3,1},{4,6},{5,7},{6,4},{7,5},{8,10},{9,11},{10,... | collective-permute-start | bytes 2359304 | tf_op jit(solution)/shard_map/ppermute | solution.py:129
  176.8 17.5 %collective-permute-start.12 = (bf16[2,1536,128]{2,1,0:T(8,128)(2,1)}, bf16[2,1536,128]{2,1,0:T(8,128)(2,1)}, u32[]{:S(2)}, u32[]{:S(2)}) collective-permute-start(bf16[2,1536,128]{2,1,0:T(8,128)(2,1)} %get-tuple-element.63.refs_0_.o_ref), channel_id=1, source_target_pairs={{0,1},{1,0},{2,3},{3,2},{4,5},{5,4},{6,7},{7,6},{8,9},{9,8},{10,11... | collective-permute-start | bytes 2359304 | tf_op jit(solution)/shard_map/ppermute | solution.py:129
  190.5 4.9 collective-permute-start.16
  190.6 4.9 collective-permute-start.23
  191.4 4.0 collective-permute-start.14
  267.8 132.6 %reduce-scatter.7.cloned.1.call-start = ((), (), s32[]{:S(2)}) async-start(), calls=%async_computation.9 | async-start | bytes 1474560 | tf_op jit(solution)/shard_map/reduce_scatter | solution.py:1231
  267.9 9.0 %collective-permute-start.25 = (bf16[4,2,192,1024]{3,2,1,0:T(8,128)(2,1)}, bf16[4,2,192,1024]{3,2,1,0:T(8,128)(2,1)S(1)}, u32[]{:S(2)}, u32[]{:S(2)}) collective-permute-start(bf16[4,2,192,1024]{3,2,1,0:T(8,128)(2,1)} %get-tuple-element.70), channel_id=1, source_target_pairs={{0,1},{1,0},{2,3},{3,2},{4,5},{5,4},{6,7},{7,6},{8,9},{9,8},{10,11... | collective-permute-start | bytes 9437192 | tf_op jit(solution)/shard_map/ppermute | solution.py:129
  268.1 78.2 %collective-permute-start.24 = (bf16[4,2,192,1024]{3,2,1,0:T(8,128)(2,1)}, bf16[4,2,192,1024]{3,2,1,0:T(8,128)(2,1)}, u32[]{:S(2)}, u32[]{:S(2)}) collective-permute-start(bf16[4,2,192,1024]{3,2,1,0:T(8,128)(2,1)} %get-tuple-element.67), channel_id=1, source_target_pairs={{0,1},{1,0},{2,3},{3,2},{4,5},{5,4},{6,7},{7,6},{8,9},{9,8},{10,11... | collective-permute-start | bytes 9437192 | tf_op jit(solution)/shard_map/ppermute | solution.py:129
  281.8 21.6 %collective-permute-start.28 = (bf16[2,192,1024]{2,1,0:T(8,128)(2,1)}, bf16[2,192,1024]{2,1,0:T(8,128)(2,1)}, u32[]{:S(2)}, u32[]{:S(2)}) collective-permute-start(bf16[2,192,1024]{2,1,0:T(8,128)(2,1)} %get-tuple-element.108), channel_id=1, source_target_pairs={{0,6},{1,7},{2,4},{3,5},{4,2},{5,3},{6,0},{7,1},{8,14},{9,15},{10,... | collective-permute-start | bytes 2359304 | tf_op jit(solution)/shard_map/ppermute | solution.py:129
  283.8 35.6 %collective-permute-start.27 = (bf16[2,192,1024]{2,1,0:T(8,128)(2,1)}, bf16[2,192,1024]{2,1,0:T(8,128)(2,1)}, u32[]{:S(2)}, u32[]{:S(2)}) collective-permute-start(bf16[2,192,1024]{2,1,0:T(8,128)(2,1)} %get-tuple-element.109), channel_id=1, source_target_pairs={{0,4},{1,5},{2,6},{3,7},{4,0},{5,1},{6,2},{7,3},{8,12},{9,13},{10,... | collective-permute-start | bytes 2359304 | tf_op jit(solution)/shard_map/ppermute | solution.py:129
  284.7 34.8 %collective-permute-start.26 = (bf16[2,192,1024]{2,1,0:T(8,128)(2,1)}, bf16[2,192,1024]{2,1,0:T(8,128)(2,1)}, u32[]{:S(2)}, u32[]{:S(2)}) collective-permute-start(bf16[2,192,1024]{2,1,0:T(8,128)(2,1)} %get-tuple-element.110), channel_id=1, source_target_pairs={{0,2},{1,3},{2,0},{3,1},{4,6},{5,7},{6,4},{7,5},{8,10},{9,11},{10,... | collective-permute-start | bytes 2359304 | tf_op jit(solution)/shard_map/ppermute | solution.py:129
  329.0 16.1 %all-to-all-start.1 = ((bf16[8,2,192,128]{3,2,1,0:T(8,128)(2,1)}), bf16[8,2,192,128]{3,2,1,0:T(8,128)(2,1)S(1)}, u32[]{:S(2)}, u32[]{:S(2)}) async-start(bf16[8,2,192,128]{3,2,1,0:T(8,128)(2,1)} %copy-done.9), calls=%async_computation.1 | async-start | bytes 1572864 | tf_op jit(solution)/shard_map/all_to_all | solution.py:224
  350.8 49.5 %collective-permute-start.29 = (bf16[2,192,1024]{2,1,0:T(8,128)(2,1)}, bf16[2,192,1024]{2,1,0:T(8,128)(2,1)S(1)}, u32[]{:S(2)}, u32[]{:S(2)}) collective-permute-start(bf16[2,192,1024]{2,1,0:T(8,128)(2,1)} %get-tuple-element.105), channel_id=1, source_target_pairs={{0,2},{1,3},{2,0},{3,1},{4,6},{5,7},{6,4},{7,5},{8,10},{9,11},{10,... | collective-permute-start | bytes 2359304 | tf_op jit(solution)/shard_map/ppermute | solution.py:129
  351.3 49.1 %collective-permute-start.31 = (bf16[2,192,1024]{2,1,0:T(8,128)(2,1)}, bf16[2,192,1024]{2,1,0:T(8,128)(2,1)S(1)}, u32[]{:S(2)}, u32[]{:S(2)}) collective-permute-start(bf16[2,192,1024]{2,1,0:T(8,128)(2,1)} %get-tuple-element.106), channel_id=1, source_target_pairs={{0,6},{1,7},{2,4},{3,5},{4,2},{5,3},{6,0},{7,1},{8,14},{9,15},{10,... | collective-permute-start | bytes 2359304 | tf_op jit(solution)/shard_map/ppermute | solution.py:129
  352.8 47.6 %collective-permute-start.30 = (bf16[2,192,1024]{2,1,0:T(8,128)(2,1)}, bf16[2,192,1024]{2,1,0:T(8,128)(2,1)}, u32[]{:S(2)}, u32[]{:S(2)}) collective-permute-start(bf16[2,192,1024]{2,1,0:T(8,128)(2,1)} %get-tuple-element.107), channel_id=1, source_target_pairs={{0,4},{1,5},{2,6},{3,7},{4,0},{5,1},{6,2},{7,3},{8,12},{9,13},{10,... | collective-permute-start | bytes 2359304 | tf_op jit(solution)/shard_map/ppermute | solution.py:129
  357.1 43.2 %all-to-all-start.2 = ((bf16[8,2,32,576]{3,2,1,0:T(8,128)(2,1)}), bf16[8,2,32,576]{3,2,1,0:T(8,128)(2,1)S(1)}, u32[]{:S(2)}, u32[]{:S(2)}) async-start(bf16[8,2,32,576]{3,2,1,0:T(8,128)(2,1)} %bitcast.120), calls=%async_computation.3 | async-start | bytes 1310720 | tf_op jit(solution)/shard_map/all_to_all | solution.py:224
  360.7 61.2 %reduce-scatter.9.cloned.1.call-start = ((), (), s32[]{:S(2)}) async-start(), calls=%async_computation.10 | async-start | bytes 2359296 | tf_op jit(solution)/shard_map/reduce_scatter | solution.py:1235
  365.0 93.7 %reduce-scatter.11.cloned.1.call-start = ((), (), s32[]{:S(2)}) async-start(), calls=%async_computation.11 | async-start | bytes 327680 | tf_op jit(solution)/shard_map/reduce_scatter | solution.py:1236
  420.7 6.0 %collective-permute-start.32 = (bf16[4,2,192,1024]{3,2,1,0:T(8,128)(2,1)}, bf16[4,2,192,1024]{3,2,1,0:T(8,128)(2,1)}, u32[]{:S(2)}, u32[]{:S(2)}) collective-permute-start(bf16[4,2,192,1024]{3,2,1,0:T(8,128)(2,1)} %get-tuple-element.83), channel_id=1, source_target_pairs={{0,1},{1,0},{2,3},{3,2},{4,5},{5,4},{6,7},{7,6},{8,9},{9,8},{10,11... | collective-permute-start | bytes 9437192 | tf_op jit(solution)/shard_map/ppermute | solution.py:129
  428.8 14.4 %collective-permute-start.37 = (bf16[272,256]{1,0:T(8,128)(2,1)S(1)}, bf16[272,256]{1,0:T(8,128)(2,1)S(1)}, u32[]{:S(2)}, u32[]{:S(2)}) collective-permute-start(bf16[272,256]{1,0:T(8,128)(2,1)S(1)} %get-tuple-element.128), channel_id=1, source_target_pairs={{0,16},{8,24},{16,0},{24,8},{1,17},{9,25},{17,1},{25,9},{2,18},{10... | collective-permute-start | bytes 417800 | tf_op jit(solution)/shard_map/ppermute | solution.py:1081
  428.8 16.2 %collective-permute-start.38 = (bf16[272,256]{1,0:T(8,128)(2,1)S(1)}, bf16[272,256]{1,0:T(8,128)(2,1)S(1)}, u32[]{:S(2)}, u32[]{:S(2)}) collective-permute-start(bf16[272,256]{1,0:T(8,128)(2,1)S(1)} %get-tuple-element.129), channel_id=1, source_target_pairs={{0,24},{8,16},{16,8},{24,0},{1,25},{9,17},{17,9},{25,1},{2,26},{10... | collective-permute-start | bytes 417800 | tf_op jit(solution)/shard_map/ppermute | solution.py:1081
  429.2 15.9 %collective-permute-start.33 = (bf16[272,256]{1,0:T(8,128)(2,1)S(1)}, bf16[272,256]{1,0:T(8,128)(2,1)S(1)}, u32[]{:S(2)}, u32[]{:S(2)}) collective-permute-start(bf16[272,256]{1,0:T(8,128)(2,1)S(1)} %get-tuple-element.130), channel_id=1, source_target_pairs={{0,8},{8,0},{16,24},{24,16},{1,9},{9,1},{17,25},{25,17},{2,10},{10... | collective-permute-start | bytes 417800 | tf_op jit(solution)/shard_map/ppermute | solution.py:1081
  436.8 50.1 %collective-permute-start.34 = (bf16[2,192,1024]{2,1,0:T(8,128)(2,1)}, bf16[2,192,1024]{2,1,0:T(8,128)(2,1)}, u32[]{:S(2)}, u32[]{:S(2)}) collective-permute-start(bf16[2,192,1024]{2,1,0:T(8,128)(2,1)} %get-tuple-element.102), channel_id=1, source_target_pairs={{0,2},{1,3},{2,0},{3,1},{4,6},{5,7},{6,4},{7,5},{8,10},{9,11},{10,... | collective-permute-start | bytes 2359304 | tf_op jit(solution)/shard_map/ppermute | solution.py:129
  438.5 48.4 %collective-permute-start.36 = (bf16[2,192,1024]{2,1,0:T(8,128)(2,1)}, bf16[2,192,1024]{2,1,0:T(8,128)(2,1)}, u32[]{:S(2)}, u32[]{:S(2)}) collective-permute-start(bf16[2,192,1024]{2,1,0:T(8,128)(2,1)} %get-tuple-element.103), channel_id=1, source_target_pairs={{0,6},{1,7},{2,4},{3,5},{4,2},{5,3},{6,0},{7,1},{8,14},{9,15},{10,... | collective-permute-start | bytes 2359304 | tf_op jit(solution)/shard_map/ppermute | solution.py:129
  443.2 43.7 %collective-permute-start.35 = (bf16[2,192,1024]{2,1,0:T(8,128)(2,1)}, bf16[2,192,1024]{2,1,0:T(8,128)(2,1)}, u32[]{:S(2)}, u32[]{:S(2)}) collective-permute-start(bf16[2,192,1024]{2,1,0:T(8,128)(2,1)} %get-tuple-element.104), channel_id=1, source_target_pairs={{0,4},{1,5},{2,6},{3,7},{4,0},{5,1},{6,2},{7,3},{8,12},{9,13},{10,... | collective-permute-start | bytes 2359304 | tf_op jit(solution)/shard_map/ppermute | solution.py:129
  447.1 34.7 %all-to-all-start.3 = ((bf16[8,48,256]{2,1,0:T(8,128)(2,1)}), bf16[8,48,256]{2,1,0:T(8,128)(2,1)S(1)}, u32[]{:S(2)}, u32[]{:S(2)}) async-start(bf16[8,48,256]{2,1,0:T(8,128)(2,1)} %pad_maximum_fusion.13), calls=%async_computation.5 | async-start | bytes 393216 | tf_op jit(solution)/shard_map/all_to_all | solution.py:224
  (46 other events, 787.3 us)
Sparse Core Ops, SparseCore 0:
  10.2 51.7 all-gather.6
  66.6 49.4 all-gather.10
  118.5 29.4 all-gather.8
  267.9 50.0 reduce-scatter.4
  320.2 28.8 reduce-scatter.6
  365.1 46.0 reduce-scatter.8
  422.1 22.3 reduce-scatter.10

commit v4 on v3

--- a/solution.py
+++ b/solution.py
@@ -129,9 +129,9 @@
     return lax.ppermute(array, "seq", [(i, i ^ mask) for i in range(groups)])
 
 
-def partner_blocks(block):
+def partner_blocks(block, direct=False):
     got = {0: block, 2: swap(block, 2), 4: swap(block, 4)}
-    got[6] = swap(got[4], 2)
+    got[6] = swap(block, 6) if direct else swap(got[4], 2)
     for mask in (0, 2, 4, 6):
         got[mask + 1] = swap(got[mask], 1)
     return [got[j] for j in range(8)]
@@ -691,7 +691,7 @@
                     out_ref[f, g, i] = total[row : row + count, begin:end].astype(bf16)
 
 
-def product(left, right, split, cuts, earlier=()):
+def product(left, right, split, cuts, cost, earlier=()):
     rows = left.shape[0]
     shape = (split[0], split[1], len(cuts), split[2], cuts[0][1] - cuts[0][0])
     tile = 512
@@ -705,7 +705,7 @@
         out_shape=jax.ShapeDtypeStruct(shape, bf16),
         scratch_shapes=[pltpu.VMEM((left.shape[1], right.shape[1]), f32)],
         compiler_params=pltpu.CompilerParams(vmem_limit_bytes=48 << 20),
-        cost_estimate=pl.CostEstimate(flops=2 * rows * left.shape[1] * right.shape[1], bytes_accessed=2 * rows * (left.shape[1] + right.shape[1]), transcendentals=0),
+        cost_estimate=pl.CostEstimate(flops=cost, bytes_accessed=cost, transcendentals=0),
         name="product",
     )(left, right, *earlier)
 
@@ -1097,12 +1097,14 @@
     return total
 
 
-def reduce_stages(even, odd, earlier=None):
+def reduce_stages(even, odd, earlier=()):
     got = swap(odd, 1)
 
     def sent(i):
         total = even[i].astype(f32) + got[i].astype(f32)
-        return swap((total if earlier is None else after(total, earlier)).astype(bf16), 2 * i)
+        for array in earlier:
+            total = after(total, array)
+        return swap(total.astype(bf16), 2 * i)
 
     return got, sent(1), sent(2), sent(3)
 
@@ -1166,7 +1168,7 @@
     packed = spread(
         pack_columns(gate_weight, up_weight, query_weight, key_weight, value_weight, gains, groups, part)
     )
-    x_blocks = partner_blocks(block_input)
+    x_blocks = partner_blocks(block_input, direct=True)
     qkv_blocks = line_blocks(packed[:, :, 2 * hidden_cols :])
     gains = [block[:, 0, 256 : 256 + 2 * shard].astype(f32) for block in qkv_blocks]
     gains = jnp.stack(
@@ -1174,12 +1176,15 @@
     )
     gain_one = gains[:, :, :shard].reshape(1, width)
     gain_two = gains[:, :, shard:].reshape(1, width)
+    inverse = rope_base ** (-(jnp.arange(HD // 2, dtype=f32) * 2.0) / HD)
+    angles = positions.astype(f32)[:, :, None] * jnp.tile(inverse, 4)[None, None, :]
+    cosine, sine = jnp.cos(angles), jnp.sin(angles)
     down_parts = lax.all_gather(
         jnp.concatenate([down_weight, output_weight], axis=0), "fsdp", axis=0, tiled=False
     )
     wo_parts = lax.all_gather(down_parts[:, part:], "seq", axis=0, tiled=False)
     w_gate_up = packed[:, :, : 2 * hidden_cols]
-    for block in qkv_blocks[1:]:
+    for block in [*qkv_blocks[1:], x_blocks[2], x_blocks[4], x_blocks[6], cosine, sine]:
         w_gate_up = after(w_gate_up, block)
     w_gate_up = lax.all_gather(w_gate_up, "fsdp", axis=0, tiled=False).reshape(width, 2 * hidden_cols)
     cot_blocks = {0: cotangent}
@@ -1189,9 +1194,6 @@
     for mask in (0, 2, 4, 6):
         cot_blocks[mask + 1] = swap(cot_blocks[mask], 1)
 
-    inverse = rope_base ** (-(jnp.arange(HD // 2, dtype=f32) * 2.0) / HD)
-    angles = positions.astype(f32)[:, :, None] * jnp.tile(inverse, 4)[None, None, :]
-    cosine, sine = jnp.cos(angles), jnp.sin(angles)
     scales = jnp.concatenate(
         [jnp.tile(query_gain, 2)[None], jnp.tile(key_gain, 2)[None], jnp.zeros((6, 128), bf16)]
     ).astype(f32)
@@ -1216,13 +1218,16 @@
 
     mid_stages = reduce_stages(gnm_even, gnm_odd)
     cuts = ((0, hidden_cols), (padded, padded + hidden_cols))
-    gate_up_term = product(flat(normed_mid), flat(ff_grads), (size, groups, shard), cuts)
-    waits = [mid_stages[0], gate_up_term]
-    down_term = product(flat(hidden), flat(cot_full), (size, 1, part), ((0, width),), waits)
+    down_term = product(
+        flat(hidden), flat(cot_full), (size, 1, part), ((0, width),), 16 * rows * width
+    )
     grad_mid, grad_mid_half, grad_attn_out = mid_bwd(
-        at, residual_mid, cotangent, gain_two, w_out, gnm_even, mid_stages, [down_term, gate_up_term]
+        at, residual_mid, cotangent, gain_two, w_out, gnm_even, mid_stages, [down_term]
     )
     grad_heads = spread(grad_attn_out)
+    gate_up_term = product(
+        flat(normed_mid), flat(ff_grads), (size, groups, shard), cuts, 32 * rows * width, [grad_mid_half]
+    )
 
     def block_rows(term, f, count):
         return lax.dynamic_slice_in_dim(term, f * count, count, term.ndim - 2)
@@ -1234,18 +1239,18 @@
     output_term = output_term.reshape(size, groups, shard, width).transpose(1, 0, 2, 3)
     output_term = lax.psum_scatter(output_term, "seq", scatter_dimension=0, tiled=False)
     output_sum = lax.psum_scatter(output_term, "fsdp", scatter_dimension=0, tiled=False)
-    out_stages = reduce_stages(out_even, out_odd, grad_heads)
+    out_stages = reduce_stages(out_even, out_odd, [grad_heads, gate_up_term])
     gate_up_home = spread(gate_up_sum)
 
     totals_row = jnp.stack([totals[:, :, 0], totals[:, :, HD]], axis=1)
     totals_row = jnp.concatenate([totals_row, jnp.zeros((seqs, 6, length), f32)], axis=1)
     starts_row = jnp.broadcast_to(starts[:, None, :], (seqs, 8, length))
     grad_q, grad_kv = attn_bwd(
-        q_rows, kv_rows, grad_heads, outputs, totals_row, starts_row, span, [out_stages[0]]
+        q_rows, kv_rows, grad_heads, outputs, totals_row, starts_row, span, [out_stages[0], gate_up_term]
     )
     gin_even, gin_odd, qkv_term, head_gains = qkv_bwd(
         at, grad_q, grad_kv, qkv_raw, normed_in, w_qkv, scales, cosine, sine,
-        [*out_stages[1:], gate_up_home, down_sum]
+        [*out_stages[1:], down_sum]
     )
     in_stages = reduce_stages(gin_even, gin_odd)
     own_in = block_input.reshape(own_rows, width).astype(f32)

time: 506 us -> 487 us (0.962)
  waiting for transfers between devices: 163 us -> 145 us
  blocking collectives: 17.7 us -> 0 us
  starting transfers between devices: 46.3 us -> 52.2 us
    ppermute x33, waiting for transfers between devices: 94.9 us -> 76.8 us  [swap(): return lax.ppermute(array, 'seq', [(i, i ^ mask) for i in range(groups)])]
    all_to_all x1 -> x0, blocking collectives: 17.7 us -> none  [spread(): lax.all_to_all(blocks, 'seq', split_axis=0, concat_axis=0, tiled=True)]
    ppermute x6, waiting for transfers between devices: 29.7 us -> 12.2 us  [swap_line(): return lax.ppermute(array, 'fsdp', [(i, i ^ mask) for i in range(size)])]
    reduce_scatter x1, waiting for transfers between devices: 0.01 us -> 15.8 us  [body(): lax.psum_scatter(gate_up_term, 'fsdp', scatter_dimension=0, tiled=False)]
    reduce_scatter x1, waiting for transfers between devices: 0.02 us -> 11.6 us  [body(): lax.psum_scatter(down_term, 'fsdp', scatter_dimension=0, tiled=False)]
    all_to_all x3 -> x4, waiting for transfers between devices: 38.1 us -> 28.1 us  [spread(): lax.all_to_all(blocks, 'seq', split_axis=0, concat_axis=0, tiled=True)]
    add x5 -> x6, other arithmetic: 4.33 us -> 11.9 us  [after(): return array + jnp.minimum(jnp.abs(first), 0).astype(array.dtype)]
    convert_element_type x3 -> x2, other arithmetic: 13.9 us -> 9.37 us  [sent(): return swap(total.astype(bf16), 2 * i)]
  transfers between devices with their start and end apart: 49 -> 50, of which waited for: 20 -> 19; matrix products, arithmetic and copies ran while one was open for 12% -> 12% of each run, Pallas kernels for 20% -> 22%
where the time goes in v4:
time: 487 us; the launch traced here: 479 us
  Pallas kernels  168 us (34%)
  waiting for transfers between devices  145 us (30%)
  starting transfers between devices  52.2 us (11%)
  other arithmetic  47.9 us (10%)
  local copies, waits for them, and re-layouts  41.3 us (8%)
  between operations  23.1 us (5%)
    ppermute x33, waiting for transfers between devices, swap(): return lax.ppermute(array, 'seq', [(i, i ^ mask) for i in range(groups)])  76.8 us
    pallas_call x1, Pallas kernels, ffn(): pl.pallas_call(functools.partial(ffn_kernel, hidden, padded), grid_spec=p...  55.3 us
    ppermute x33, starting transfers between devices, swap(): return lax.ppermute(array, 'seq', [(i, i ^ mask) for i in range(groups)])  28.5 us
    all_to_all x4, waiting for transfers between devices, spread(): lax.all_to_all(blocks, 'seq', split_axis=0, concat_axis=0, tiled=True)  28.1 us
    pallas_call x1, Pallas kernels, attn_bwd(): pl.pallas_call(functools.partial(attn_bwd_kernel, block), grid=(seqs, len...  26.8 us
    pallas_call x2, Pallas kernels, product(): pl.pallas_call(functools.partial(product_kernel, cuts), grid=(rows // til...  25.7 us
    pallas_call x1, Pallas kernels, qkv_bwd(): pl.pallas_call(qkv_bwd_kernel, grid_spec=pltpu.PrefetchScalarGridSpec(num...  16.7 us
    pallas_call x1, Pallas kernels, attn_fwd(): pl.pallas_call(functools.partial(attn_fwd_kernel, block), grid=(seqs, len...  16.4 us
  transfers between devices with their start and end apart: 50, of which 19 were waited for; matrix products, arithmetic and copies ran while one was open for 12% of the time, Pallas kernels for 22%

profile of v4, /device:TPU:0, one launch (start us, length us, event | category | flops | bytes accessed | tf_op | source)
XLA Modules:
  0.0 478.9 jit_solution(505282896206979771)
XLA Ops:
  7.2 1.8 pad_maximum_fusion
  9.0 4.0 collective-permute-start.5
  14.3 2.9 pack.1
  17.2 3.6 all-to-all-start
  20.9 2.0 collective-permute-start.3
  25.0 15.0 %all-to-all-done = bf16[8,32,1536]{2,1,0:T(8,128)(2,1)S(1)} async-done(((bf16[8,32,1536]{2,1,0:T(8,128)(2,1)}), bf16[8,32,1536]{2,1,0:T(8,128)(2,1)S(1)}, u32[]{:S(2)}, u32[]{:S(2)}) %all-to-all-start) | async-done | bytes 786464 | tf_op jit(solution)/shard_map/all_to_all | solution.py:224
  40.1 4.2 collective-permute-start.9
  45.0 5.5 %multiply_sine_fusion = (f32[2,1536,128]{2,1,0:T(8,128)S(1)}, f32[2,1536,128]{2,1,0:T(8,128)S(1)}) fusion(f32[128]{0:T(128)S(1)} %mul.94, f32[2,1536]{1,0:T(2,128)S(1)} %get-tuple-element.127), kind=kLoop, calls=%fused_computation | loop fusion | flops 393216 | bytes 3158528 | tf_op jit(solution)/shard_map/sin | solution.py:1181
  62.3 2.0 collective-permute-done.8.refs_10_
  65.5 2.1 fusion.27
  75.5 1.7 slice.260
  83.7 14.5 %qkv_fwd.1 = (bf16[2,1536,1024]{2,1,0:T(8,128)(2,1)}, bf16[2,1536,1024]{2,1,0:T(8,128)(2,1)}, f32[2,1536,256]{2,1,0:T(8,128)}, bf16[2,1536,128]{2,1,0:T(8,128)(2...) custom-call(s32[2]{0:T(128)S(1)} %pad_add_fusion.at_ref, bf16[2,192,1024]{2,1,0:T(8,128)(2,1)S(1)} %copy-done.1, ...), custom_call_target="tpu_custom_call" | custom-call | flops 12884901888 | bytes 18874368 | tf_op jit(solution)/shard_map/qkv_fwd/pallas_call | solution.py:527
  98.8 1.8 broadcast_in_dim.50.start_ref
  100.5 16.4 %attn_fwd.1 = (bf16[2,1536,128]{2,1,0:T(8,128)(2,1)S(1)}, f32[2,1536,128]{2,1,0:T(8,128)S(1)}) custom-call(bf16[2,1536,128]{2,1,0:T(8,128)(2,1)S(1)} %get-tuple-element.61.q_ref, bf16[2,1536,128]{2,1,0:T(8,128)(2,1)S(1)} %get-tuple-element.62.kv_ref, s32[2,1536,128]{2,1,0:T(8,128)} %broadcast_in_dim.50.start_ref, ...), custom_call_target="tpu_custom_call" | custom-call | flops 1207959552 | bytes 5505024 | tf_op jit(solution)/shard_map/attn_fwd/pallas_call | solution.py:308
  121.6 19.9 %collective-permute-done.15.refs_4_ = bf16[2,1536,128]{2,1,0:T(8,128)(2,1)S(1)} collective-permute-done((bf16[2,1536,128]{2,1,0:T(8,128)(2,1)S(1)}, bf16[2,1536,128]{2,1,0:T(8,128)(2,1)S(1)}, u32[]{:S(2)}, u32[]{:S(2)}) %collective-permute-start.15) | collective-permute-done | bytes 786464 | tf_op jit(solution)/shard_map/ppermute | solution.py:129
  142.6 19.9 %collective-permute-done.22.refs_14_ = bf16[2,192,1024]{2,1,0:T(8,128)(2,1)} collective-permute-done((bf16[2,192,1024]{2,1,0:T(8,128)(2,1)S(1)}, bf16[2,192,1024]{2,1,0:T(8,128)(2,1)}, u32[]{:S(2)}, u32[]{:S(2)}) %collective-permute-start.22) | collective-permute-done | bytes 786464 | tf_op jit(solution)/shard_map/ppermute | solution.py:129
  163.1 2.4 collective-permute-done.17.refs_6_
  168.6 55.3 %ffn.1 = (bf16[2,1536,1024]{2,1,0:T(8,128)(2,1)}, f32[2,1536,1024]{2,1,0:T(8,128)}, bf16[2,1536,1024]{2,1,0:T(8,128)(2,1)}, bf16[2,1536,640]{2,1,0:T(8,128)(2,1)...) custom-call(s32[2]{0:T(128)} %copy-done.20, ...), custom_call_target="tpu_custom_call" | custom-call | flops 30601641984 | bytes 62914560 | tf_op jit(solution)/shard_map/ffn/pallas_call | solution.py:643
  224.1 5.7 %collective-permute-done.25.got_ref = bf16[4,2,192,1024]{3,2,1,0:T(8,128)(2,1)S(1)} collective-permute-done((bf16[4,2,192,1024]{3,2,1,0:T(8,128)(2,1)}, bf16[4,2,192,1024]{3,2,1,0:T(8,128)(2,1)S(1)}, u32[]{:S(2)}, u32[]{:S(2)}) %collective-permute-start.25) | collective-permute-done | bytes 3145760 | tf_op jit(solution)/shard_map/ppermute | solution.py:129
  229.9 4.9 %fusion.14 = (bf16[2,192,1024]{2,1,0:T(8,128)(2,1)}, bf16[2,192,1024]{2,1,0:T(8,128)(2,1)}, bf16[2,192,1024]{2,1,0:T(8,128)(2,1)}) fusion(bf16[4,2,192,1024]{3,2,1,0:T(8,128)(2,1)S(1)} %collective-permute-done.25.got_ref, bf16[4,2,192,1024]{3,2,1,0:T(8,128)(2,1)} %get-tuple-element.69.even_ref), kind=kLoop, calls=%fused_computation.33 | loop fusion | flops 4718592 | bytes 7077888 | tf_op jit(solution)/shard_map/convert_element_type | solution.py:1107
  238.2 2.1 copy-done.3
  240.3 9.5 %product.2.refs_3_ = bf16[4,1,1,144,1024]{4,3,2,1,0:T(8,128)(2,1)} custom-call(bf16[3072,640]{1,0:T(8,128)(2,1)S(1)} %bitcast.119, bf16[3072,1024]{1,0:T(8,128)(2,1)} %bitcast.124), custom_call_target="tpu_custom_call" | custom-call | flops 50331648 | bytes 50331648 | tf_op jit(solution)/shard_map/product/pallas_call | solution.py:699
  251.1 5.3 %collective-permute-done.28.refs_2_ = bf16[2,192,1024]{2,1,0:T(8,128)(2,1)} collective-permute-done((bf16[2,192,1024]{2,1,0:T(8,128)(2,1)}, bf16[2,192,1024]{2,1,0:T(8,128)(2,1)}, u32[]{:S(2)}, u32[]{:S(2)}) %collective-permute-start.28) | collective-permute-done | bytes 786464 | tf_op jit(solution)/shard_map/ppermute | solution.py:129
  256.4 16.0 %collective-permute-done.27.refs_1_ = bf16[2,192,1024]{2,1,0:T(8,128)(2,1)} collective-permute-done((bf16[2,192,1024]{2,1,0:T(8,128)(2,1)}, bf16[2,192,1024]{2,1,0:T(8,128)(2,1)}, u32[]{:S(2)}, u32[]{:S(2)}) %collective-permute-start.27) | collective-permute-done | bytes 786464 | tf_op jit(solution)/shard_map/ppermute | solution.py:129
  274.0 5.6 %mid_bwd.1 = (f32[384,1024]{1,0:T(8,128)S(1)}, bf16[384,1024]{1,0:T(8,128)(2,1)S(1)}, bf16[8,2,192,128]{3,2,1,0:T(8,128)(2,1)}) custom-call(s32[2]{0:T(128)S(1)} %copy-done.21, f32[2,1536,1024]{2,1,0:T(8,128)} %get-tuple-element.65.mid_ref, bf16[2,192,1024]{2,1,0:T(8,128)(2,1)S(1)} %copy-done.5, f32[1,1024]{1,0:T(1,128)S(1)} %copy-done.19, ...), custom_call_target="tpu_custom_call" | custom-call | flops 805306368 | bytes 7864320 | tf_op jit(solution)/shard_map/mid_bwd/pallas_call | solution.py:740
  283.3 3.6 all-to-all-start.1
  287.0 1.7 copy.109
  288.6 16.2 %product.3.refs_1_ = bf16[4,8,2,32,576]{4,3,2,1,0:T(8,128)(2,1)} custom-call(bf16[3072,1024]{1,0:T(8,128)(2,1)} %bitcast.123, bf16[3072,1280]{1,0:T(8,128)(2,1)} %bitcast.122, bf16[384,1024]{1,0:T(8,128)(2,1)S(1)} %copy-done.15), custom_call_target="tpu_custom_call" | custom-call | flops 100663296 | bytes 100663296 | tf_op jit(solution)/shard_map/product/pallas_call | solution.py:699
  307.9 4.6 fusion.15
  312.5 1.9 collective-permute-start.29
  318.4 26.8 %attn_bwd.1 = (f32[2,1536,128]{2,1,0:T(8,128)}, f32[2,1536,128]{2,1,0:T(8,128)}) custom-call(bf16[2,1536,128]{2,1,0:T(8,128)(2,1)} %copy-done.30, bf16[2,1536,128]{2,1,0:T(8,128)(2,1)} %copy-done.31, bf16[8,2,192,128]{3,2,1,0:T(8,128)(2,1)} %copy-done.37, bf16[2,1536,128]{2,1,0:T(8,128)(2,1)} %copy-done.26, f32[2,8,1536]{2,1,0:T(8,128)} %maximum_maximum_fusion.lse_ref, ...), custom_call_target="tpu_custom_call" | custom-call | flops 3019898880 | bytes 7864320 | tf_op jit(solution)/shard_map/attn_bwd/pallas_call | solution.py:375
  345.3 11.6 %reduce-scatter.5.cloned.1.call-done = bf16[1,1,1,144,1024]{4,3,2,1,0:T(8,128)(2,1)} async-done(((bf16[4,1,1,144,1024]{4,3,2,1,0:T(8,128)(2,1)}), bf16[1,1,1,144,1024]{4,3,2,1,0:T(8,128)(2,1)}) %reduce-scatter.5.cloned.1.call-update) | async-done | bytes 294928 | tf_op jit(solution)/shard_map/reduce_scatter | solution.py:1236
  359.3 16.7 %qkv_bwd.1 = (bf16[4,2,192,1024]{3,2,1,0:T(8,128)(2,1)}, bf16[4,2,192,1024]{3,2,1,0:T(8,128)(2,1)}, bf16[1024,256]{1,0:T(8,128)(2,1)S(1)}, f32[8,128]{1,0:T(8,128)S(1)}) custom-call(s32[2]{0:T(128)S(1)} %copy-done.21, f32[2,1536,128]{2,1,0:T(8,128)S(1)} %copy-done.29, f32[2,1536,128]{2,1,0:T(8,128)} %get-tuple-element.79.dkv_ref, ...), custom_call_target="tpu_custom_call" | custom-call | flops 12884901888 | bytes 18874368 | tf_op jit(solution)/shard_map/qkv_bwd/pallas_call | solution.py:812
  378.3 4.4 collective-permute-done.32
  384.6 1.9 dynamic-slice_add_fusion.2
  389.1 1.6 collective-permute-start.33
  390.7 4.5 fusion.18
  398.2 10.1 %collective-permute-done.33._ = bf16[272,256]{1,0:T(8,128)(2,1)S(1)} collective-permute-done((bf16[272,256]{1,0:T(8,128)(2,1)S(1)}, bf16[272,256]{1,0:T(8,128)(2,1)S(1)}, u32[]{:S(2)}, u32[]{:S(2)}) %collective-permute-start.33) | collective-permute-done | bytes 139296 | tf_op jit(solution)/shard_map/ppermute | solution.py:1081
  413.1 4.0 all-to-all-start.2
  418.0 3.7 fusion.11
  423.2 15.8 %reduce-scatter.11.cloned.1.call-done = bf16[1,8,2,32,576]{4,3,2,1,0:T(8,128)(2,1)} async-done(((bf16[4,8,2,32,576]{4,3,2,1,0:T(8,128)(2,1)}), bf16[1,8,2,32,576]{4,3,2,1,0:T(8,128)(2,1)}) %reduce-scatter.11.cloned.1.call-update) | async-done | bytes 589840 | tf_op jit(solution)/shard_map/reduce_scatter | solution.py:1235
  439.0 6.4 %all-to-all-done.2.home_ref = bf16[8,48,256]{2,1,0:T(8,128)(2,1)} async-done(((bf16[8,48,256]{2,1,0:T(8,128)(2,1)}), bf16[8,48,256]{2,1,0:T(8,128)(2,1)}, u32[]{:S(2)}, u32[]{:S(2)}) %all-to-all-start.2) | async-done | bytes 196640 | tf_op jit(solution)/shard_map/all_to_all | solution.py:224
  445.3 3.8 all-to-all-start.3
  449.1 1.7 unpack_heads.1
  453.6 6.7 %all-to-all-done.3.home_ref = bf16[8,2,32,576]{3,2,1,0:T(8,128)(2,1)S(1)} async-done(((bf16[8,2,32,576]{3,2,1,0:T(8,128)(2,1)}), bf16[8,2,32,576]{3,2,1,0:T(8,128)(2,1)S(1)}, u32[]{:S(2)}, u32[]{:S(2)}) %all-to-all-start.3) | async-done | bytes 589856 | tf_op jit(solution)/shard_map/all_to_all | solution.py:224
  461.1 2.5 unpack.1
  464.9 4.1 multiply_reduce_fusion
  469.1 2.7 fusion.4
  (265 shorter events, 75.0 us)
Async XLA Ops:
  7.2 68.3 %all-gather.7.cloned.1.call-start = ((), (), s32[]{:S(2)}) async-start(), calls=%async_computation.12 | async-start | bytes 1802240 | tf_op jit(solution)/shard_map/all_gather | solution.py:1182
  9.0 35.3 %collective-permute-start.5 = (bf16[2,192,1024]{2,1,0:T(8,128)(2,1)}, bf16[2,192,1024]{2,1,0:T(8,128)(2,1)}, u32[]{:S(2)}, u32[]{:S(2)}) collective-permute-start(bf16[2,192,1024]{2,1,0:T(8,128)(2,1)} %refs_0_.1), channel_id=1, source_target_pairs={{0,6},{1,7},{2,4},{3,5},{4,2},{5,3},{6,0},{7,1},{8,14},{9,15},{10,... | collective-permute-start | bytes 2359304 | tf_op jit(solution)/shard_map/ppermute | solution.py:129
  17.2 22.8 %all-to-all-start = ((bf16[8,32,1536]{2,1,0:T(8,128)(2,1)}), bf16[8,32,1536]{2,1,0:T(8,128)(2,1)S(1)}, u32[]{:S(2)}, u32[]{:S(2)}) async-start(bf16[8,32,1536]{2,1,0:T(8,128)(2,1)} %pack.1), calls=%async_computation | async-start | bytes 1572864 | tf_op jit(solution)/shard_map/all_to_all | solution.py:224
  20.8 147.7 %all-gather.11.cloned.1.call-start = ((), (), s32[]{:S(2)}) async-start(), calls=%async_computation.14 | async-start | bytes 2949120 | tf_op jit(solution)/shard_map/all_gather | solution.py:1189
  20.9 35.3 %collective-permute-start.3 = (bf16[2,192,1024]{2,1,0:T(8,128)(2,1)S(1)}, bf16[2,192,1024]{2,1,0:T(8,128)(2,1)}, u32[]{:S(2)}, u32[]{:S(2)}) collective-permute-start(bf16[2,192,1024]{2,1,0:T(8,128)(2,1)S(1)} %copy-done.1), channel_id=1, source_target_pairs={{0,4},{1,5},{2,6},{3,7},{4,0},{5,1},{6,2},{7,3},{8,12},{9,13},{10,... | collective-permute-start | bytes 2359304 | tf_op jit(solution)/shard_map/ppermute | solution.py:129
  22.8 35.2 %collective-permute-start.1 = (bf16[2,192,1024]{2,1,0:T(8,128)(2,1)S(1)}, bf16[2,192,1024]{2,1,0:T(8,128)(2,1)}, u32[]{:S(2)}, u32[]{:S(2)}) collective-permute-start(bf16[2,192,1024]{2,1,0:T(8,128)(2,1)S(1)} %copy-done.1), channel_id=1, source_target_pairs={{0,2},{1,3},{2,0},{3,1},{4,6},{5,7},{6,4},{7,5},{8,10},{9,11},{10,... | collective-permute-start | bytes 2359304 | tf_op jit(solution)/shard_map/ppermute | solution.py:129
  40.1 20.9 %collective-permute-start.9 = (bf16[8,32,384]{2,1,0:T(8,128)(2,1)S(1)}, bf16[8,32,384]{2,1,0:T(8,128)(2,1)S(1)}, u32[]{:S(2)}, u32[]{:S(2)}) collective-permute-start(bf16[8,32,384]{2,1,0:T(8,128)(2,1)S(1)} %slice.253.refs_8_), channel_id=1, source_target_pairs={{0,24},{8,16},{16,8},{24,0},{1,25},{9,17},{17,9},{25,1},{2,26},{10... | collective-permute-start | bytes 589832 | tf_op jit(solution)/shard_map/ppermute | solution.py:1081
  44.3 20.0 %collective-permute-start.8 = (bf16[8,32,384]{2,1,0:T(8,128)(2,1)S(1)}, bf16[8,32,384]{2,1,0:T(8,128)(2,1)S(1)}, u32[]{:S(2)}, u32[]{:S(2)}) collective-permute-start(bf16[8,32,384]{2,1,0:T(8,128)(2,1)S(1)} %slice.253.refs_8_), channel_id=1, source_target_pairs={{0,16},{8,24},{16,0},{24,8},{1,17},{9,25},{17,1},{25,9},{2,18},{10... | collective-permute-start | bytes 589832 | tf_op jit(solution)/shard_map/ppermute | solution.py:1081
  44.3 15.5 %collective-permute-start.7 = (bf16[8,32,384]{2,0,1:T(8,128)(2,1)S(1)}, bf16[8,32,384]{2,0,1:T(8,128)(2,1)S(1)}, u32[]{:S(2)}, u32[]{:S(2)}) collective-permute-start(bf16[8,32,384]{2,0,1:T(8,128)(2,1)S(1)} %copy.112), channel_id=1, source_target_pairs={{0,8},{8,0},{16,24},{24,16},{1,9},{9,1},{17,25},{25,17},{2,10},{10... | collective-permute-start | bytes 589832 | tf_op jit(solution)/shard_map/ppermute | solution.py:1081
  67.6 100.9 %all-gather.9.cloned.1.call-start = ((), (), s32[]{:S(2)}) async-start(), calls=%async_computation.13 | async-start | bytes 2359296 | tf_op jit(solution)/shard_map/all_gather | solution.py:1185
  67.7 9.7 %collective-permute-start = (bf16[2,192,1024]{2,1,0:T(8,128)(2,1)S(1)}, bf16[2,192,1024]{2,1,0:T(8,128)(2,1)}, u32[]{:S(2)}, u32[]{:S(2)}) collective-permute-start(bf16[2,192,1024]{2,1,0:T(8,128)(2,1)S(1)} %copy-done.1), channel_id=1, source_target_pairs={{0,1},{1,0},{2,3},{3,2},{4,5},{5,4},{6,7},{7,6},{8,9},{9,8},{10,11... | collective-permute-start | bytes 2359304 | tf_op jit(solution)/shard_map/ppermute | solution.py:129
  67.8 52.6 %collective-permute-start.19 = (bf16[2,192,1024]{2,1,0:T(8,128)(2,1)S(1)}, bf16[2,192,1024]{2,1,0:T(8,128)(2,1)}, u32[]{:S(2)}, u32[]{:S(2)}) collective-permute-start(bf16[2,192,1024]{2,1,0:T(8,128)(2,1)S(1)} %copy-done.4), channel_id=1, source_target_pairs={{0,1},{1,0},{2,3},{3,2},{4,5},{5,4},{6,7},{7,6},{8,9},{9,8},{10,11... | collective-permute-start | bytes 2359304 | tf_op jit(solution)/shard_map/ppermute | solution.py:129
  69.4 9.5 %collective-permute-start.6 = (bf16[2,192,1024]{2,1,0:T(8,128)(2,1)}, bf16[2,192,1024]{2,1,0:T(8,128)(2,1)}, u32[]{:S(2)}, u32[]{:S(2)}) collective-permute-start(bf16[2,192,1024]{2,1,0:T(8,128)(2,1)} %collective-permute-done.5.refs_6_), channel_id=1, source_target_pairs={{0,1},{1,0},{2,3},{3,2},{4,5},{5,4},{6,7},{7,6},{8,9},{9,8},{10,11... | collective-permute-start | bytes 2359304 | tf_op jit(solution)/shard_map/ppermute | solution.py:129
  69.5 10.9 %collective-permute-start.4 = (bf16[2,192,1024]{2,1,0:T(8,128)(2,1)}, bf16[2,192,1024]{2,1,0:T(8,128)(2,1)}, u32[]{:S(2)}, u32[]{:S(2)}) collective-permute-start(bf16[2,192,1024]{2,1,0:T(8,128)(2,1)} %collective-permute-done.3.refs_4_), channel_id=1, source_target_pairs={{0,1},{1,0},{2,3},{3,2},{4,5},{5,4},{6,7},{7,6},{8,9},{9,8},{10,11... | collective-permute-start | bytes 2359304 | tf_op jit(solution)/shard_map/ppermute | solution.py:129
  69.9 10.5 %collective-permute-start.2 = (bf16[2,192,1024]{2,1,0:T(8,128)(2,1)}, bf16[2,192,1024]{2,1,0:T(8,128)(2,1)}, u32[]{:S(2)}, u32[]{:S(2)}) collective-permute-start(bf16[2,192,1024]{2,1,0:T(8,128)(2,1)} %collective-permute-done.1.refs_2_), channel_id=1, source_target_pairs={{0,1},{1,0},{2,3},{3,2},{4,5},{5,4},{6,7},{7,6},{8,9},{9,8},{10,11... | collective-permute-start | bytes 2359304 | tf_op jit(solution)/shard_map/ppermute | solution.py:129
  77.2 268.0 %reduce-scatter.7.cloned.1.call-start = ((), (), s32[]{:S(2)}) async-start(), calls=%async_computation.9 | async-start | bytes 2359296 | tf_op jit(solution)/shard_map/reduce_scatter | solution.py:1240
  77.4 20.8 %collective-permute-start.11 = (bf16[2,192,1024]{2,1,0:T(8,128)(2,1)}, bf16[2,192,1024]{2,1,0:T(8,128)(2,1)S(1)}, u32[]{:S(2)}, u32[]{:S(2)}) collective-permute-start(bf16[2,192,1024]{2,1,0:T(8,128)(2,1)} %broadcast_add_fusion), channel_id=1, source_target_pairs={{0,4},{1,5},{2,6},{3,7},{4,0},{5,1},{6,2},{7,3},{8,12},{9,13},{10,... | collective-permute-start | bytes 2359304 | tf_op jit(solution)/shard_map/ppermute | solution.py:129
  78.9 19.8 %collective-permute-start.10 = (bf16[2,192,1024]{2,1,0:T(8,128)(2,1)}, bf16[2,192,1024]{2,1,0:T(8,128)(2,1)S(1)}, u32[]{:S(2)}, u32[]{:S(2)}) collective-permute-start(bf16[2,192,1024]{2,1,0:T(8,128)(2,1)} %broadcast_add_fusion), channel_id=1, source_target_pairs={{0,2},{1,3},{2,0},{3,1},{4,6},{5,7},{6,4},{7,5},{8,10},{9,11},{10,... | collective-permute-start | bytes 2359304 | tf_op jit(solution)/shard_map/ppermute | solution.py:129
  118.1 23.3 %collective-permute-start.15 = (bf16[2,1536,128]{2,1,0:T(8,128)(2,1)S(1)}, bf16[2,1536,128]{2,1,0:T(8,128)(2,1)S(1)}, u32[]{:S(2)}, u32[]{:S(2)}) collective-permute-start(bf16[2,1536,128]{2,1,0:T(8,128)(2,1)S(1)} %get-tuple-element.63.refs_0_.o_ref), channel_id=1, source_target_pairs={{0,4},{1,5},{2,6},{3,7},{4,0},{5,1},{6,2},{7,3},{8,12},{9,13},{10,... | collective-permute-start | bytes 2359304 | tf_op jit(solution)/shard_map/ppermute | solution.py:129
  118.7 23.8 %collective-permute-start.21 = (bf16[2,192,1024]{2,1,0:T(8,128)(2,1)S(1)}, bf16[2,192,1024]{2,1,0:T(8,128)(2,1)S(1)}, u32[]{:S(2)}, u32[]{:S(2)}) collective-permute-start(bf16[2,192,1024]{2,1,0:T(8,128)(2,1)S(1)} %collective-permute-done.11.refs_1_.refs_12_), channel_id=1, source_target_pairs={{0,1},{1,0},{2,3},{3,2},{4,5},{5,4},{6,7},{7,6},{8,9},{9,8},{10,11... | collective-permute-start | bytes 2359304 | tf_op jit(solution)/shard_map/ppermute | solution.py:129
  118.8 43.8 %collective-permute-start.22 = (bf16[2,192,1024]{2,1,0:T(8,128)(2,1)S(1)}, bf16[2,192,1024]{2,1,0:T(8,128)(2,1)}, u32[]{:S(2)}, u32[]{:S(2)}) collective-permute-start(bf16[2,192,1024]{2,1,0:T(8,128)(2,1)S(1)} %collective-permute-done.10.refs_0_.refs_10_), channel_id=1, source_target_pairs={{0,4},{1,5},{2,6},{3,7},{4,0},{5,1},{6,2},{7,3},{8,12},{9,13},{10,... | collective-permute-start | bytes 2359304 | tf_op jit(solution)/shard_map/ppermute | solution.py:129
  120.2 42.4 %collective-permute-start.20 = (bf16[2,192,1024]{2,1,0:T(8,128)(2,1)S(1)}, bf16[2,192,1024]{2,1,0:T(8,128)(2,1)S(1)}, u32[]{:S(2)}, u32[]{:S(2)}) collective-permute-start(bf16[2,192,1024]{2,1,0:T(8,128)(2,1)S(1)} %collective-permute-done.10.refs_0_.refs_10_), channel_id=1, source_target_pairs={{0,1},{1,0},{2,3},{3,2},{4,5},{5,4},{6,7},{7,6},{8,9},{9,8},{10,11... | collective-permute-start | bytes 2359304 | tf_op jit(solution)/shard_map/ppermute | solution.py:129
  120.4 42.6 %collective-permute-start.13 = (bf16[2,1536,128]{2,1,0:T(8,128)(2,1)S(1)}, bf16[2,1536,128]{2,1,0:T(8,128)(2,1)S(1)}, u32[]{:S(2)}, u32[]{:S(2)}) collective-permute-start(bf16[2,1536,128]{2,1,0:T(8,128)(2,1)S(1)} %get-tuple-element.63.refs_0_.o_ref), channel_id=1, source_target_pairs={{0,2},{1,3},{2,0},{3,1},{4,6},{5,7},{6,4},{7,5},{8,10},{9,11},{10,... | collective-permute-start | bytes 2359304 | tf_op jit(solution)/shard_map/ppermute | solution.py:129
  141.4 24.1 %collective-permute-start.17 = (bf16[2,1536,128]{2,1,0:T(8,128)(2,1)S(1)}, bf16[2,1536,128]{2,1,0:T(8,128)(2,1)}, u32[]{:S(2)}, u32[]{:S(2)}) collective-permute-start(bf16[2,1536,128]{2,1,0:T(8,128)(2,1)S(1)} %collective-permute-done.15.refs_4_), channel_id=1, source_target_pairs={{0,2},{1,3},{2,0},{3,1},{4,6},{5,7},{6,4},{7,5},{8,10},{9,11},{10,... | collective-permute-start | bytes 2359304 | tf_op jit(solution)/shard_map/ppermute | solution.py:129
  142.6 23.6 %collective-permute-start.12 = (bf16[2,1536,128]{2,1,0:T(8,128)(2,1)S(1)}, bf16[2,1536,128]{2,1,0:T(8,128)(2,1)}, u32[]{:S(2)}, u32[]{:S(2)}) collective-permute-start(bf16[2,1536,128]{2,1,0:T(8,128)(2,1)S(1)} %get-tuple-element.63.refs_0_.o_ref), channel_id=1, source_target_pairs={{0,1},{1,0},{2,3},{3,2},{4,5},{5,4},{6,7},{7,6},{8,9},{9,8},{10,11... | collective-permute-start | bytes 2359304 | tf_op jit(solution)/shard_map/ppermute | solution.py:129
  162.5 4.5 collective-permute-start.16
  163.1 4.5 collective-permute-start.14
  223.9 5.9 %collective-permute-start.25 = (bf16[4,2,192,1024]{3,2,1,0:T(8,128)(2,1)}, bf16[4,2,192,1024]{3,2,1,0:T(8,128)(2,1)S(1)}, u32[]{:S(2)}, u32[]{:S(2)}) collective-permute-start(bf16[4,2,192,1024]{3,2,1,0:T(8,128)(2,1)} %get-tuple-element.70), channel_id=1, source_target_pairs={{0,1},{1,0},{2,3},{3,2},{4,5},{5,4},{6,7},{7,6},{8,9},{9,8},{10,11... | collective-permute-start | bytes 9437192 | tf_op jit(solution)/shard_map/ppermute | solution.py:129
  234.7 21.6 %collective-permute-start.28 = (bf16[2,192,1024]{2,1,0:T(8,128)(2,1)}, bf16[2,192,1024]{2,1,0:T(8,128)(2,1)}, u32[]{:S(2)}, u32[]{:S(2)}) collective-permute-start(bf16[2,192,1024]{2,1,0:T(8,128)(2,1)} %get-tuple-element.108), channel_id=1, source_target_pairs={{0,6},{1,7},{2,4},{3,5},{4,2},{5,3},{6,0},{7,1},{8,14},{9,15},{10,... | collective-permute-start | bytes 2359304 | tf_op jit(solution)/shard_map/ppermute | solution.py:129
  236.1 36.3 %collective-permute-start.27 = (bf16[2,192,1024]{2,1,0:T(8,128)(2,1)}, bf16[2,192,1024]{2,1,0:T(8,128)(2,1)}, u32[]{:S(2)}, u32[]{:S(2)}) collective-permute-start(bf16[2,192,1024]{2,1,0:T(8,128)(2,1)} %get-tuple-element.109), channel_id=1, source_target_pairs={{0,4},{1,5},{2,6},{3,7},{4,0},{5,1},{6,2},{7,3},{8,12},{9,13},{10,... | collective-permute-start | bytes 2359304 | tf_op jit(solution)/shard_map/ppermute | solution.py:129
  237.3 35.1 %collective-permute-start.26 = (bf16[2,192,1024]{2,1,0:T(8,128)(2,1)}, bf16[2,192,1024]{2,1,0:T(8,128)(2,1)}, u32[]{:S(2)}, u32[]{:S(2)}) collective-permute-start(bf16[2,192,1024]{2,1,0:T(8,128)(2,1)} %get-tuple-element.110), channel_id=1, source_target_pairs={{0,2},{1,3},{2,0},{3,1},{4,6},{5,7},{6,4},{7,5},{8,10},{9,11},{10,... | collective-permute-start | bytes 2359304 | tf_op jit(solution)/shard_map/ppermute | solution.py:129
  282.7 74.2 %reduce-scatter.5.cloned.1.call-start = ((), (), s32[]{:S(2)}) async-start(), calls=%async_computation.8 | async-start | bytes 1474560 | tf_op jit(solution)/shard_map/reduce_scatter | solution.py:1236
  282.7 25.2 %collective-permute-start.24 = (bf16[4,2,192,1024]{3,2,1,0:T(8,128)(2,1)}, bf16[4,2,192,1024]{3,2,1,0:T(8,128)(2,1)}, u32[]{:S(2)}, u32[]{:S(2)}) collective-permute-start(bf16[4,2,192,1024]{3,2,1,0:T(8,128)(2,1)} %get-tuple-element.67), channel_id=1, source_target_pairs={{0,1},{1,0},{2,3},{3,2},{4,5},{5,4},{6,7},{7,6},{8,9},{9,8},{10,11... | collective-permute-start | bytes 9437192 | tf_op jit(solution)/shard_map/ppermute | solution.py:129
  283.3 23.4 %all-to-all-start.1 = ((bf16[8,2,192,128]{3,2,1,0:T(8,128)(2,1)}), bf16[8,2,192,128]{3,2,1,0:T(8,128)(2,1)S(1)}, u32[]{:S(2)}, u32[]{:S(2)}) async-start(bf16[8,2,192,128]{3,2,1,0:T(8,128)(2,1)} %get-tuple-element.73), calls=%async_computation.1 | async-start | bytes 1572864 | tf_op jit(solution)/shard_map/all_to_all | solution.py:224
  286.8 134.9 %reduce-scatter.9.cloned.1.call-start = ((), (), s32[]{:S(2)}) async-start(), calls=%async_computation.10 | async-start | bytes 327680 | tf_op jit(solution)/shard_map/reduce_scatter | solution.py:1241
  312.5 44.4 %collective-permute-start.29 = (bf16[2,192,1024]{2,1,0:T(8,128)(2,1)}, bf16[2,192,1024]{2,1,0:T(8,128)(2,1)S(1)}, u32[]{:S(2)}, u32[]{:S(2)}) collective-permute-start(bf16[2,192,1024]{2,1,0:T(8,128)(2,1)} %get-tuple-element.105), channel_id=1, source_target_pairs={{0,2},{1,3},{2,0},{3,1},{4,6},{5,7},{6,4},{7,5},{8,10},{9,11},{10,... | collective-permute-start | bytes 2359304 | tf_op jit(solution)/shard_map/ppermute | solution.py:129
  314.4 42.4 %collective-permute-start.31 = (bf16[2,192,1024]{2,1,0:T(8,128)(2,1)}, bf16[2,192,1024]{2,1,0:T(8,128)(2,1)S(1)}, u32[]{:S(2)}, u32[]{:S(2)}) collective-permute-start(bf16[2,192,1024]{2,1,0:T(8,128)(2,1)} %get-tuple-element.106), channel_id=1, source_target_pairs={{0,6},{1,7},{2,4},{3,5},{4,2},{5,3},{6,0},{7,1},{8,14},{9,15},{10,... | collective-permute-start | bytes 2359304 | tf_op jit(solution)/shard_map/ppermute | solution.py:129
  315.9 41.0 %collective-permute-start.30 = (bf16[2,192,1024]{2,1,0:T(8,128)(2,1)}, bf16[2,192,1024]{2,1,0:T(8,128)(2,1)S(1)}, u32[]{:S(2)}, u32[]{:S(2)}) collective-permute-start(bf16[2,192,1024]{2,1,0:T(8,128)(2,1)} %get-tuple-element.107), channel_id=1, source_target_pairs={{0,4},{1,5},{2,6},{3,7},{4,0},{5,1},{6,2},{7,3},{8,12},{9,13},{10,... | collective-permute-start | bytes 2359304 | tf_op jit(solution)/shard_map/ppermute | solution.py:129
  345.2 93.8 %reduce-scatter.11.cloned.1.call-start = ((), (), s32[]{:S(2)}) async-start(), calls=%async_computation.11 | async-start | bytes 3276800 | tf_op jit(solution)/shard_map/reduce_scatter | solution.py:1235
  376.8 6.0 %collective-permute-start.32 = (bf16[4,2,192,1024]{3,2,1,0:T(8,128)(2,1)}, bf16[4,2,192,1024]{3,2,1,0:T(8,128)(2,1)}, u32[]{:S(2)}, u32[]{:S(2)}) collective-permute-start(bf16[4,2,192,1024]{3,2,1,0:T(8,128)(2,1)} %get-tuple-element.84), channel_id=1, source_target_pairs={{0,1},{1,0},{2,3},{3,2},{4,5},{5,4},{6,7},{7,6},{8,9},{9,8},{10,11... | collective-permute-start | bytes 9437192 | tf_op jit(solution)/shard_map/ppermute | solution.py:129
  387.2 23.9 %collective-permute-start.37 = (bf16[272,256]{1,0:T(8,128)(2,1)}, bf16[272,256]{1,0:T(8,128)(2,1)}, u32[]{:S(2)}, u32[]{:S(2)}) collective-permute-start(bf16[272,256]{1,0:T(8,128)(2,1)} %get-tuple-element.128), channel_id=1, source_target_pairs={{0,16},{8,24},{16,0},{24,8},{1,17},{9,25},{17,1},{25,9},{2,18},{10... | collective-permute-start | bytes 417800 | tf_op jit(solution)/shard_map/ppermute | solution.py:1081
  388.5 22.7 %collective-permute-start.38 = (bf16[272,256]{1,0:T(8,128)(2,1)}, bf16[272,256]{1,0:T(8,128)(2,1)}, u32[]{:S(2)}, u32[]{:S(2)}) collective-permute-start(bf16[272,256]{1,0:T(8,128)(2,1)} %get-tuple-element.129), channel_id=1, source_target_pairs={{0,24},{8,16},{16,8},{24,0},{1,25},{9,17},{17,9},{25,1},{2,26},{10... | collective-permute-start | bytes 417800 | tf_op jit(solution)/shard_map/ppermute | solution.py:1081
  389.1 19.2 %collective-permute-start.33 = (bf16[272,256]{1,0:T(8,128)(2,1)S(1)}, bf16[272,256]{1,0:T(8,128)(2,1)S(1)}, u32[]{:S(2)}, u32[]{:S(2)}) collective-permute-start(bf16[272,256]{1,0:T(8,128)(2,1)S(1)} %get-tuple-element.130), channel_id=1, source_target_pairs={{0,8},{8,0},{16,24},{24,16},{1,9},{9,1},{17,25},{25,17},{2,10},{10... | collective-permute-start | bytes 417800 | tf_op jit(solution)/shard_map/ppermute | solution.py:1081
  395.3 69.7 %collective-permute-start.34 = (bf16[2,192,1024]{2,1,0:T(8,128)(2,1)}, bf16[2,192,1024]{2,1,0:T(8,128)(2,1)}, u32[]{:S(2)}, u32[]{:S(2)}) collective-permute-start(bf16[2,192,1024]{2,1,0:T(8,128)(2,1)} %get-tuple-element.102), channel_id=1, source_target_pairs={{0,2},{1,3},{2,0},{3,1},{4,6},{5,7},{6,4},{7,5},{8,10},{9,11},{10,... | collective-permute-start | bytes 2359304 | tf_op jit(solution)/shard_map/ppermute | solution.py:129
  396.8 68.2 %collective-permute-start.36 = (bf16[2,192,1024]{2,1,0:T(8,128)(2,1)}, bf16[2,192,1024]{2,1,0:T(8,128)(2,1)}, u32[]{:S(2)}, u32[]{:S(2)}) collective-permute-start(bf16[2,192,1024]{2,1,0:T(8,128)(2,1)} %get-tuple-element.103), channel_id=1, source_target_pairs={{0,6},{1,7},{2,4},{3,5},{4,2},{5,3},{6,0},{7,1},{8,14},{9,15},{10,... | collective-permute-start | bytes 2359304 | tf_op jit(solution)/shard_map/ppermute | solution.py:129
  408.3 56.6 %collective-permute-start.35 = (bf16[2,192,1024]{2,1,0:T(8,128)(2,1)}, bf16[2,192,1024]{2,1,0:T(8,128)(2,1)}, u32[]{:S(2)}, u32[]{:S(2)}) collective-permute-start(bf16[2,192,1024]{2,1,0:T(8,128)(2,1)} %get-tuple-element.104), channel_id=1, source_target_pairs={{0,4},{1,5},{2,6},{3,7},{4,0},{5,1},{6,2},{7,3},{8,12},{9,13},{10,... | collective-permute-start | bytes 2359304 | tf_op jit(solution)/shard_map/ppermute | solution.py:129
  413.1 32.2 %all-to-all-start.2 = ((bf16[8,48,256]{2,1,0:T(8,128)(2,1)}), bf16[8,48,256]{2,1,0:T(8,128)(2,1)}, u32[]{:S(2)}, u32[]{:S(2)}) async-start(bf16[8,48,256]{2,1,0:T(8,128)(2,1)} %pad_maximum_fusion.13), calls=%async_computation.3 | async-start | bytes 393216 | tf_op jit(solution)/shard_map/all_to_all | solution.py:224
  445.3 14.9 %all-to-all-start.3 = ((bf16[8,2,32,576]{3,2,1,0:T(8,128)(2,1)}), bf16[8,2,32,576]{3,2,1,0:T(8,128)(2,1)S(1)}, u32[]{:S(2)}, u32[]{:S(2)}) async-start(bf16[8,2,32,576]{3,2,1,0:T(8,128)(2,1)} %bitcast.128), calls=%async_computation.7 | async-start | bytes 1310720 | tf_op jit(solution)/shard_map/all_to_all | solution.py:224
  (56 other events, 742.5 us)
Sparse Core Ops, SparseCore 0:
  10.2 48.2 all-gather.6
  67.7 49.9 all-gather.10
  120.2 35.3 all-gather.8
  282.8 42.5 reduce-scatter.6
  327.6 29.1 reduce-scatter.4
  359.1 18.3 reduce-scatter.8
  379.8 59.1 reduce-scatter.10

commit v5 on v4

--- a/solution.py
+++ b/solution.py
@@ -391,7 +391,7 @@
         ],
         scratch_shapes=[pltpu.VMEM((length, HD), f32), pltpu.VMEM((length, HD), f32)],
         compiler_params=pltpu.CompilerParams(vmem_limit_bytes=56 << 20),
-        cost_estimate=pl.CostEstimate(flops=seqs * length * length * 640, bytes_accessed=seqs * length * 2560, transcendentals=seqs * length * length),
+        cost_estimate=pl.CostEstimate(flops=seqs * length * length * 8192, bytes_accessed=seqs * length * 2560, transcendentals=seqs * length * length),
         name="attn_bwd",
     )(q, kv, do, out, lse, starts, *earlier)
 
@@ -1235,10 +1235,10 @@
     gate_up_sum = lax.psum_scatter(gate_up_term, "fsdp", scatter_dimension=0, tiled=False)
     down_sum = lax.psum_scatter(down_term, "fsdp", scatter_dimension=0, tiled=False)
     attn_own = lax.dynamic_slice_in_dim(attn_rows, me * span, span, 1).reshape(own_rows, width)
+    attn_own = after(attn_own, gate_up_term)
     output_term = matmul_tn(attn_own, grad_mid_half).astype(bf16)
     output_term = output_term.reshape(size, groups, shard, width).transpose(1, 0, 2, 3)
     output_term = lax.psum_scatter(output_term, "seq", scatter_dimension=0, tiled=False)
-    output_sum = lax.psum_scatter(output_term, "fsdp", scatter_dimension=0, tiled=False)
     out_stages = reduce_stages(out_even, out_odd, [grad_heads, gate_up_term])
     gate_up_home = spread(gate_up_sum)
 
@@ -1246,11 +1246,11 @@
     totals_row = jnp.concatenate([totals_row, jnp.zeros((seqs, 6, length), f32)], axis=1)
     starts_row = jnp.broadcast_to(starts[:, None, :], (seqs, 8, length))
     grad_q, grad_kv = attn_bwd(
-        q_rows, kv_rows, grad_heads, outputs, totals_row, starts_row, span, [out_stages[0], gate_up_term]
+        q_rows, kv_rows, grad_heads, outputs, totals_row, starts_row, span, [out_stages[0], gate_up_term, down_sum]
     )
     gin_even, gin_odd, qkv_term, head_gains = qkv_bwd(
         at, grad_q, grad_kv, qkv_raw, normed_in, w_qkv, scales, cosine, sine,
-        [*out_stages[1:], down_sum]
+        [*out_stages[1:], gate_up_sum]
     )
     in_stages = reduce_stages(gin_even, gin_odd)
     own_in = block_input.reshape(own_rows, width).astype(f32)
@@ -1285,7 +1285,9 @@
     residual_own = lax.dynamic_slice_in_dim(residual_mid, me * span, span, 1)
     block_output = after(residual_own + own_sum(out_even, out_stages), qkv_parts[0]).astype(bf16)
     down_grad = after(down_sum.astype(f32), qkv_parts[0]).reshape(part, width)
-    output_grad = after(output_sum.astype(f32), qkv_parts[0])
+    output_grad = lax.psum_scatter(
+        after(output_term, qkv_parts[0]), "fsdp", scatter_dimension=0, tiled=False
+    ).astype(f32)
     gate_grad, up_grad, gain_two_sum = unpack_columns(gate_up_home, gate_weight, up_weight, part, qkv_parts[0])
 
     gain_one_grad = gain_one_sum[:, 0] / attention_gain.astype(f32)

time: 487 us -> 496 us (1.018)
  local copies, waits for them, and re-layouts: 41.3 us -> 47.9 us
    reduce_scatter x1, waiting for transfers between devices: 0.01 us -> 38.9 us  [body(): lax.psum_scatter(output_term, 'seq', scatter_dimension=0, tiled=False)]
    all_to_all x4, waiting for transfers between devices: 28.1 us -> 15 us  [spread(): lax.all_to_all(blocks, 'seq', split_axis=0, concat_axis=0, tiled=True)]
    reduce_scatter x1, waiting for transfers between devices: 15.8 us -> 2.73 us  [body(): lax.psum_scatter(gate_up_term, 'fsdp', scatter_dimension=0, tiled=False)]
    reduce_scatter x1, waiting for transfers between devices: 11.6 us -> 0.01 us  [body(): lax.psum_scatter(down_term, 'fsdp', scatter_dimension=0, tiled=False)]
    ppermute x6, waiting for transfers between devices: 12.2 us -> 4.95 us  [swap_line(): return lax.ppermute(array, 'fsdp', [(i, i ^ mask) for i in range(size)])]
    ppermute x33, waiting for transfers between devices: 76.8 us -> 84 us  [swap(): return lax.ppermute(array, 'seq', [(i, i ^ mask) for i in range(groups)])]
    unnamed x109 -> x113, local copies, waits for them, and re-layouts: 15.4 us -> 21.7 us
    add x6 -> x7, other arithmetic: 11.9 us -> 12.1 us  [after(): return array + jnp.minimum(jnp.abs(first), 0).astype(array.dtype)]
  transfers between devices with their start and end apart: 50 -> 50, of which waited for: 19 -> 16; matrix products, arithmetic and copies ran while one was open for 12% -> 14% of each run, Pallas kernels for 22% -> 19%
where the time goes in v5:
time: 496 us; the launch traced here: 487 us
  Pallas kernels  167 us (34%)
  waiting for transfers between devices  147 us (30%)
  starting transfers between devices  52.8 us (11%)
  other arithmetic  48.5 us (10%)
  local copies, waits for them, and re-layouts  47.9 us (10%)
  between operations  23.3 us (5%)
    ppermute x33, waiting for transfers between devices, swap(): return lax.ppermute(array, 'seq', [(i, i ^ mask) for i in range(groups)])  84 us
    pallas_call x1, Pallas kernels, ffn(): pl.pallas_call(functools.partial(ffn_kernel, hidden, padded), grid_spec=p...  55.1 us
    reduce_scatter x1, waiting for transfers between devices, body(): lax.psum_scatter(output_term, 'seq', scatter_dimension=0, tiled=False)  38.9 us
    ppermute x33, starting transfers between devices, swap(): return lax.ppermute(array, 'seq', [(i, i ^ mask) for i in range(groups)])  28.9 us
    pallas_call x1, Pallas kernels, attn_bwd(): pl.pallas_call(functools.partial(attn_bwd_kernel, block), grid=(seqs, len...  27 us
    pallas_call x2, Pallas kernels, product(): pl.pallas_call(functools.partial(product_kernel, cuts), grid=(rows // til...  25.5 us
    unnamed x113, local copies, waits for them, and re-layouts  21.7 us
    pallas_call x1, Pallas kernels, qkv_bwd(): pl.pallas_call(qkv_bwd_kernel, grid_spec=pltpu.PrefetchScalarGridSpec(num...  16.7 us
  transfers between devices with their start and end apart: 50, of which 16 were waited for; matrix products, arithmetic and copies ran while one was open for 14% of the time, Pallas kernels for 19%

profile of v5, /device:TPU:0, one launch (start us, length us, event | category | flops | bytes accessed | tf_op | source)
XLA Modules:
  0.0 487.4 jit_solution(11919751303118044522)
XLA Ops:
  7.2 1.8 pad_maximum_fusion
  9.0 4.0 collective-permute-start.5
  14.3 2.9 pack.1
  17.2 3.6 all-to-all-start
  20.9 2.0 collective-permute-start.3
  25.0 15.0 %all-to-all-done = bf16[8,32,1536]{2,1,0:T(8,128)(2,1)S(1)} async-done(((bf16[8,32,1536]{2,1,0:T(8,128)(2,1)}), bf16[8,32,1536]{2,1,0:T(8,128)(2,1)S(1)}, u32[]{:S(2)}, u32[]{:S(2)}) %all-to-all-start) | async-done | bytes 786464 | tf_op jit(solution)/shard_map/all_to_all | solution.py:224
  40.1 4.2 collective-permute-start.9
  45.2 5.5 %multiply_sine_fusion = (f32[2,1536,128]{2,1,0:T(8,128)S(1)}, f32[2,1536,128]{2,1,0:T(8,128)S(1)}) fusion(f32[128]{0:T(128)S(1)} %mul.94, f32[2,1536]{1,0:T(2,128)S(1)} %get-tuple-element.127), kind=kLoop, calls=%fused_computation | loop fusion | flops 393216 | bytes 3158528 | tf_op jit(solution)/shard_map/sin | solution.py:1181
  62.3 2.0 collective-permute-done.8.refs_10_
  74.4 1.7 slice.261
  76.7 1.5 collective-permute-start.11
  84.1 14.2 %qkv_fwd.1 = (bf16[2,1536,1024]{2,1,0:T(8,128)(2,1)}, bf16[2,1536,1024]{2,1,0:T(8,128)(2,1)}, f32[2,1536,256]{2,1,0:T(8,128)}, bf16[2,1536,128]{2,1,0:T(8,128)(2...) custom-call(s32[2]{0:T(128)S(1)} %pad_add_fusion.at_ref, bf16[2,192,1024]{2,1,0:T(8,128)(2,1)S(1)} %copy-done.1, ...), custom_call_target="tpu_custom_call" | custom-call | flops 12884901888 | bytes 18874368 | tf_op jit(solution)/shard_map/qkv_fwd/pallas_call | solution.py:527
  98.4 1.9 broadcast_in_dim.50.start_ref
  100.3 16.4 %attn_fwd.1 = (bf16[2,1536,128]{2,1,0:T(8,128)(2,1)S(1)}, f32[2,1536,128]{2,1,0:T(8,128)S(1)}) custom-call(bf16[2,1536,128]{2,1,0:T(8,128)(2,1)S(1)} %get-tuple-element.61.q_ref, bf16[2,1536,128]{2,1,0:T(8,128)(2,1)S(1)} %get-tuple-element.62.kv_ref, s32[2,1536,128]{2,1,0:T(8,128)} %broadcast_in_dim.50.start_ref, ...), custom_call_target="tpu_custom_call" | custom-call | flops 1207959552 | bytes 5505024 | tf_op jit(solution)/shard_map/attn_fwd/pallas_call | solution.py:308
  121.1 20.0 %collective-permute-done.15.refs_4_ = bf16[2,1536,128]{2,1,0:T(8,128)(2,1)S(1)} collective-permute-done((bf16[2,1536,128]{2,1,0:T(8,128)(2,1)S(1)}, bf16[2,1536,128]{2,1,0:T(8,128)(2,1)S(1)}, u32[]{:S(2)}, u32[]{:S(2)}) %collective-permute-start.15) | collective-permute-done | bytes 786464 | tf_op jit(solution)/shard_map/ppermute | solution.py:129
  142.2 20.4 %collective-permute-done.22.refs_14_ = bf16[2,192,1024]{2,1,0:T(8,128)(2,1)} collective-permute-done((bf16[2,192,1024]{2,1,0:T(8,128)(2,1)S(1)}, bf16[2,192,1024]{2,1,0:T(8,128)(2,1)}, u32[]{:S(2)}, u32[]{:S(2)}) %collective-permute-start.22) | collective-permute-done | bytes 786464 | tf_op jit(solution)/shard_map/ppermute | solution.py:129
  163.2 2.1 collective-permute-done.17.refs_6_
  168.6 55.1 %ffn.1 = (bf16[2,1536,1024]{2,1,0:T(8,128)(2,1)}, f32[2,1536,1024]{2,1,0:T(8,128)}, bf16[2,1536,1024]{2,1,0:T(8,128)(2,1)}, bf16[2,1536,640]{2,1,0:T(8,128)(2,1)...) custom-call(s32[2]{0:T(128)} %copy-done.19, ...), custom_call_target="tpu_custom_call" | custom-call | flops 30601641984 | bytes 62914560 | tf_op jit(solution)/shard_map/ffn/pallas_call | solution.py:643
  223.9 2.1 copy-done.3
  226.1 9.5 %product.2.refs_3_ = bf16[4,1,1,144,1024]{4,3,2,1,0:T(8,128)(2,1)} custom-call(bf16[3072,640]{1,0:T(8,128)(2,1)S(1)} %bitcast.119, bf16[3072,1024]{1,0:T(8,128)(2,1)} %bitcast.125), custom_call_target="tpu_custom_call" | custom-call | flops 50331648 | bytes 50331648 | tf_op jit(solution)/shard_map/product/pallas_call | solution.py:699
  236.0 3.8 fusion.14
  243.4 3.1 copy.109
  246.4 15.0 %collective-permute-done.28.refs_2_ = bf16[2,192,1024]{2,1,0:T(8,128)(2,1)} collective-permute-done((bf16[2,192,1024]{2,1,0:T(8,128)(2,1)}, bf16[2,192,1024]{2,1,0:T(8,128)(2,1)}, u32[]{:S(2)}, u32[]{:S(2)}) %collective-permute-start.28) | collective-permute-done | bytes 786464 | tf_op jit(solution)/shard_map/ppermute | solution.py:129
  261.4 15.5 %collective-permute-done.27.refs_1_ = bf16[2,192,1024]{2,1,0:T(8,128)(2,1)} collective-permute-done((bf16[2,192,1024]{2,1,0:T(8,128)(2,1)}, bf16[2,192,1024]{2,1,0:T(8,128)(2,1)}, u32[]{:S(2)}, u32[]{:S(2)}) %collective-permute-start.27) | collective-permute-done | bytes 786464 | tf_op jit(solution)/shard_map/ppermute | solution.py:129
  278.1 1.6 copy-done.6
  279.7 4.8 mid_bwd.1
  287.4 3.7 all-to-all-start.1
  291.2 16.1 %product.3.refs_1_ = bf16[4,8,2,32,576]{4,3,2,1,0:T(8,128)(2,1)} custom-call(bf16[3072,1024]{1,0:T(8,128)(2,1)} %bitcast.124, bf16[3072,1280]{1,0:T(8,128)(2,1)} %bitcast.123, bf16[384,1024]{1,0:T(8,128)(2,1)S(1)} %copy-done.14), custom_call_target="tpu_custom_call" | custom-call | flops 100663296 | bytes 100663296 | tf_op jit(solution)/shard_map/product/pallas_call | solution.py:699
  312.1 5.1 %fusion.15 = (bf16[2,192,1024]{2,1,0:T(8,128)(2,1)}, bf16[2,192,1024]{2,1,0:T(8,128)(2,1)}, bf16[2,192,1024]{2,1,0:T(8,128)(2,1)}) fusion(bf16[4,2,192,1024]{3,2,1,0:T(8,128)(2,1)} %collective-permute-done.24.refs_0_, f32[]{:T(128)S(6)} %convert_element_type.397, f32[]{:T(128)S(6)} %convert.19, bf16[4,2,192,1024]{3,2,1,0:T(8,128)(2,1)} %get-tuple-element.66), kind=kLoop, calls=%fused_computation.34 | loop fusion | flops 7077888 | bytes 7077896 | tf_op jit(solution)/shard_map/add | solution.py:1076
  317.2 1.9 collective-permute-start.29
  321.3 27.0 %attn_bwd.1 = (f32[2,1536,128]{2,1,0:T(8,128)}, f32[2,1536,128]{2,1,0:T(8,128)}) custom-call(bf16[2,1536,128]{2,1,0:T(8,128)(2,1)} %copy-done.30, bf16[2,1536,128]{2,1,0:T(8,128)(2,1)} %copy-done.31, bf16[8,2,192,128]{3,2,1,0:T(8,128)(2,1)} %copy-done.37, bf16[2,1536,128]{2,1,0:T(8,128)(2,1)} %copy-done.27, f32[2,8,1536]{2,1,0:T(8,128)} %maximum_maximum_fusion.lse_ref, ...), custom_call_target="tpu_custom_call" | custom-call | flops 38654705664 | bytes 7864320 | tf_op jit(solution)/shard_map/attn_bwd/pallas_call | solution.py:375
  348.3 7.0 %collective-permute-done.31.refs_2_ = bf16[2,192,1024]{2,1,0:T(8,128)(2,1)S(1)} collective-permute-done((bf16[2,192,1024]{2,1,0:T(8,128)(2,1)}, bf16[2,192,1024]{2,1,0:T(8,128)(2,1)S(1)}, u32[]{:S(2)}, u32[]{:S(2)}) %collective-permute-start.31) | collective-permute-done | bytes 786464 | tf_op jit(solution)/shard_map/ppermute | solution.py:129
  356.6 2.7 reduce-scatter.7.cloned.1.call-done
  362.9 16.7 %qkv_bwd.1 = (bf16[4,2,192,1024]{3,2,1,0:T(8,128)(2,1)}, bf16[4,2,192,1024]{3,2,1,0:T(8,128)(2,1)}, bf16[1024,256]{1,0:T(8,128)(2,1)S(1)}, f32[8,128]{1,0:T(8,128)S(1)}) custom-call(s32[2]{0:T(128)S(1)} %copy-done.20, f32[2,1536,128]{2,1,0:T(8,128)S(1)} %copy-done.32, f32[2,1536,128]{2,1,0:T(8,128)} %get-tuple-element.79.dkv_ref, ...), custom_call_target="tpu_custom_call" | custom-call | flops 12884901888 | bytes 18874368 | tf_op jit(solution)/shard_map/qkv_bwd/pallas_call | solution.py:812
  386.0 4.2 all-to-all-start.3
  394.2 2.1 collective-permute-start.37
  397.7 4.5 fusion.18
  402.2 1.9 collective-permute-start.34
  405.5 3.0 collective-permute-done.33._
  408.5 1.5 collective-permute-start.35
  411.2 38.9 %reduce-scatter.9.cloned.1.call-done = bf16[1,4,32,1024]{3,2,1,0:T(8,128)(2,1)} async-done(((bf16[8,4,32,1024]{3,2,1,0:T(8,128)(2,1)}), bf16[1,4,32,1024]{3,2,1,0:T(8,128)(2,1)}) %reduce-scatter.9.cloned.1.call-update) | async-done | bytes 262160 | tf_op jit(solution)/shard_map/reduce_scatter | solution.py:1241
  450.1 1.7 add_bitcast_fusion.1
  453.6 3.4 all-to-all-start.2
  457.0 2.5 unpack.1
  460.4 3.7 fusion.11
  466.2 1.7 unpack_heads.1
  473.2 4.1 multiply_reduce_fusion
  477.4 2.7 fusion.4
  (270 shorter events, 78.7 us)
Async XLA Ops:
  7.2 67.2 %all-gather.7.cloned.1.call-start = ((), (), s32[]{:S(2)}) async-start(), calls=%async_computation.12 | async-start | bytes 1802240 | tf_op jit(solution)/shard_map/all_gather | solution.py:1182
  9.0 35.3 %collective-permute-start.5 = (bf16[2,192,1024]{2,1,0:T(8,128)(2,1)}, bf16[2,192,1024]{2,1,0:T(8,128)(2,1)S(1)}, u32[]{:S(2)}, u32[]{:S(2)}) collective-permute-start(bf16[2,192,1024]{2,1,0:T(8,128)(2,1)} %refs_0_.1), channel_id=1, source_target_pairs={{0,6},{1,7},{2,4},{3,5},{4,2},{5,3},{6,0},{7,1},{8,14},{9,15},{10,... | collective-permute-start | bytes 2359304 | tf_op jit(solution)/shard_map/ppermute | solution.py:129
  17.2 22.8 %all-to-all-start = ((bf16[8,32,1536]{2,1,0:T(8,128)(2,1)}), bf16[8,32,1536]{2,1,0:T(8,128)(2,1)S(1)}, u32[]{:S(2)}, u32[]{:S(2)}) async-start(bf16[8,32,1536]{2,1,0:T(8,128)(2,1)} %pack.1), calls=%async_computation | async-start | bytes 1572864 | tf_op jit(solution)/shard_map/all_to_all | solution.py:224
  20.8 147.8 %all-gather.11.cloned.1.call-start = ((), (), s32[]{:S(2)}) async-start(), calls=%async_computation.14 | async-start | bytes 2949120 | tf_op jit(solution)/shard_map/all_gather | solution.py:1189
  20.9 35.3 %collective-permute-start.3 = (bf16[2,192,1024]{2,1,0:T(8,128)(2,1)S(1)}, bf16[2,192,1024]{2,1,0:T(8,128)(2,1)}, u32[]{:S(2)}, u32[]{:S(2)}) collective-permute-start(bf16[2,192,1024]{2,1,0:T(8,128)(2,1)S(1)} %copy-done.1), channel_id=1, source_target_pairs={{0,4},{1,5},{2,6},{3,7},{4,0},{5,1},{6,2},{7,3},{8,12},{9,13},{10,... | collective-permute-start | bytes 2359304 | tf_op jit(solution)/shard_map/ppermute | solution.py:129
  22.8 35.2 %collective-permute-start.1 = (bf16[2,192,1024]{2,1,0:T(8,128)(2,1)S(1)}, bf16[2,192,1024]{2,1,0:T(8,128)(2,1)}, u32[]{:S(2)}, u32[]{:S(2)}) collective-permute-start(bf16[2,192,1024]{2,1,0:T(8,128)(2,1)S(1)} %copy-done.1), channel_id=1, source_target_pairs={{0,2},{1,3},{2,0},{3,1},{4,6},{5,7},{6,4},{7,5},{8,10},{9,11},{10,... | collective-permute-start | bytes 2359304 | tf_op jit(solution)/shard_map/ppermute | solution.py:129
  40.1 21.0 %collective-permute-start.9 = (bf16[8,32,384]{2,1,0:T(8,128)(2,1)S(1)}, bf16[8,32,384]{2,1,0:T(8,128)(2,1)S(1)}, u32[]{:S(2)}, u32[]{:S(2)}) collective-permute-start(bf16[8,32,384]{2,1,0:T(8,128)(2,1)S(1)} %slice.254.refs_8_), channel_id=1, source_target_pairs={{0,24},{8,16},{16,8},{24,0},{1,25},{9,17},{17,9},{25,1},{2,26},{10... | collective-permute-start | bytes 589832 | tf_op jit(solution)/shard_map/ppermute | solution.py:1081
  44.3 20.0 %collective-permute-start.8 = (bf16[8,32,384]{2,1,0:T(8,128)(2,1)S(1)}, bf16[8,32,384]{2,1,0:T(8,128)(2,1)S(1)}, u32[]{:S(2)}, u32[]{:S(2)}) collective-permute-start(bf16[8,32,384]{2,1,0:T(8,128)(2,1)S(1)} %slice.254.refs_8_), channel_id=1, source_target_pairs={{0,16},{8,24},{16,0},{24,8},{1,17},{9,25},{17,1},{25,9},{2,18},{10... | collective-permute-start | bytes 589832 | tf_op jit(solution)/shard_map/ppermute | solution.py:1081
  44.3 15.5 %collective-permute-start.7 = (bf16[8,32,384]{2,0,1:T(8,128)(2,1)S(1)}, bf16[8,32,384]{2,0,1:T(8,128)(2,1)S(1)}, u32[]{:S(2)}, u32[]{:S(2)}) collective-permute-start(bf16[8,32,384]{2,0,1:T(8,128)(2,1)S(1)} %copy.112), channel_id=1, source_target_pairs={{0,8},{8,0},{16,24},{24,16},{1,9},{9,1},{17,25},{25,17},{2,10},{10... | collective-permute-start | bytes 589832 | tf_op jit(solution)/shard_map/ppermute | solution.py:1081
  66.6 102.0 %all-gather.9.cloned.1.call-start = ((), (), s32[]{:S(2)}) async-start(), calls=%async_computation.13 | async-start | bytes 2359296 | tf_op jit(solution)/shard_map/all_gather | solution.py:1185
  66.6 10.0 %collective-permute-start = (bf16[2,192,1024]{2,1,0:T(8,128)(2,1)S(1)}, bf16[2,192,1024]{2,1,0:T(8,128)(2,1)}, u32[]{:S(2)}, u32[]{:S(2)}) collective-permute-start(bf16[2,192,1024]{2,1,0:T(8,128)(2,1)S(1)} %copy-done.1), channel_id=1, source_target_pairs={{0,1},{1,0},{2,3},{3,2},{4,5},{5,4},{6,7},{7,6},{8,9},{9,8},{10,11... | collective-permute-start | bytes 2359304 | tf_op jit(solution)/shard_map/ppermute | solution.py:129
  66.7 53.4 %collective-permute-start.19 = (bf16[2,192,1024]{2,1,0:T(8,128)(2,1)S(1)}, bf16[2,192,1024]{2,1,0:T(8,128)(2,1)}, u32[]{:S(2)}, u32[]{:S(2)}) collective-permute-start(bf16[2,192,1024]{2,1,0:T(8,128)(2,1)S(1)} %copy-done.4), channel_id=1, source_target_pairs={{0,1},{1,0},{2,3},{3,2},{4,5},{5,4},{6,7},{7,6},{8,9},{9,8},{10,11... | collective-permute-start | bytes 2359304 | tf_op jit(solution)/shard_map/ppermute | solution.py:129
  68.3 9.8 %collective-permute-start.6 = (bf16[2,192,1024]{2,1,0:T(8,128)(2,1)}, bf16[2,192,1024]{2,1,0:T(8,128)(2,1)}, u32[]{:S(2)}, u32[]{:S(2)}) collective-permute-start(bf16[2,192,1024]{2,1,0:T(8,128)(2,1)} %copy-done.25), channel_id=1, source_target_pairs={{0,1},{1,0},{2,3},{3,2},{4,5},{5,4},{6,7},{7,6},{8,9},{9,8},{10,11... | collective-permute-start | bytes 2359304 | tf_op jit(solution)/shard_map/ppermute | solution.py:129
  68.4 11.2 %collective-permute-start.4 = (bf16[2,192,1024]{2,1,0:T(8,128)(2,1)}, bf16[2,192,1024]{2,1,0:T(8,128)(2,1)}, u32[]{:S(2)}, u32[]{:S(2)}) collective-permute-start(bf16[2,192,1024]{2,1,0:T(8,128)(2,1)} %collective-permute-done.3.refs_4_), channel_id=1, source_target_pairs={{0,1},{1,0},{2,3},{3,2},{4,5},{5,4},{6,7},{7,6},{8,9},{9,8},{10,11... | collective-permute-start | bytes 2359304 | tf_op jit(solution)/shard_map/ppermute | solution.py:129
  68.9 10.8 %collective-permute-start.2 = (bf16[2,192,1024]{2,1,0:T(8,128)(2,1)}, bf16[2,192,1024]{2,1,0:T(8,128)(2,1)}, u32[]{:S(2)}, u32[]{:S(2)}) collective-permute-start(bf16[2,192,1024]{2,1,0:T(8,128)(2,1)} %collective-permute-done.1.refs_2_), channel_id=1, source_target_pairs={{0,1},{1,0},{2,3},{3,2},{4,5},{5,4},{6,7},{7,6},{8,9},{9,8},{10,11... | collective-permute-start | bytes 2359304 | tf_op jit(solution)/shard_map/ppermute | solution.py:129
  76.1 244.6 %reduce-scatter.5.cloned.1.call-start = ((), (), s32[]{:S(2)}) async-start(), calls=%async_computation.8 | async-start | bytes 1474560 | tf_op jit(solution)/shard_map/reduce_scatter | solution.py:1236
  76.7 21.7 %collective-permute-start.11 = (bf16[2,192,1024]{2,1,0:T(8,128)(2,1)}, bf16[2,192,1024]{2,1,0:T(8,128)(2,1)S(1)}, u32[]{:S(2)}, u32[]{:S(2)}) collective-permute-start(bf16[2,192,1024]{2,1,0:T(8,128)(2,1)} %broadcast_add_fusion), channel_id=1, source_target_pairs={{0,4},{1,5},{2,6},{3,7},{4,0},{5,1},{6,2},{7,3},{8,12},{9,13},{10,... | collective-permute-start | bytes 2359304 | tf_op jit(solution)/shard_map/ppermute | solution.py:129
  78.2 20.2 %collective-permute-start.10 = (bf16[2,192,1024]{2,1,0:T(8,128)(2,1)}, bf16[2,192,1024]{2,1,0:T(8,128)(2,1)S(1)}, u32[]{:S(2)}, u32[]{:S(2)}) collective-permute-start(bf16[2,192,1024]{2,1,0:T(8,128)(2,1)} %broadcast_add_fusion), channel_id=1, source_target_pairs={{0,2},{1,3},{2,0},{3,1},{4,6},{5,7},{6,4},{7,5},{8,10},{9,11},{10,... | collective-permute-start | bytes 2359304 | tf_op jit(solution)/shard_map/ppermute | solution.py:129
  117.9 23.2 %collective-permute-start.15 = (bf16[2,1536,128]{2,1,0:T(8,128)(2,1)S(1)}, bf16[2,1536,128]{2,1,0:T(8,128)(2,1)S(1)}, u32[]{:S(2)}, u32[]{:S(2)}) collective-permute-start(bf16[2,1536,128]{2,1,0:T(8,128)(2,1)S(1)} %get-tuple-element.63.refs_0_.o_ref), channel_id=1, source_target_pairs={{0,4},{1,5},{2,6},{3,7},{4,0},{5,1},{6,2},{7,3},{8,12},{9,13},{10,... | collective-permute-start | bytes 2359304 | tf_op jit(solution)/shard_map/ppermute | solution.py:129
  118.4 23.8 %collective-permute-start.21 = (bf16[2,192,1024]{2,1,0:T(8,128)(2,1)S(1)}, bf16[2,192,1024]{2,1,0:T(8,128)(2,1)S(1)}, u32[]{:S(2)}, u32[]{:S(2)}) collective-permute-start(bf16[2,192,1024]{2,1,0:T(8,128)(2,1)S(1)} %collective-permute-done.11.refs_1_.refs_12_), channel_id=1, source_target_pairs={{0,1},{1,0},{2,3},{3,2},{4,5},{5,4},{6,7},{7,6},{8,9},{9,8},{10,11... | collective-permute-start | bytes 2359304 | tf_op jit(solution)/shard_map/ppermute | solution.py:129
  118.4 44.2 %collective-permute-start.22 = (bf16[2,192,1024]{2,1,0:T(8,128)(2,1)S(1)}, bf16[2,192,1024]{2,1,0:T(8,128)(2,1)}, u32[]{:S(2)}, u32[]{:S(2)}) collective-permute-start(bf16[2,192,1024]{2,1,0:T(8,128)(2,1)S(1)} %collective-permute-done.10.refs_0_.refs_10_), channel_id=1, source_target_pairs={{0,4},{1,5},{2,6},{3,7},{4,0},{5,1},{6,2},{7,3},{8,12},{9,13},{10,... | collective-permute-start | bytes 2359304 | tf_op jit(solution)/shard_map/ppermute | solution.py:129
  119.9 42.7 %collective-permute-start.20 = (bf16[2,192,1024]{2,1,0:T(8,128)(2,1)S(1)}, bf16[2,192,1024]{2,1,0:T(8,128)(2,1)S(1)}, u32[]{:S(2)}, u32[]{:S(2)}) collective-permute-start(bf16[2,192,1024]{2,1,0:T(8,128)(2,1)S(1)} %collective-permute-done.10.refs_0_.refs_10_), channel_id=1, source_target_pairs={{0,1},{1,0},{2,3},{3,2},{4,5},{5,4},{6,7},{7,6},{8,9},{9,8},{10,11... | collective-permute-start | bytes 2359304 | tf_op jit(solution)/shard_map/ppermute | solution.py:129
  120.1 43.0 %collective-permute-start.13 = (bf16[2,1536,128]{2,1,0:T(8,128)(2,1)S(1)}, bf16[2,1536,128]{2,1,0:T(8,128)(2,1)S(1)}, u32[]{:S(2)}, u32[]{:S(2)}) collective-permute-start(bf16[2,1536,128]{2,1,0:T(8,128)(2,1)S(1)} %get-tuple-element.63.refs_0_.o_ref), channel_id=1, source_target_pairs={{0,2},{1,3},{2,0},{3,1},{4,6},{5,7},{6,4},{7,5},{8,10},{9,11},{10,... | collective-permute-start | bytes 2359304 | tf_op jit(solution)/shard_map/ppermute | solution.py:129
  141.1 24.1 %collective-permute-start.17 = (bf16[2,1536,128]{2,1,0:T(8,128)(2,1)S(1)}, bf16[2,1536,128]{2,1,0:T(8,128)(2,1)}, u32[]{:S(2)}, u32[]{:S(2)}) collective-permute-start(bf16[2,1536,128]{2,1,0:T(8,128)(2,1)S(1)} %collective-permute-done.15.refs_4_), channel_id=1, source_target_pairs={{0,2},{1,3},{2,0},{3,1},{4,6},{5,7},{6,4},{7,5},{8,10},{9,11},{10,... | collective-permute-start | bytes 2359304 | tf_op jit(solution)/shard_map/ppermute | solution.py:129
  142.2 23.8 %collective-permute-start.12 = (bf16[2,1536,128]{2,1,0:T(8,128)(2,1)S(1)}, bf16[2,1536,128]{2,1,0:T(8,128)(2,1)}, u32[]{:S(2)}, u32[]{:S(2)}) collective-permute-start(bf16[2,1536,128]{2,1,0:T(8,128)(2,1)S(1)} %get-tuple-element.63.refs_0_.o_ref), channel_id=1, source_target_pairs={{0,1},{1,0},{2,3},{3,2},{4,5},{5,4},{6,7},{7,6},{8,9},{9,8},{10,11... | collective-permute-start | bytes 2359304 | tf_op jit(solution)/shard_map/ppermute | solution.py:129
  162.6 4.5 collective-permute-start.16
  163.1 4.5 collective-permute-start.14
  223.7 12.3 %collective-permute-start.25 = (bf16[4,2,192,1024]{3,2,1,0:T(8,128)(2,1)}, bf16[4,2,192,1024]{3,2,1,0:T(8,128)(2,1)}, u32[]{:S(2)}, u32[]{:S(2)}) collective-permute-start(bf16[4,2,192,1024]{3,2,1,0:T(8,128)(2,1)} %get-tuple-element.70), channel_id=1, source_target_pairs={{0,1},{1,0},{2,3},{3,2},{4,5},{5,4},{6,7},{7,6},{8,9},{9,8},{10,11... | collective-permute-start | bytes 9437192 | tf_op jit(solution)/shard_map/ppermute | solution.py:129
  235.5 76.5 %collective-permute-start.24 = (bf16[4,2,192,1024]{3,2,1,0:T(8,128)(2,1)}, bf16[4,2,192,1024]{3,2,1,0:T(8,128)(2,1)}, u32[]{:S(2)}, u32[]{:S(2)}) collective-permute-start(bf16[4,2,192,1024]{3,2,1,0:T(8,128)(2,1)} %get-tuple-element.67), channel_id=1, source_target_pairs={{0,1},{1,0},{2,3},{3,2},{4,5},{5,4},{6,7},{7,6},{8,9},{9,8},{10,11... | collective-permute-start | bytes 9437192 | tf_op jit(solution)/shard_map/ppermute | solution.py:129
  239.8 21.7 %collective-permute-start.28 = (bf16[2,192,1024]{2,1,0:T(8,128)(2,1)}, bf16[2,192,1024]{2,1,0:T(8,128)(2,1)}, u32[]{:S(2)}, u32[]{:S(2)}) collective-permute-start(bf16[2,192,1024]{2,1,0:T(8,128)(2,1)} %get-tuple-element.108), channel_id=1, source_target_pairs={{0,6},{1,7},{2,4},{3,5},{4,2},{5,3},{6,0},{7,1},{8,14},{9,15},{10,... | collective-permute-start | bytes 2359304 | tf_op jit(solution)/shard_map/ppermute | solution.py:129
  240.5 36.4 %collective-permute-start.27 = (bf16[2,192,1024]{2,1,0:T(8,128)(2,1)}, bf16[2,192,1024]{2,1,0:T(8,128)(2,1)}, u32[]{:S(2)}, u32[]{:S(2)}) collective-permute-start(bf16[2,192,1024]{2,1,0:T(8,128)(2,1)} %get-tuple-element.109), channel_id=1, source_target_pairs={{0,4},{1,5},{2,6},{3,7},{4,0},{5,1},{6,2},{7,3},{8,12},{9,13},{10,... | collective-permute-start | bytes 2359304 | tf_op jit(solution)/shard_map/ppermute | solution.py:129
  241.8 35.1 %collective-permute-start.26 = (bf16[2,192,1024]{2,1,0:T(8,128)(2,1)}, bf16[2,192,1024]{2,1,0:T(8,128)(2,1)}, u32[]{:S(2)}, u32[]{:S(2)}) collective-permute-start(bf16[2,192,1024]{2,1,0:T(8,128)(2,1)} %get-tuple-element.110), channel_id=1, source_target_pairs={{0,2},{1,3},{2,0},{3,1},{4,6},{5,7},{6,4},{7,5},{8,10},{9,11},{10,... | collective-permute-start | bytes 2359304 | tf_op jit(solution)/shard_map/ppermute | solution.py:129
  287.4 23.4 %all-to-all-start.1 = ((bf16[8,2,192,128]{3,2,1,0:T(8,128)(2,1)}), bf16[8,2,192,128]{3,2,1,0:T(8,128)(2,1)S(1)}, u32[]{:S(2)}, u32[]{:S(2)}) async-start(bf16[8,2,192,128]{3,2,1,0:T(8,128)(2,1)} %copy-done.15), calls=%async_computation.1 | async-start | bytes 1572864 | tf_op jit(solution)/shard_map/all_to_all | solution.py:224
  291.1 68.3 %reduce-scatter.7.cloned.1.call-start = ((), (), s32[]{:S(2)}) async-start(), calls=%async_computation.9 | async-start | bytes 3276800 | tf_op jit(solution)/shard_map/reduce_scatter | solution.py:1235
  307.2 142.9 %reduce-scatter.9.cloned.1.call-start = ((), (), s32[]{:S(2)}) async-start(), calls=%async_computation.10 | async-start | bytes 2359296 | tf_op jit(solution)/shard_map/reduce_scatter | solution.py:1241
  317.2 31.1 %collective-permute-start.29 = (bf16[2,192,1024]{2,1,0:T(8,128)(2,1)}, bf16[2,192,1024]{2,1,0:T(8,128)(2,1)S(1)}, u32[]{:S(2)}, u32[]{:S(2)}) collective-permute-start(bf16[2,192,1024]{2,1,0:T(8,128)(2,1)} %get-tuple-element.105), channel_id=1, source_target_pairs={{0,2},{1,3},{2,0},{3,1},{4,6},{5,7},{6,4},{7,5},{8,10},{9,11},{10,... | collective-permute-start | bytes 2359304 | tf_op jit(solution)/shard_map/ppermute | solution.py:129
  319.1 36.2 %collective-permute-start.31 = (bf16[2,192,1024]{2,1,0:T(8,128)(2,1)}, bf16[2,192,1024]{2,1,0:T(8,128)(2,1)S(1)}, u32[]{:S(2)}, u32[]{:S(2)}) collective-permute-start(bf16[2,192,1024]{2,1,0:T(8,128)(2,1)} %get-tuple-element.106), channel_id=1, source_target_pairs={{0,6},{1,7},{2,4},{3,5},{4,2},{5,3},{6,0},{7,1},{8,14},{9,15},{10,... | collective-permute-start | bytes 2359304 | tf_op jit(solution)/shard_map/ppermute | solution.py:129
  320.5 36.1 %collective-permute-start.30 = (bf16[2,192,1024]{2,1,0:T(8,128)(2,1)}, bf16[2,192,1024]{2,1,0:T(8,128)(2,1)S(1)}, u32[]{:S(2)}, u32[]{:S(2)}) collective-permute-start(bf16[2,192,1024]{2,1,0:T(8,128)(2,1)} %get-tuple-element.107), channel_id=1, source_target_pairs={{0,4},{1,5},{2,6},{3,7},{4,0},{5,1},{6,2},{7,3},{8,12},{9,13},{10,... | collective-permute-start | bytes 2359304 | tf_op jit(solution)/shard_map/ppermute | solution.py:129
  380.4 9.9 %collective-permute-start.32 = (bf16[4,2,192,1024]{3,2,1,0:T(8,128)(2,1)}, bf16[4,2,192,1024]{3,2,1,0:T(8,128)(2,1)}, u32[]{:S(2)}, u32[]{:S(2)}) collective-permute-start(bf16[4,2,192,1024]{3,2,1,0:T(8,128)(2,1)} %get-tuple-element.84), channel_id=1, source_target_pairs={{0,1},{1,0},{2,3},{3,2},{4,5},{5,4},{6,7},{7,6},{8,9},{9,8},{10,11... | collective-permute-start | bytes 9437192 | tf_op jit(solution)/shard_map/ppermute | solution.py:129
  386.0 67.6 %all-to-all-start.3 = ((bf16[8,2,32,576]{3,2,1,0:T(8,128)(2,1)}), bf16[8,2,32,576]{3,2,1,0:T(8,128)(2,1)}, u32[]{:S(2)}, u32[]{:S(2)}) async-start(bf16[8,2,32,576]{3,2,1,0:T(8,128)(2,1)} %bitcast.120), calls=%async_computation.7 | async-start | bytes 1310720 | tf_op jit(solution)/shard_map/all_to_all | solution.py:224
  390.2 81.4 %reduce-scatter.11.cloned.1.call-start = ((), (), s32[]{:S(2)}) async-start(), calls=%async_computation.11 | async-start | bytes 327680 | tf_op jit(solution)/shard_map/reduce_scatter | solution.py:1288
  394.2 57.6 %collective-permute-start.37 = (bf16[272,256]{1,0:T(8,128)(2,1)}, bf16[272,256]{1,0:T(8,128)(2,1)}, u32[]{:S(2)}, u32[]{:S(2)}) collective-permute-start(bf16[272,256]{1,0:T(8,128)(2,1)} %get-tuple-element.128), channel_id=1, source_target_pairs={{0,16},{8,24},{16,0},{24,8},{1,17},{9,25},{17,1},{25,9},{2,18},{10... | collective-permute-start | bytes 417800 | tf_op jit(solution)/shard_map/ppermute | solution.py:1081
  396.3 55.5 %collective-permute-start.38 = (bf16[272,256]{1,0:T(8,128)(2,1)}, bf16[272,256]{1,0:T(8,128)(2,1)}, u32[]{:S(2)}, u32[]{:S(2)}) collective-permute-start(bf16[272,256]{1,0:T(8,128)(2,1)} %get-tuple-element.129), channel_id=1, source_target_pairs={{0,24},{8,16},{16,8},{24,0},{1,25},{9,17},{17,9},{25,1},{2,26},{10... | collective-permute-start | bytes 417800 | tf_op jit(solution)/shard_map/ppermute | solution.py:1081
  397.2 11.3 %collective-permute-start.33 = (bf16[272,256]{1,0:T(8,128)(2,1)S(1)}, bf16[272,256]{1,0:T(8,128)(2,1)S(1)}, u32[]{:S(2)}, u32[]{:S(2)}) collective-permute-start(bf16[272,256]{1,0:T(8,128)(2,1)S(1)} %get-tuple-element.130), channel_id=1, source_target_pairs={{0,8},{8,0},{16,24},{24,16},{1,9},{9,1},{17,25},{25,17},{2,10},{10... | collective-permute-start | bytes 417800 | tf_op jit(solution)/shard_map/ppermute | solution.py:1081
  402.2 71.0 %collective-permute-start.34 = (bf16[2,192,1024]{2,1,0:T(8,128)(2,1)}, bf16[2,192,1024]{2,1,0:T(8,128)(2,1)}, u32[]{:S(2)}, u32[]{:S(2)}) collective-permute-start(bf16[2,192,1024]{2,1,0:T(8,128)(2,1)} %get-tuple-element.102), channel_id=1, source_target_pairs={{0,2},{1,3},{2,0},{3,1},{4,6},{5,7},{6,4},{7,5},{8,10},{9,11},{10,... | collective-permute-start | bytes 2359304 | tf_op jit(solution)/shard_map/ppermute | solution.py:129
  404.0 69.2 %collective-permute-start.36 = (bf16[2,192,1024]{2,1,0:T(8,128)(2,1)}, bf16[2,192,1024]{2,1,0:T(8,128)(2,1)}, u32[]{:S(2)}, u32[]{:S(2)}) collective-permute-start(bf16[2,192,1024]{2,1,0:T(8,128)(2,1)} %get-tuple-element.103), channel_id=1, source_target_pairs={{0,6},{1,7},{2,4},{3,5},{4,2},{5,3},{6,0},{7,1},{8,14},{9,15},{10,... | collective-permute-start | bytes 2359304 | tf_op jit(solution)/shard_map/ppermute | solution.py:129
  408.5 64.7 %collective-permute-start.35 = (bf16[2,192,1024]{2,1,0:T(8,128)(2,1)}, bf16[2,192,1024]{2,1,0:T(8,128)(2,1)}, u32[]{:S(2)}, u32[]{:S(2)}) collective-permute-start(bf16[2,192,1024]{2,1,0:T(8,128)(2,1)} %get-tuple-element.104), channel_id=1, source_target_pairs={{0,4},{1,5},{2,6},{3,7},{4,0},{5,1},{6,2},{7,3},{8,12},{9,13},{10,... | collective-permute-start | bytes 2359304 | tf_op jit(solution)/shard_map/ppermute | solution.py:129
  453.6 11.9 %all-to-all-start.2 = ((bf16[8,48,256]{2,1,0:T(8,128)(2,1)}), bf16[8,48,256]{2,1,0:T(8,128)(2,1)S(1)}, u32[]{:S(2)}, u32[]{:S(2)}) async-start(bf16[8,48,256]{2,1,0:T(8,128)(2,1)} %pad_maximum_fusion.13), calls=%async_computation.4 | async-start | bytes 393216 | tf_op jit(solution)/shard_map/all_to_all | solution.py:224
  (58 other events, 662.7 us)
Sparse Core Ops, SparseCore 0:
  10.2 48.2 all-gather.6
  66.7 49.9 all-gather.10
  119.1 35.3 all-gather.8
  235.7 26.9 reduce-scatter.4
  307.4 51.9 reduce-scatter.6
  384.7 65.4 reduce-scatter.8
  452.5 19.1 reduce-scatter.10
